TPU v7x, 32 devices: a whole 2x2x4 slice. The times are simulated.
32 devices in a mesh: lat: 8 (over y, x, core), lon: 4 (over z).
Axes of the slice: x: 2, y: 2, z: 4, core: 2. Of those that a mesh axis runs over, the one named last changes fastest.
Arguments:
- ocean_state: bfloat16 [1, 96, 640, 768], P(None, 'lat', None, 'lon'), may hold values from -6 to 6
- zonal_kernel: bfloat16 [2, 5, 256, 640], replicated, may hold values from -0.15625 to 0.15625
- norm_gain: bfloat16 [2, 640], replicated, may hold values from 0.099609375 to 1.8984375
- input_weight: bfloat16 [2, 640, 1280], replicated, may hold values from -0.25 to 0.25
- output_weight: bfloat16 [2, 1280, 640], replicated, may hold values from -0.15625 to 0.15625
Outputs:
- state_out: bfloat16 [1, 96, 640, 768], P(None, 'lat', None, 'lon')
All inputs are finite; a program needn't handle non-finite values.
Results may differ from a plain program's by a relative error of at most 0.009.
Values may be sent and summed in bfloat16 or wider, within the bound.
No kernel may reach another device: no remote copies, remote signals or barrier semaphores. Data moves between devices by JAX's collectives and lax.ppermute only.
A program may use at most 128 MiB of HBM per device.

v0:
```python
import functools
import math

import jax
import jax.numpy as jnp
import numpy as np
from jax import lax
from jax.experimental import pallas as pl
from jax.experimental.pallas import tpu as pltpu
from jax.sharding import PartitionSpec as P


LANES = 128
PACK = 16
SUBLANES = 8


def bases(width, taps):
    length = -(-(width + taps) // (2 * PACK)) * 2 * PACK
    odd = 2 * np.arange(length // 2) + 1

    def wave(points):
        angle = np.pi / length * (points[:, None] * odd[None, :] % (2 * length))
        return np.concatenate([np.cos(angle), -np.sin(angle)], axis=1)

    forward = wave(np.arange(width + taps)).T
    inverse = 2.0 / length * wave(taps + np.arange(width))
    tap_basis = wave(np.arange(taps)).T
    return tuple(jnp.asarray(a, jnp.bfloat16) for a in (forward, inverse, tap_basis))


def gelu(values):
    return 0.5 * values * (1.0 + lax.erf(values * math.sqrt(0.5)))


def conv_kernel(*refs, windows, row_refs, counts, begin, lanes):
    quad, forward, inverse, factors = refs[:4]
    sources = refs[4 : 4 + counts]
    out, spectra, product = refs[4 + counts :]
    step = pl.program_id(0)
    part = out.shape[2]

    def block_of(ref):
        offset = 0 if ref.shape[2] == part else begin
        return pl.ds(pl.multiple_of((step + offset) * lanes, lanes), lanes)

    ours = [block_of(ref) for ref in sources]
    freqs = forward.shape[0] // 2
    every = len(row_refs)
    taps_r = factors.shape[0]

    def row(g):
        return jnp.concatenate([sources[s][at, lon, ours[s]] for s, at, lon in row_refs[g][1]], axis=0)

    for g in range(0, every, 2):
        two = jnp.concatenate([row(g), row(g + 1)], axis=1)
        result = jnp.dot(forward[...], two, preferred_element_type=jnp.float32)
        for j in range(2):
            spectra[g + j] = result[:, j * lanes : (j + 1) * lanes] * quad[row_refs[g + j][0]]

    def block(f, carry):
        start = pl.multiple_of(f * SUBLANES, SUBLANES)
        re = pl.ds(start, SUBLANES)
        im = pl.ds(pl.multiple_of(freqs + start, SUBLANES), SUBLANES)
        fr = [factors[r, re] for r in range(taps_r)]
        fi = [factors[r, im] for r in range(taps_r)]
        fd = [b - a for a, b in zip(fr, fi)]
        fs = [b + a for a, b in zip(fr, fi)]
        h = 0
        for first, count in windows:
            xr = [spectra[first + g, re] for g in range(taps_r - 1)]
            xi = [spectra[first + g, im] for g in range(taps_r - 1)]
            xs = [a + b for a, b in zip(xr, xi)]
            for k in range(count):
                xr.append(spectra[first + k + taps_r - 1, re])
                xi.append(spectra[first + k + taps_r - 1, im])
                xs.append(xr[-1] + xi[-1])
                both, up, down = xs[0] * fr[0], xr[0] * fd[0], xi[0] * fs[0]
                for r in range(1, taps_r):
                    both, up, down = both + xs[r] * fr[r], up + xr[r] * fd[r], down + xi[r] * fs[r]
                here = slice(h * lanes, (h + 1) * lanes)
                product[re, here] = both - down
                product[im, here] = both + up
                for window in (xr, xi, xs):
                    window.pop(0)
                h += 1
        return carry

    lax.fori_loop(0, freqs // SUBLANES, block, 0, unroll=4)
    own = [row_refs[first + taps_r // 2 + k][1] for first, count in windows for k in range(count)]
    for h in range(0, len(own), 2):
        two = slice(h * lanes, (h + 2) * lanes)
        conv = jnp.dot(inverse[...], product[:, two].astype(jnp.bfloat16), preferred_element_type=jnp.float32)
        for j in range(2):
            source, at, _ = own[h + j][1]
            value = sources[source][at, :, ours[source]].astype(jnp.float32)
            out[h + j, :, block_of(out)] = (value + gelu(conv[:, j * lanes : (j + 1) * lanes])).astype(out.dtype)


def convolve(quad, tables, factors, sources, rows, windows, part):
    forward, inverse = tables
    taps_r, length, _ = factors.shape
    start, blocks = part
    out_rows = sum(count for _, count in windows)
    width = inverse.shape[0]
    lanes = blocks * LANES

    held = pl.BlockSpec(memory_space=pltpu.VMEM)
    out = jax.ShapeDtypeStruct((out_rows, width, lanes), jnp.bfloat16)
    kernel = functools.partial(
        conv_kernel, windows=windows, row_refs=rows, counts=len(sources), begin=start, lanes=LANES
    )
    return pl.pallas_call(
        kernel,
        grid=(blocks,),
        out_shape=out,
        in_specs=[
            pl.BlockSpec(memory_space=pltpu.SMEM),
            held,
            held,
            pl.BlockSpec((taps_r, length, LANES), lambda i: (0, 0, i + start)),
        ]
        + [held] * len(sources),
        out_specs=held,
        scratch_shapes=[
            pltpu.VMEM((len(rows), length, LANES), jnp.float32),
            pltpu.VMEM((length, out_rows * LANES), jnp.float32),
        ],
        compiler_params=pltpu.CompilerParams(vmem_limit_bytes=20 << 20),
        cost_estimate=pl.CostEstimate(
            flops=2 * lanes * length * (len(rows) * forward.shape[1] + out_rows * width),
            bytes_accessed=2 * lanes * (len(rows) * forward.shape[1] + 2 * taps_r * length),
            transcendentals=out_rows * lanes * width,
        ),
        name="zonal_conv",
    )(quad, forward, inverse, factors, *sources)


def mlp_kernel(gain, w_in, w_out, *refs, half, kept, parts, together):
    mixed = refs[: parts * together]
    given = refs[parts * together + kept :]
    count, width, _ = mixed[0].shape
    channels = w_in.shape[0]

    def load(t):
        pieces = mixed[t * parts : (t + 1) * parts]
        values = [m[...].reshape(count * width, m.shape[2]).astype(jnp.float32) for m in pieces]
        values = values[0] if parts == 1 else jnp.concatenate(values, axis=1)
        average = jnp.mean(values, axis=1, keepdims=True)
        centred = values - average
        variance = jnp.mean(jnp.square(centred), axis=1, keepdims=True)
        return values, (centred * lax.rsqrt(variance + 1e-05) * gain[...]).astype(jnp.bfloat16)

    following = load(0)
    for t in range(together):
        values, normed = following
        hidden = jnp.dot(normed, w_in[...], preferred_element_type=jnp.float32)
        hidden = gelu(hidden).astype(jnp.bfloat16)
        if t + 1 < together:
            following = load(t + 1)
        result = values + jnp.dot(hidden, w_out[...], preferred_element_type=jnp.float32)
        result = result.astype(jnp.bfloat16).reshape(count, width, channels)
        here = slice(t * count, (t + 1) * count)
        given[0][here] = result
        start = 0
        for first, last in zip(given[1::2], given[2::2]):
            cut = slice(start, start + first.shape[2])
            first[here] = result[:, :half, cut]
            last[here] = result[:, width - half :, cut]
            start += first.shape[2]


def mlp(gain, w_in, w_out, mixed, steps, out_rows, edge, cuts=(), kept=None):
    width = mixed[0].shape[1]
    channels, hidden_units = w_in.shape
    together = len(steps[0][0])

    def chosen(values):
        def index(i):
            at = values[0]
            for k in range(1, len(values)):
                at = at + (values[k] - values[k - 1]) * (i >= k).astype(jnp.int32)
            return (at, 0, 0)

        return index

    def whole(array):
        return pl.BlockSpec(array.shape, lambda i: (0,) * array.ndim)

    def given(lon, lanes):
        sizes = (pl.Element(2 * together), pl.Element(lon), pl.Element(lanes))
        return pl.BlockSpec(sizes, chosen([row for _, row in steps]))

    lasts = [(width, channels)] + [(edge, cut) for cut in cuts for _ in range(2)]
    extra = [] if kept is None else [kept]
    return pl.pallas_call(
        functools.partial(mlp_kernel, half=edge, kept=len(extra), parts=len(mixed), together=together),
        grid=(len(steps),),
        out_shape=[jax.ShapeDtypeStruct((out_rows, *last), jnp.bfloat16) for last in lasts],
        in_specs=[whole(gain), whole(w_in), whole(w_out)]
        + [
            pl.BlockSpec((2, *m.shape[1:]), chosen([pairs[t] for pairs, _ in steps]))
            for t in range(together)
            for m in mixed
        ]
        + [pl.BlockSpec(memory_space=pl.ANY) for _ in extra],
        out_specs=[given(*last) for last in lasts],
        input_output_aliases={3 + together * len(mixed): 0} if extra else {},
        compiler_params=pltpu.CompilerParams(vmem_limit_bytes=20 << 20),
        cost_estimate=pl.CostEstimate(
            flops=8 * len(steps) * together * width * channels * hidden_units,
            bytes_accessed=8 * len(steps) * together * width * channels + 4 * channels * hidden_units,
            transcendentals=2 * len(steps) * together * width * hidden_units,
        ),
        name="channel_mlp",
    )(gain, w_in, w_out, *(list(mixed) * together), *extra)


def edge_kernel(state, first, last, sems, *, spans):
    edge, width = first.shape[1], state.shape[1]
    copies = []
    for k, (row, at, count) in enumerate(spans):
        for side, (target, lon) in enumerate([(last, width - edge), (first, 0)]):
            source = state.at[pl.ds(row, count), pl.ds(lon, edge)]
            copy = pltpu.make_async_copy(source, target.at[pl.ds(at, count)], sems.at[2 * k + side])
            copy.start()
            copies.append(copy)
    for copy in copies:
        copy.wait()


def edges(state, spans, edge):
    rows = sum(count for _, _, count in spans)
    out = jax.ShapeDtypeStruct((rows, edge, state.shape[2]), state.dtype)
    return pl.pallas_call(
        functools.partial(edge_kernel, spans=spans),
        out_shape=[out, out],
        in_specs=[pl.BlockSpec(memory_space=pltpu.HBM)],
        out_specs=[pl.BlockSpec(memory_space=pltpu.VMEM)] * 2,
        scratch_shapes=[pltpu.SemaphoreType.DMA((2 * len(spans),))],
        compiler_params=pltpu.CompilerParams(vmem_limit_bytes=60 << 20),
        name="edges",
    )(state)


def rotate(block, axis, hops):
    count = lax.axis_size(axis)
    return lax.ppermute(block, axis, [(i, (i + hops) % count) for i in range(count)])


def zonal_halos(first, last, half):
    width = first.shape[1]
    lefts, rights, hops, missing = [], [], 1, half
    while missing > 0:
        take = min(width, missing)
        lefts.insert(0, rotate(last[:, width - take :], "lon", hops))
        rights.append(rotate(first[:, :take], "lon", -hops))
        missing -= take
        hops += 1
    if len(lefts) == 1:
        return lefts[0], rights[0]
    return jnp.concatenate(lefts, axis=1), jnp.concatenate(rights, axis=1)


def step_rows(block, hops):
    count = lax.axis_size("lat")
    pairs = [(i, i + hops) for i in range(count) if 0 <= i + hops < count]
    return lax.ppermute(block, "lat", pairs)


def lane_parts(channels):
    units = channels // LANES
    least = max(1, units // 5)
    sizes = [(units - least + 1) // 2, (units - least) // 2, least]
    return [(sum(sizes[:k]), size) for k, size in enumerate(sizes) if size]


def body(ocean_state, zonal_kernel, norm_gain, input_weight, output_weight):
    blocks, kernel_rows, taps, channels = zonal_kernel.shape
    _, rows, _, width = ocean_state.shape
    rim = kernel_rows // 2
    half = taps // 2
    edge = min(half, width)
    forward, inverse, tap_basis = bases(width, taps)
    total_rows = rows * lax.axis_size("lat")
    index = lax.axis_index("lat") * rows - rim + jnp.arange(rows + 2 * rim, dtype=jnp.int32)
    quad = jnp.sin(jnp.pi * (index.astype(jnp.float32) + 0.5) / total_rows)
    quad = jnp.where((index >= 0) & (index < total_rows), quad, 0.0)
    factors = []
    for layer in range(blocks):
        taps_of = zonal_kernel[layer]
        factors.append(jnp.einsum("kt,rtc->rkc", tap_basis, taps_of, preferred_element_type=jnp.float32))
    gains = norm_gain.astype(jnp.float32)[:, None, :]

    groups = [
        list(range(rim)) + list(range(rows - rim, rows)),
        list(range(rim, 2 * rim)) + list(range(rows - 2 * rim, rows - rim)),
        list(range(2 * rim, rows - 2 * rim)),
    ]
    group_of = {row: (k, at) for k, members in enumerate(groups) for at, row in enumerate(members)}
    state = jnp.swapaxes(ocean_state[0], 1, 2)
    mids = [state]
    mid_of = {row: (0, row) for row in range(rows)}

    pairs = state.reshape(rows // rim, rim, width, channels)

    def pick(pairs, members, lon, cut):
        first, last = members[0] // rim, members[-1] // rim
        stride = max(1, (last - first) // (len(members) // rim - 1))
        low, high = (first, 0, lon.start, cut.start), (last + 1, rim, lon.stop, cut.stop)
        chosen = lax.slice(pairs, low, high, (stride, 1, 1, 1))
        return chosen.reshape(len(members), *chosen.shape[2:])

    parts = lane_parts(channels)
    pieces = [slice(start * LANES, (start + count) * LANES) for start, count in parts]
    cuts = [count * LANES for _, count in parts]
    lanes = [slice(0, channels)] * 2 + pieces
    groups_of = [groups[0], groups[1]] + [groups[2]] * len(parts)
    head, tail = slice(0, edge), slice(width - edge, width)
    first, last = edges(state, [(0, 0, rim), (rows - rim, rim, rim)], edge)
    firsts, lasts = [first], [last]
    pairs, _ = lax.optimization_barrier((pairs, first[:1, :1, :1]))
    firsts += [pick(pairs, members, head, cut) for members, cut in zip(groups_of[1:], lanes[1:])]
    lasts += [pick(pairs, members, tail, cut) for members, cut in zip(groups_of[1:], lanes[1:])]
    tables = (forward, inverse)
    out = None
    for layer in range(blocks):
        final = layer + 1 == blocks
        halos = [zonal_halos(f, b, half) for f, b in zip(firsts, lasts)]

        def near(start):
            source, row = mid_of[start]
            return mids[source][row : row + rim]

        def far(start):
            at = group_of[start][1]
            return jnp.concatenate([halo[at : at + rim] for halo in halos[0]], axis=1)

        low = [step_rows(near(rows - rim), 1), step_rows(far(rows - rim), 1)]
        high = [step_rows(near(0), -1), step_rows(far(0), -1)]

        def own(row, used_mids, used):
            k, at = group_of[row]
            source, mid_row = mid_of[row]
            n = len(used_mids)
            j = used.index(k)
            every = slice(None)
            middle = (used_mids.index(source), mid_row, every)
            return (row + rim, [(n + j, at, every), middle, (n + len(used) + j, at, every)])

        def lat(number, at, place):
            return (
                place,
                [
                    (number + 1, at, slice(0, half)),
                    (number, at, slice(None)),
                    (number + 1, at, slice(half, 2 * half)),
                ],
            )

        used = [0, 1]
        used_mids = sorted({mid_of[row][0] for k in used for row in groups[k]})
        sources = [mids[s] for s in used_mids] + [halos[k][side] for side in (0, 1) for k in used]
        sources = sources + low + high
        n = len(sources)
        outer = (
            [lat(n - 4, r, r) for r in range(rim)]
            + [own(row, used_mids, used) for row in range(2 * rim)]
            + [own(row, used_mids, used) for row in range(rows - 2 * rim, rows)]
            + [lat(n - 2, r, rows + rim + r) for r in range(rim)]
        )
        windows = [(0, rim), (3 * rim, rim)]
        mixed_outer = [
            convolve(quad, tables, factors[layer], sources, outer, windows, (0, channels // LANES))
        ]
        used = [0, 1, 2]
        used_mids = sorted({source for source, _ in mid_of.values()})
        inner = [own(row, used_mids, used) for row in range(rows)]
        mixed_inner = []
        for k, part in enumerate(parts):
            chosen = [halos[0], halos[1], halos[2 + k]]
            sources = [mids[s] for s in used_mids] + [pair[side] for side in (0, 1) for pair in chosen]
            mixed_inner.append(
                convolve(quad, tables, factors[layer], sources, inner, [(0, rows - 2 * rim)], part)
            )
        weights = (gains[layer], input_weight[layer], output_weight[layer])
        count = rows // 2
        if final:
            (out,) = mlp(*weights, mixed_outer, [([0], 0), ([1], rows - 2)], rows, 0)
            steps = [([p, p + 1], 2 * p + rim) for p in range(0, count - 2, 2)]
            (out,) = mlp(*weights, mixed_inner, steps, rows, 0, kept=out)
        else:
            outs = [mlp(*weights, mixed_outer, [([0], 0), ([1], 2)], 2 * rim, edge, [channels])]
            outs.append(mlp(*weights, mixed_inner, [([0], 0), ([count - 3], 2)], 2 * rim, edge, [channels]))
            steps = [([p + 1], 2 * p) for p in range(count - 4)]
            outs.append(mlp(*weights, mixed_inner, steps, rows - 4 * rim, edge, cuts))
            mids = [o[0] for o in outs]
            mid_of = group_of
            firsts = [f for o in outs for f in o[1::2]]
            lasts = [b for o in outs for b in o[2::2]]
    return jnp.swapaxes(out, 1, 2)[None]


def solution(mesh):
    in_specs = (P(None, "lat", None, "lon"), P(), P(), P(), P())
    out_specs = P(None, "lat", None, "lon")
    return jax.shard_map(body, mesh=mesh, in_specs=in_specs, out_specs=out_specs, check_vma=False)
```

profile of v0, /device:TPU:20, one launch (start us, length us, event | category | flops | bytes accessed | tf_op | source)
XLA Modules:
  0.0 265.4 jit_solution(9553386533352538128)
XLA Ops:
  0.0 1.0 fusion.4
  1.0 1.6 collective-permute-start.12
  2.6 0.4 collective-permute-start.13
  3.1 2.2 fusion.5
  5.3 1.6 collective-permute-start.10
  6.9 2.5 edges.1
  9.4 2.1 collective-permute-start
  11.4 1.0 fusion.7
  12.4 4.0 %slice_bitcast_fusion.1 = (bf16[640,1280]{1,0:T(8,128)(2,1)}, bf16[640,1280]{1,0:T(8,128)(2,1)}) fusion(bf16[2,640,1280]{2,1,0:T(8,128)(2,1)} %param.11), kind=kLoop, calls=%fused_computation.6 | loop fusion | bytes 6553600 | tf_op jit(solution)/shard_map/squeeze | solution.py:386
  16.5 2.0 slice_bitcast_fusion
  18.5 1.1 fusion.6
  19.7 0.3 copy-done.26
  20.1 3.4 %convolution_bitcast_fusion.refs_3_ = f32[5,448,640]{2,1,0:T(8,128)} fusion(bf16[448,256,1]{1,0,2:T(8,128)(2,1)S(1)} %copy-done.26, bf16[2,5,256,640]{3,2,1,0:T(8,128)(2,1)S(1)} %copy-done.24), kind=kOutput, calls=%fused_computation | convolution fusion | flops 734003200 | bytes 7602176 | tf_op jit(solution)/shard_map/kt,rtc->rkc/dot_general | solution.py:292
  23.5 6.0 %collective-permute-done.refs_5_ = bf16[4,128,640]{2,1,0:T(8,128)(2,1)S(1)} collective-permute-done((bf16[4,128,640]{2,1,0:T(8,128)(2,1)}, bf16[4,128,640]{2,1,0:T(8,128)(2,1)S(1)}, u32[]{:S(2)}, u32[]{:S(2)}) %collective-permute-start) | collective-permute-done | bytes 655392 | tf_op jit(solution)/shard_map/ppermute | solution.py:248
  29.5 14.5 %collective-permute-start.1 = (bf16[4,128,640]{2,1,0:T(8,128)(2,1)S(1)}, bf16[4,128,640]{2,1,0:T(8,128)(2,1)S(1)}, u32[]{:S(2)}, u32[]{:S(2)}) collective-permute-start(bf16[4,128,640]{2,1,0:T(8,128)(2,1)S(1)} %bitcast.46), channel_id=1, source_target_pairs={{0,1},{1,2},{2,3},{3,0},{4,5},{5,6},{6,7},{7,4},{8,9},{9,10},{10,1... | collective-permute-start | bytes 1966088 | tf_op jit(solution)/shard_map/ppermute | solution.py:248
  44.1 0.7 copy-done.21
  44.8 2.9 %collective-permute-start.3 = (bf16[4,128,640]{2,1,0:T(8,128)(2,1)}, bf16[4,128,640]{2,1,0:T(8,128)(2,1)}, u32[]{:S(2)}, u32[]{:S(2)}) collective-permute-start(bf16[4,128,640]{2,1,0:T(8,128)(2,1)} %bitcast.14), channel_id=1, source_target_pairs={{0,3},{1,0},{2,1},{3,2},{4,7},{5,4},{6,5},{7,6},{8,11},{9,8},{10,9... | collective-permute-start | bytes 1966088 | tf_op jit(solution)/shard_map/ppermute | solution.py:248
  47.8 1.0 pad_maximum_fusion.1
  48.8 0.9 pad_maximum_fusion
  49.7 0.7 copy-done.15
  50.4 1.9 collective-permute-start.6
  52.3 12.9 %collective-permute-done.11.refs_10_ = bf16[4,128,256]{2,1,0:T(8,128)(2,1)S(1)} collective-permute-done((bf16[4,128,256]{2,1,0:T(8,128)(2,1)S(1)}, bf16[4,128,256]{2,1,0:T(8,128)(2,1)S(1)}, u32[]{:S(2)}, u32[]{:S(2)}) %collective-permute-start.11) | collective-permute-done | bytes 262176 | tf_op jit(solution)/shard_map/ppermute | solution.py:248
  65.2 0.7 copy-done.17
  65.9 1.9 collective-permute-start.4
  67.8 3.0 %collective-permute-done.9.refs_10_ = bf16[4,128,256]{2,1,0:T(8,128)(2,1)S(1)} collective-permute-done((bf16[4,128,256]{2,1,0:T(8,128)(2,1)S(1)}, bf16[4,128,256]{2,1,0:T(8,128)(2,1)S(1)}, u32[]{:S(2)}, u32[]{:S(2)}) %collective-permute-start.9) | collective-permute-done | bytes 262176 | tf_op jit(solution)/shard_map/ppermute | solution.py:248
  70.8 0.7 copy-done.19
  71.5 1.9 collective-permute-start.5
  73.4 0.8 copy-done.9
  74.3 4.5 %collective-permute-start.7 = (bf16[2,256,640]{2,1,0:T(8,128)(2,1)}, bf16[2,256,640]{2,1,0:T(8,128)(2,1)}, u32[]{:S(2)}, u32[]{:S(2)}) collective-permute-start(bf16[2,256,640]{2,1,0:T(8,128)(2,1)} %pad_maximum_fusion.1), channel_id=1, source_target_pairs={{4,0},{8,4},{12,8},{16,12},{20,16},{24,20},{28,24},{5,1},{9,5},{13... | collective-permute-start | bytes 1966088 | tf_op jit(solution)/shard_map/ppermute | solution.py:268
  78.8 3.5 %collective-permute-done.3.refs_8_.refs_9_ = bf16[4,128,640]{2,1,0:T(8,128)(2,1)} collective-permute-done((bf16[4,128,640]{2,1,0:T(8,128)(2,1)}, bf16[4,128,640]{2,1,0:T(8,128)(2,1)}, u32[]{:S(2)}, u32[]{:S(2)}) %collective-permute-start.3) | collective-permute-done | bytes 655392 | tf_op jit(solution)/shard_map/ppermute | solution.py:248
  82.3 4.3 %collective-permute-start.8 = (bf16[4,128,256]{2,1,0:T(8,128)(2,1)}, bf16[4,128,256]{2,1,0:T(8,128)(2,1)S(1)}, u32[]{:S(2)}, u32[]{:S(2)}) collective-permute-start(bf16[4,128,256]{2,1,0:T(8,128)(2,1)} %bitcast.47), channel_id=1, source_target_pairs={{0,1},{1,2},{2,3},{3,0},{4,5},{5,6},{6,7},{7,4},{8,9},{9,10},{10,1... | collective-permute-start | bytes 786440 | tf_op jit(solution)/shard_map/ppermute | solution.py:248
  86.6 2.6 copy-done
  89.3 1.1 copy-done.4
  90.3 1.1 copy-done.6
  91.4 0.9 copy-done.7
  92.4 1.1 copy-done.10
  93.4 0.9 copy-done.22
  94.4 3.5 %zonal_conv.11.refs_2_ = bf16[8,192,128]{2,1,0:T(8,128)(2,1)S(1)} custom-call(f32[16]{0:T(128)S(1)} %and_select_fusion.refs_0_, bf16[448,448]{1,0:T(8,128)(2,1)S(1)} %copy-done.2, bf16[192,448]{1,0:T(8,128)(2,1)S(1)} %copy-done.7, f32[5,448,640]{2,1,0:T(8,128)S(1)} %copy-done, bf16[12,192,640]{2,1,0:T(8,128)(2,1)S(1)} %bitcast.42, ...), custom_call_target="tpu_custom_call" | custom-call | flops 792723456 | bytes 2523136 | tf_op jit(solution)/shard_map/zonal_conv/pallas_call | solution.py:113
  97.9 5.9 %zonal_conv.10.refs_1_ = bf16[8,192,256]{2,1,0:T(8,128)(2,1)S(1)} custom-call(f32[16]{0:T(128)S(1)} %and_select_fusion.refs_0_, bf16[448,448]{1,0:T(8,128)(2,1)S(1)} %copy-done.2, bf16[192,448]{1,0:T(8,128)(2,1)S(1)} %copy-done.7, f32[5,448,640]{2,1,0:T(8,128)S(1)} %copy-done, bf16[12,192,640]{2,1,0:T(8,128)(2,1)S(1)} %bitcast.43, ...), custom_call_target="tpu_custom_call" | custom-call | flops 1585446912 | bytes 5046272 | tf_op jit(solution)/shard_map/zonal_conv/pallas_call | solution.py:113
  103.9 5.9 %zonal_conv.9.refs_0_ = bf16[8,192,256]{2,1,0:T(8,128)(2,1)S(1)} custom-call(f32[16]{0:T(128)S(1)} %and_select_fusion.refs_0_, bf16[448,448]{1,0:T(8,128)(2,1)S(1)} %copy-done.2, bf16[192,448]{1,0:T(8,128)(2,1)S(1)} %copy-done.7, f32[5,448,640]{2,1,0:T(8,128)S(1)} %copy-done, bf16[12,192,640]{2,1,0:T(8,128)(2,1)S(1)} %bitcast.44, ...), custom_call_target="tpu_custom_call" | custom-call | flops 1585446912 | bytes 5046272 | tf_op jit(solution)/shard_map/zonal_conv/pallas_call | solution.py:113
  109.9 11.4 %zonal_conv.8.refs_0_ = bf16[4,192,640]{2,1,0:T(8,128)(2,1)S(1)} custom-call(f32[16]{0:T(128)S(1)} %and_select_fusion.refs_0_, bf16[448,448]{1,0:T(8,128)(2,1)S(1)} %copy-done.2, bf16[192,448]{1,0:T(8,128)(2,1)S(1)} %copy-done.7, f32[5,448,640]{2,1,0:T(8,128)S(1)} %copy-done, bf16[12,192,640]{2,1,0:T(8,128)(2,1)S(1)} %bitcast.45, ...), custom_call_target="tpu_custom_call" | custom-call | flops 3523215360 | bytes 12615680 | tf_op jit(solution)/shard_map/zonal_conv/pallas_call | solution.py:113
  121.4 4.1 %channel_mlp.5 = (bf16[4,192,640]{2,1,0:T(8,128)(2,1)S(1)}, bf16[4,128,640]{2,1,0:T(8,128)(2,1)S(1)}, bf16[4,128,640]{2,1,0:T(8,128)(2,1)S(1)}) custom-call(f32[1,640]{1,0:T(1,128)S(1)} %get-tuple-element.59.gain, bf16[640,1280]{1,0:T(8,128)(2,1)S(1)} %copy-done.13, bf16[1280,640]{1,0:T(8,128)(2,1)S(1)} %copy-done.14, bf16[4,192,640]{2,1,0:T(8,128)(2,1)S(1)} %zonal_conv.8.refs_0_), custom_call_target="tpu_custom_call" | custom-call | flops 2516582400 | bytes 5242880 | tf_op jit(solution)/shard_map/channel_mlp/pallas_call | solution.py:196
  125.5 0.2 collective-permute-start.14
  125.7 4.1 %channel_mlp.7 = (bf16[4,192,640]{2,1,0:T(8,128)(2,1)S(1)}, bf16[4,128,256]{2,1,0:T(8,128)(2,1)S(1)}, bf16[4,128,256]{2,1,0:T(8,128)(2,1)S(1)}, bf16[4,128,256]{...) custom-call(f32[1,640]{1,0:T(1,128)S(1)} %get-tuple-element.59.gain,, ...), custom_call_target="tpu_custom_call" | custom-call | flops 2516582400 | bytes 5242880 | tf_op jit(solution)/shard_map/channel_mlp/pallas_call | solution.py:196
  129.8 2.0 collective-permute-start.23
  131.9 2.0 collective-permute-start.17
  133.8 4.0 %channel_mlp.6 = (bf16[4,192,640]{2,1,0:T(8,128)(2,1)S(1)}, bf16[4,128,640]{2,1,0:T(8,128)(2,1)S(1)}, bf16[4,128,640]{2,1,0:T(8,128)(2,1)S(1)}) custom-call(f32[1,640]{1,0:T(1,128)S(1)} %get-tuple-element.59.gain, bf16[640,1280]{1,0:T(8,128)(2,1)S(1)} %copy-done.13, bf16[1280,640]{1,0:T(8,128)(2,1)S(1)} %copy-done.14, ...), custom_call_target="tpu_custom_call" | custom-call | flops 2516582400 | bytes 5242880 | tf_op jit(solution)/shard_map/channel_mlp/pallas_call | solution.py:196
  138.1 22.0 %collective-permute-done.14.refs_7_.refs_6_ = bf16[4,128,640]{2,1,0:T(8,128)(2,1)S(1)} collective-permute-done((bf16[4,128,640]{2,1,0:T(8,128)(2,1)S(1)}, bf16[4,128,640]{2,1,0:T(8,128)(2,1)S(1)}, u32[]{:S(2)}, u32[]{:S(2)}) %collective-permute-start.14) | collective-permute-done | bytes 655392 | tf_op jit(solution)/shard_map/ppermute | solution.py:248
  160.1 2.8 %collective-permute-done.22.refs_9_ = bf16[4,128,128]{2,1,0:T(8,128)(2,1)S(1)} collective-permute-done((bf16[4,128,128]{2,1,0:T(8,128)(2,1)S(1)}, bf16[4,128,128]{2,1,0:T(8,128)(2,1)S(1)}, u32[]{:S(2)}, u32[]{:S(2)}) %collective-permute-start.22) | collective-permute-done | bytes 131104 | tf_op jit(solution)/shard_map/ppermute | solution.py:248
  163.0 2.1 collective-permute-start.21
  165.3 31.8 %collective-permute-done.16.refs_9_ = bf16[4,128,256]{2,1,0:T(8,128)(2,1)S(1)} collective-permute-done((bf16[4,128,256]{2,1,0:T(8,128)(2,1)S(1)}, bf16[4,128,256]{2,1,0:T(8,128)(2,1)S(1)}, u32[]{:S(2)}, u32[]{:S(2)}) %collective-permute-start.16) | collective-permute-done | bytes 262176 | tf_op jit(solution)/shard_map/ppermute | solution.py:248
  197.0 15.7 %collective-permute-done.20.refs_9_ = bf16[4,128,256]{2,1,0:T(8,128)(2,1)S(1)} collective-permute-done((bf16[4,128,256]{2,1,0:T(8,128)(2,1)S(1)}, bf16[4,128,256]{2,1,0:T(8,128)(2,1)S(1)}, u32[]{:S(2)}, u32[]{:S(2)}) %collective-permute-start.20) | collective-permute-done | bytes 262176 | tf_op jit(solution)/shard_map/ppermute | solution.py:248
  212.8 2.3 collective-permute-start.26
  215.1 2.2 collective-permute-start.24
  217.3 3.7 %collective-permute-start.25 = (bf16[2,256,640]{2,1,0:T(8,128)(2,1)S(1)}, bf16[2,256,640]{2,1,0:T(8,128)(2,1)S(1)}, u32[]{:S(2)}, u32[]{:S(2)}) collective-permute-start(bf16[2,256,640]{2,1,0:T(8,128)(2,1)S(1)} %pad_maximum_fusion.2), channel_id=1, source_target_pairs={{0,4},{4,8},{8,12},{12,16},{16,20},{20,24},{24,28},{1,5},{5,9},{9,... | collective-permute-start | bytes 1966088 | tf_op jit(solution)/shard_map/ppermute | solution.py:268
  220.9 2.8 %collective-permute-start.27 = (bf16[2,256,640]{2,1,0:T(8,128)(2,1)S(1)}, bf16[2,256,640]{2,1,0:T(8,128)(2,1)S(1)}, u32[]{:S(2)}, u32[]{:S(2)}) collective-permute-start(bf16[2,256,640]{2,1,0:T(8,128)(2,1)S(1)} %pad_maximum_fusion.3), channel_id=1, source_target_pairs={{4,0},{8,4},{12,8},{16,12},{20,16},{24,20},{28,24},{5,1},{9,5},{13... | collective-permute-start | bytes 1966088 | tf_op jit(solution)/shard_map/ppermute | solution.py:268
  223.8 0.9 convolution_bitcast_fusion.1.refs_3_
  224.7 2.9 %zonal_conv.14.refs_2_.refs_5_ = bf16[8,192,128]{2,1,0:T(8,128)(2,1)S(1)} custom-call(f32[16]{0:T(128)S(1)} %and_select_fusion.refs_0_, bf16[448,448]{1,0:T(8,128)(2,1)S(1)} %copy-done.2, bf16[192,448]{1,0:T(8,128)(2,1)S(1)} %copy-done.8, f32[5,448,640]{2,1,0:T(8,128)S(1)} %convolution_bitcast_fusion.1.refs_3_, ...), custom_call_target="tpu_custom_call" | custom-call | flops 792723456 | bytes 2523136 | tf_op jit(solution)/shard_map/zonal_conv/pallas_call | solution.py:113
  227.6 5.4 %zonal_conv.13.refs_1_.refs_4_ = bf16[8,192,256]{2,1,0:T(8,128)(2,1)S(1)} custom-call(f32[16]{0:T(128)S(1)} %and_select_fusion.refs_0_, bf16[448,448]{1,0:T(8,128)(2,1)S(1)} %copy-done.2, bf16[192,448]{1,0:T(8,128)(2,1)S(1)} %copy-done.8, f32[5,448,640]{2,1,0:T(8,128)S(1)} %convolution_bitcast_fusion.1.refs_3_, ...), custom_call_target="tpu_custom_call" | custom-call | flops 1585446912 | bytes 5046272 | tf_op jit(solution)/shard_map/zonal_conv/pallas_call | solution.py:113
  233.0 5.4 %zonal_conv.12.refs_0_.refs_3_ = bf16[8,192,256]{2,1,0:T(8,128)(2,1)S(1)} custom-call(f32[16]{0:T(128)S(1)} %and_select_fusion.refs_0_, bf16[448,448]{1,0:T(8,128)(2,1)S(1)} %copy-done.2, bf16[192,448]{1,0:T(8,128)(2,1)S(1)} %copy-done.8, f32[5,448,640]{2,1,0:T(8,128)S(1)} %convolution_bitcast_fusion.1.refs_3_, ...), custom_call_target="tpu_custom_call" | custom-call | flops 1585446912 | bytes 5046272 | tf_op jit(solution)/shard_map/zonal_conv/pallas_call | solution.py:113
  238.4 3.9 %collective-permute-done.25.refs_11_ = bf16[2,256,640]{2,1,0:T(8,128)(2,1)S(1)} collective-permute-done((bf16[2,256,640]{2,1,0:T(8,128)(2,1)S(1)}, bf16[2,256,640]{2,1,0:T(8,128)(2,1)S(1)}, u32[]{:S(2)}, u32[]{:S(2)}) %collective-permute-start.25) | collective-permute-done | bytes 655392 | tf_op jit(solution)/shard_map/ppermute | solution.py:268
  242.3 9.9 %zonal_conv.15.refs_0_ = bf16[4,192,640]{2,1,0:T(8,128)(2,1)S(1)} custom-call(f32[16]{0:T(128)S(1)} %and_select_fusion.refs_0_, bf16[448,448]{1,0:T(8,128)(2,1)S(1)} %copy-done.2, bf16[192,448]{1,0:T(8,128)(2,1)S(1)} %copy-done.8, f32[5,448,640]{2,1,0:T(8,128)S(1)} %convolution_bitcast_fusion.1.refs_3_, bf16[4,192,640]{2,1,0:T(8,128)(2,1)S(1)} %get-tuple-element.22.refs_4_, ...), custom_call_target="tpu_custom_call" | custom-call | flops 3523215360 | bytes 12615680 | tf_op jit(solution)/shard_map/zonal_conv/pallas_call | solution.py:113
  252.3 4.8 %channel_mlp.8.refs_6_ = bf16[12,192,640]{2,1,0:T(8,128)(2,1)} custom-call(f32[1,640]{1,0:T(1,128)S(1)} %get-tuple-element.60.gain, bf16[640,1280]{1,0:T(8,128)(2,1)S(1)} %copy-done.11, bf16[1280,640]{1,0:T(8,128)(2,1)S(1)} %copy-done.12, bf16[4,192,640]{2,1,0:T(8,128)(2,1)S(1)} %zonal_conv.15.refs_0_), custom_call_target="tpu_custom_call" | custom-call | flops 2516582400 | bytes 5242880 | tf_op jit(solution)/shard_map/channel_mlp/pallas_call | solution.py:196
  257.1 8.2 %channel_mlp.9 = bf16[12,192,640]{2,1,0:T(8,128)(2,1)} custom-call(f32[1,640]{1,0:T(1,128)S(1)} %get-tuple-element.60.gain, bf16[640,1280]{1,0:T(8,128)(2,1)S(1)} %copy-done.11, bf16[1280,640]{1,0:T(8,128)(2,1)S(1)} %copy-done.12, bf16[8,192,256]{2,1,0:T(8,128)(2,1)S(1)} %zonal_conv.12.refs_0_.refs_3_, ...), custom_call_target="tpu_custom_call", output_to_operand_aliasing={{}: (9, {})} | custom-call | flops 5033164800 | bytes 7208960 | tf_op jit(solution)/shard_map/channel_mlp/pallas_call | solution.py:196
  (87 shorter events, 1.1 us)
Async XLA Ops:
  1.0 43.0 %collective-permute-start.12 = (bf16[4,128,128]{2,1,0:T(8,128)(2,1)S(1)}, bf16[4,128,128]{2,1,0:T(8,128)(2,1)S(1)}, u32[]{:S(2)}, u32[]{:S(2)}) collective-permute-start(bf16[4,128,128]{2,1,0:T(8,128)(2,1)S(1)} %bitcast.51), channel_id=1, source_target_pairs={{0,1},{1,2},{2,3},{3,0},{4,5},{5,6},{6,7},{7,4},{8,9},{9,10},{10,1... | collective-permute-start | bytes 393224 | tf_op jit(solution)/shard_map/ppermute | solution.py:248
  2.6 41.5 %collective-permute-start.13 = (bf16[4,128,128]{2,1,0:T(8,128)(2,1)S(1)}, bf16[4,128,128]{2,1,0:T(8,128)(2,1)S(1)}, u32[]{:S(2)}, u32[]{:S(2)}) collective-permute-start(bf16[4,128,128]{2,1,0:T(8,128)(2,1)S(1)} %bitcast.50), channel_id=1, source_target_pairs={{0,3},{1,0},{2,1},{3,2},{4,7},{5,4},{6,5},{7,6},{8,11},{9,8},{10,9... | collective-permute-start | bytes 393224 | tf_op jit(solution)/shard_map/ppermute | solution.py:248
  5.3 6.1 %copy-start.1 = (bf16[1,12,640,192]{2,3,1,0:T(8,128)(2,1)S(1)}, bf16[1,12,640,192]{2,3,1,0:T(8,128)(2,1)}, u32[]{:S(2)}) copy-start(bf16[1,12,640,192]{2,3,1,0:T(8,128)(2,1)} %param.8) | copy-start | bytes 8847364
  5.3 44.4 %collective-permute-start.10 = (bf16[4,128,256]{2,1,0:T(8,128)(2,1)}, bf16[4,128,256]{2,1,0:T(8,128)(2,1)S(1)}, u32[]{:S(2)}, u32[]{:S(2)}) collective-permute-start(bf16[4,128,256]{2,1,0:T(8,128)(2,1)} %bitcast.17), channel_id=1, source_target_pairs={{0,1},{1,2},{2,3},{3,0},{4,5},{5,6},{6,7},{7,4},{8,9},{9,10},{10,1... | collective-permute-start | bytes 786440 | tf_op jit(solution)/shard_map/ppermute | solution.py:248
  9.4 20.1 %collective-permute-start = (bf16[4,128,640]{2,1,0:T(8,128)(2,1)}, bf16[4,128,640]{2,1,0:T(8,128)(2,1)S(1)}, u32[]{:S(2)}, u32[]{:S(2)}) collective-permute-start(bf16[4,128,640]{2,1,0:T(8,128)(2,1)} %get-tuple-element.20), channel_id=1, source_target_pairs={{0,1},{1,2},{2,3},{3,0},{4,5},{5,6},{6,7},{7,4},{8,9},{9,10},{10,1... | collective-permute-start | bytes 1966088 | tf_op jit(solution)/shard_map/ppermute | solution.py:248
  11.4 33.4 %collective-permute-start.2 = (bf16[4,128,640]{2,1,0:T(8,128)(2,1)}, bf16[4,128,640]{2,1,0:T(8,128)(2,1)S(1)}, u32[]{:S(2)}, u32[]{:S(2)}) collective-permute-start(bf16[4,128,640]{2,1,0:T(8,128)(2,1)} %get-tuple-element.21), channel_id=1, source_target_pairs={{0,3},{1,0},{2,1},{3,2},{4,7},{5,4},{6,5},{7,6},{8,11},{9,8},{10,9... | collective-permute-start | bytes 1966088 | tf_op jit(solution)/shard_map/ppermute | solution.py:248
  12.4 4.0 %copy-start.23 = (bf16[2,1280,640]{2,1,0:T(8,128)(2,1)S(1)}, bf16[2,1280,640]{2,1,0:T(8,128)(2,1)}, u32[]{:S(2)}) copy-start(bf16[2,1280,640]{2,1,0:T(8,128)(2,1)} %param.12) | copy-start | bytes 9830404
  16.4 3.3 %copy-start.24 = (bf16[2,5,256,640]{3,2,1,0:T(8,128)(2,1)S(1)}, bf16[2,5,256,640]{3,2,1,0:T(8,128)(2,1)}, u32[]{:S(2)}) copy-start(bf16[2,5,256,640]{3,2,1,0:T(8,128)(2,1)} %param.9) | copy-start | bytes 9830404
  18.5 1.6 copy-start.26
  20.1 24.0 %copy-start.29 = (bf16[2,2,128,256]{3,2,1,0:T(8,128)(2,1)S(1)}, bf16[2,2,128,256]{3,2,1,0:T(8,128)(2,1)}, u32[]{:S(2)}) copy-start(bf16[2,2,128,256]{3,2,1,0:T(8,128)(2,1)} %get-tuple-element.41) | copy-start | bytes 786436
  20.1 24.7 %copy-start.28 = (bf16[2,2,128,256]{3,2,1,0:T(8,128)(2,1)S(1)}, bf16[2,2,128,256]{3,2,1,0:T(8,128)(2,1)}, u32[]{:S(2)}) copy-start(bf16[2,2,128,256]{3,2,1,0:T(8,128)(2,1)} %get-tuple-element.43) | copy-start | bytes 786436
  29.5 19.3 %copy-start.3 = (bf16[4,128,640]{2,1,0:T(8,128)(2,1)}, bf16[4,128,640]{2,1,0:T(8,128)(2,1)S(1)}, u32[]{:S(2)}) copy-start(bf16[4,128,640]{2,1,0:T(8,128)(2,1)S(1)} %collective-permute-done.refs_5_) | copy-start | bytes 1966084
  29.5 43.9 %collective-permute-start.1 = (bf16[4,128,640]{2,1,0:T(8,128)(2,1)S(1)}, bf16[4,128,640]{2,1,0:T(8,128)(2,1)S(1)}, u32[]{:S(2)}, u32[]{:S(2)}) collective-permute-start(bf16[4,128,640]{2,1,0:T(8,128)(2,1)S(1)} %bitcast.46), channel_id=1, source_target_pairs={{0,1},{1,2},{2,3},{3,0},{4,5},{5,6},{6,7},{7,4},{8,9},{9,10},{10,1... | collective-permute-start | bytes 1966088 | tf_op jit(solution)/shard_map/ppermute | solution.py:248
  44.0 21.1 %collective-permute-start.11 = (bf16[4,128,256]{2,1,0:T(8,128)(2,1)S(1)}, bf16[4,128,256]{2,1,0:T(8,128)(2,1)S(1)}, u32[]{:S(2)}, u32[]{:S(2)}) collective-permute-start(bf16[4,128,256]{2,1,0:T(8,128)(2,1)S(1)} %bitcast.49), channel_id=1, source_target_pairs={{0,3},{1,0},{2,1},{3,2},{4,7},{5,4},{6,5},{7,6},{8,11},{9,8},{10,9... | collective-permute-start | bytes 786440 | tf_op jit(solution)/shard_map/ppermute | solution.py:248
  44.1 0.7 copy-start.21
  44.8 26.0 %collective-permute-start.9 = (bf16[4,128,256]{2,1,0:T(8,128)(2,1)S(1)}, bf16[4,128,256]{2,1,0:T(8,128)(2,1)S(1)}, u32[]{:S(2)}, u32[]{:S(2)}) collective-permute-start(bf16[4,128,256]{2,1,0:T(8,128)(2,1)S(1)} %bitcast.48), channel_id=1, source_target_pairs={{0,3},{1,0},{2,1},{3,2},{4,7},{5,4},{6,5},{7,6},{8,11},{9,8},{10,9... | collective-permute-start | bytes 786440 | tf_op jit(solution)/shard_map/ppermute | solution.py:248
  44.8 4.9 %copy-start.5 = (bf16[4,128,640]{2,1,0:T(8,128)(2,1)}, bf16[4,128,640]{2,1,0:T(8,128)(2,1)S(1)}, u32[]{:S(2)}) copy-start(bf16[4,128,640]{2,1,0:T(8,128)(2,1)S(1)} %collective-permute-done.2.refs_7_.refs_8_) | copy-start | bytes 1966084
  44.8 37.5 %collective-permute-start.3 = (bf16[4,128,640]{2,1,0:T(8,128)(2,1)}, bf16[4,128,640]{2,1,0:T(8,128)(2,1)}, u32[]{:S(2)}, u32[]{:S(2)}) collective-permute-start(bf16[4,128,640]{2,1,0:T(8,128)(2,1)} %bitcast.14), channel_id=1, source_target_pairs={{0,3},{1,0},{2,1},{3,2},{4,7},{5,4},{6,5},{7,6},{8,11},{9,8},{10,9... | collective-permute-start | bytes 1966088 | tf_op jit(solution)/shard_map/ppermute | solution.py:248
  47.8 31.0 %copy-start.30 = (bf16[2,640]{1,0:T(2,128)(2,1)S(1)}, bf16[2,640]{1,0:T(2,128)(2,1)}, u32[]{:S(2)}) copy-start(bf16[2,640]{1,0:T(2,128)(2,1)} %param.10) | copy-start | bytes 7684
  47.8 38.8 %copy-start.2 = (bf16[448,448]{1,0:T(8,128)(2,1)S(1)}, bf16[448,448]{1,0:T(8,128)(2,1)}, u32[]{:S(2)}) copy-start(bf16[448,448]{1,0:T(8,128)(2,1)} %constant.30.clone.refs_1_) | copy-start | bytes 1204228
  49.7 0.7 copy-start.15
  50.4 59.5 %collective-permute-start.6 = (bf16[2,192,640]{2,1,0:T(8,128)(2,1)}, bf16[2,192,640]{2,1,0:T(8,128)(2,1)}, u32[]{:S(2)}, u32[]{:S(2)}) collective-permute-start(bf16[2,192,640]{2,1,0:T(8,128)(2,1)} %get-tuple-element.45), channel_id=1, source_target_pairs={{4,0},{8,4},{12,8},{16,12},{20,16},{24,20},{28,24},{5,1},{9,5},{13... | collective-permute-start | bytes 1474568 | tf_op jit(solution)/shard_map/ppermute | solution.py:268
  65.2 0.7 copy-start.17
  65.9 44.0 %collective-permute-start.4 = (bf16[2,192,640]{2,1,0:T(8,128)(2,1)}, bf16[2,192,640]{2,1,0:T(8,128)(2,1)}, u32[]{:S(2)}, u32[]{:S(2)}) collective-permute-start(bf16[2,192,640]{2,1,0:T(8,128)(2,1)} %get-tuple-element.46), channel_id=1, source_target_pairs={{0,4},{4,8},{8,12},{12,16},{16,20},{20,24},{24,28},{1,5},{5,9},{9,... | collective-permute-start | bytes 1474568 | tf_op jit(solution)/shard_map/ppermute | solution.py:268
  70.8 0.7 copy-start.19
  71.5 38.4 %collective-permute-start.5 = (bf16[2,256,640]{2,1,0:T(8,128)(2,1)}, bf16[2,256,640]{2,1,0:T(8,128)(2,1)}, u32[]{:S(2)}, u32[]{:S(2)}) collective-permute-start(bf16[2,256,640]{2,1,0:T(8,128)(2,1)} %pad_maximum_fusion), channel_id=1, source_target_pairs={{0,4},{4,8},{8,12},{12,16},{16,20},{20,24},{24,28},{1,5},{5,9},{9,... | collective-permute-start | bytes 1966088 | tf_op jit(solution)/shard_map/ppermute | solution.py:268
  73.4 0.8 copy-start.9
  74.3 35.7 %collective-permute-start.7 = (bf16[2,256,640]{2,1,0:T(8,128)(2,1)}, bf16[2,256,640]{2,1,0:T(8,128)(2,1)}, u32[]{:S(2)}, u32[]{:S(2)}) collective-permute-start(bf16[2,256,640]{2,1,0:T(8,128)(2,1)} %pad_maximum_fusion.1), channel_id=1, source_target_pairs={{4,0},{8,4},{12,8},{16,12},{20,16},{24,20},{28,24},{5,1},{9,5},{13... | collective-permute-start | bytes 1966088 | tf_op jit(solution)/shard_map/ppermute | solution.py:268
  82.3 21.6 %collective-permute-start.8 = (bf16[4,128,256]{2,1,0:T(8,128)(2,1)}, bf16[4,128,256]{2,1,0:T(8,128)(2,1)S(1)}, u32[]{:S(2)}, u32[]{:S(2)}) collective-permute-start(bf16[4,128,256]{2,1,0:T(8,128)(2,1)} %bitcast.47), channel_id=1, source_target_pairs={{0,1},{1,2},{2,3},{3,0},{4,5},{5,6},{6,7},{7,4},{8,9},{9,10},{10,1... | collective-permute-start | bytes 786440 | tf_op jit(solution)/shard_map/ppermute | solution.py:248
  86.6 2.6 copy-start
  89.3 1.1 copy-start.4
  90.3 1.1 copy-start.6
  91.4 0.9 copy-start.7
  92.4 1.1 copy-start.10
  93.4 0.9 copy-start.22
  94.3 3.6 %copy-start.16 = (bf16[4,128,256]{2,1,0:T(8,128)(2,1)S(1)}, bf16[4,128,256]{2,1,0:T(8,128)(2,1)}, u32[]{:S(2)}) copy-start(bf16[4,128,256]{2,1,0:T(8,128)(2,1)} %copy-done.15) | copy-start | bytes 786436
  94.4 3.6 %copy-start.18 = (bf16[4,128,256]{2,1,0:T(8,128)(2,1)S(1)}, bf16[4,128,256]{2,1,0:T(8,128)(2,1)}, u32[]{:S(2)}) copy-start(bf16[4,128,256]{2,1,0:T(8,128)(2,1)} %copy-done.17) | copy-start | bytes 786436
  97.9 6.0 %copy-start.20 = (bf16[4,128,256]{2,1,0:T(8,128)(2,1)S(1)}, bf16[4,128,256]{2,1,0:T(8,128)(2,1)}, u32[]{:S(2)}) copy-start(bf16[4,128,256]{2,1,0:T(8,128)(2,1)} %copy-done.19) | copy-start | bytes 786436
  109.9 11.5 %copy-start.13 = (bf16[640,1280]{1,0:T(8,128)(2,1)S(1)}, bf16[640,1280]{1,0:T(8,128)(2,1)}, u32[]{:S(2)}) copy-start(bf16[640,1280]{1,0:T(8,128)(2,1)} %get-tuple-element.37.w_in) | copy-start | bytes 4915204
  109.9 11.5 %copy-start.14 = (bf16[1280,640]{1,0:T(8,128)(2,1)S(1)}, bf16[1280,640]{1,0:T(8,128)(2,1)}, u32[]{:S(2)}) copy-start(bf16[1280,640]{1,0:T(8,128)(2,1)} %get-tuple-element.35.w_out) | copy-start | bytes 4915204
  125.5 34.6 %collective-permute-start.14 = (bf16[4,128,640]{2,1,0:T(8,128)(2,1)S(1)}, bf16[4,128,640]{2,1,0:T(8,128)(2,1)S(1)}, u32[]{:S(2)}, u32[]{:S(2)}) collective-permute-start(bf16[4,128,640]{2,1,0:T(8,128)(2,1)S(1)} %get-tuple-element.25), channel_id=1, source_target_pairs={{0,1},{1,2},{2,3},{3,0},{4,5},{5,6},{6,7},{7,4},{8,9},{9,10},{10,1... | collective-permute-start | bytes 1966088 | tf_op jit(solution)/shard_map/ppermute | solution.py:248
  129.8 33.2 %collective-permute-start.22 = (bf16[4,128,128]{2,1,0:T(8,128)(2,1)S(1)}, bf16[4,128,128]{2,1,0:T(8,128)(2,1)S(1)}, u32[]{:S(2)}, u32[]{:S(2)}) collective-permute-start(bf16[4,128,128]{2,1,0:T(8,128)(2,1)S(1)} %get-tuple-element.33), channel_id=1, source_target_pairs={{0,1},{1,2},{2,3},{3,0},{4,5},{5,6},{6,7},{7,4},{8,9},{9,10},{10,1... | collective-permute-start | bytes 393224 | tf_op jit(solution)/shard_map/ppermute | solution.py:248
  129.8 33.1 %collective-permute-start.23 = (bf16[4,128,128]{2,1,0:T(8,128)(2,1)S(1)}, bf16[4,128,128]{2,1,0:T(8,128)(2,1)S(1)}, u32[]{:S(2)}, u32[]{:S(2)}) collective-permute-start(bf16[4,128,128]{2,1,0:T(8,128)(2,1)S(1)} %get-tuple-element.34), channel_id=1, source_target_pairs={{0,3},{1,0},{2,1},{3,2},{4,7},{5,4},{6,5},{7,6},{8,11},{9,8},{10,9... | collective-permute-start | bytes 393224 | tf_op jit(solution)/shard_map/ppermute | solution.py:248
  131.9 31.1 %collective-permute-start.17 = (bf16[4,128,640]{2,1,0:T(8,128)(2,1)S(1)}, bf16[4,128,640]{2,1,0:T(8,128)(2,1)S(1)}, u32[]{:S(2)}, u32[]{:S(2)}) collective-permute-start(bf16[4,128,640]{2,1,0:T(8,128)(2,1)S(1)} %get-tuple-element.28), channel_id=1, source_target_pairs={{0,3},{1,0},{2,1},{3,2},{4,7},{5,4},{6,5},{7,6},{8,11},{9,8},{10,9... | collective-permute-start | bytes 1966088 | tf_op jit(solution)/shard_map/ppermute | solution.py:248
  137.9 79.4 %collective-permute-start.15 = (bf16[4,128,640]{2,1,0:T(8,128)(2,1)S(1)}, bf16[4,128,640]{2,1,0:T(8,128)(2,1)S(1)}, u32[]{:S(2)}, u32[]{:S(2)}) collective-permute-start(bf16[4,128,640]{2,1,0:T(8,128)(2,1)S(1)} %get-tuple-element.26), channel_id=1, source_target_pairs={{0,1},{1,2},{2,3},{3,0},{4,5},{5,6},{6,7},{7,4},{8,9},{9,10},{10,1... | collective-permute-start | bytes 1966088 | tf_op jit(solution)/shard_map/ppermute | solution.py:248
  160.1 60.8 %collective-permute-start.18 = (bf16[4,128,640]{2,1,0:T(8,128)(2,1)S(1)}, bf16[4,128,640]{2,1,0:T(8,128)(2,1)S(1)}, u32[]{:S(2)}, u32[]{:S(2)}) collective-permute-start(bf16[4,128,640]{2,1,0:T(8,128)(2,1)S(1)} %get-tuple-element.29), channel_id=1, source_target_pairs={{0,3},{1,0},{2,1},{3,2},{4,7},{5,4},{6,5},{7,6},{8,11},{9,8},{10,9... | collective-permute-start | bytes 1966088 | tf_op jit(solution)/shard_map/ppermute | solution.py:248
  163.0 34.1 %collective-permute-start.16 = (bf16[4,128,256]{2,1,0:T(8,128)(2,1)S(1)}, bf16[4,128,256]{2,1,0:T(8,128)(2,1)S(1)}, u32[]{:S(2)}, u32[]{:S(2)}) collective-permute-start(bf16[4,128,256]{2,1,0:T(8,128)(2,1)S(1)} %get-tuple-element.27), channel_id=1, source_target_pairs={{0,1},{1,2},{2,3},{3,0},{4,5},{5,6},{6,7},{7,4},{8,9},{9,10},{10,1... | collective-permute-start | bytes 786440 | tf_op jit(solution)/shard_map/ppermute | solution.py:248
  163.0 49.8 %collective-permute-start.20 = (bf16[4,128,256]{2,1,0:T(8,128)(2,1)S(1)}, bf16[4,128,256]{2,1,0:T(8,128)(2,1)S(1)}, u32[]{:S(2)}, u32[]{:S(2)}) collective-permute-start(bf16[4,128,256]{2,1,0:T(8,128)(2,1)S(1)} %get-tuple-element.31), channel_id=1, source_target_pairs={{0,1},{1,2},{2,3},{3,0},{4,5},{5,6},{6,7},{7,4},{8,9},{9,10},{10,1... | collective-permute-start | bytes 786440 | tf_op jit(solution)/shard_map/ppermute | solution.py:248
  163.0 52.1 %collective-permute-start.21 = (bf16[4,128,256]{2,1,0:T(8,128)(2,1)S(1)}, bf16[4,128,256]{2,1,0:T(8,128)(2,1)S(1)}, u32[]{:S(2)}, u32[]{:S(2)}) collective-permute-start(bf16[4,128,256]{2,1,0:T(8,128)(2,1)S(1)} %get-tuple-element.32), channel_id=1, source_target_pairs={{0,3},{1,0},{2,1},{3,2},{4,7},{5,4},{6,5},{7,6},{8,11},{9,8},{10,9... | collective-permute-start | bytes 786440 | tf_op jit(solution)/shard_map/ppermute | solution.py:248
  165.1 58.7 %copy-start.25 = (bf16[2,5,256,640]{3,2,1,0:T(8,128)(2,1)S(1)}, bf16[2,5,256,640]{3,2,1,0:T(8,128)(2,1)}, u32[]{:S(2)}) copy-start(bf16[2,5,256,640]{3,2,1,0:T(8,128)(2,1)} %param.9) | copy-start | bytes 9830404
  165.1 58.6 %copy-start.27 = (bf16[448,256,1]{1,0,2:T(8,128)(2,1)S(1)}, bf16[448,256,1]{1,0,2:T(8,128)(2,1)}, u32[]{:S(2)}) copy-start(bf16[448,256,1]{1,0,2:T(8,128)(2,1)} %constant.34) | copy-start | bytes 688132
  197.0 36.0 %collective-permute-start.19 = (bf16[4,128,256]{2,1,0:T(8,128)(2,1)S(1)}, bf16[4,128,256]{2,1,0:T(8,128)(2,1)S(1)}, u32[]{:S(2)}, u32[]{:S(2)}) collective-permute-start(bf16[4,128,256]{2,1,0:T(8,128)(2,1)S(1)} %get-tuple-element.30), channel_id=1, source_target_pairs={{0,3},{1,0},{2,1},{3,2},{4,7},{5,4},{6,5},{7,6},{8,11},{9,8},{10,9... | collective-permute-start | bytes 786440 | tf_op jit(solution)/shard_map/ppermute | solution.py:248
  212.8 25.7 %collective-permute-start.26 = (bf16[2,192,640]{2,1,0:T(8,128)(2,1)S(1)}, bf16[2,192,640]{2,1,0:T(8,128)(2,1)S(1)}, u32[]{:S(2)}, u32[]{:S(2)}) collective-permute-start(bf16[2,192,640]{2,1,0:T(8,128)(2,1)S(1)} %get-tuple-element.49), channel_id=1, source_target_pairs={{4,0},{8,4},{12,8},{16,12},{20,16},{24,20},{28,24},{5,1},{9,5},{13... | collective-permute-start | bytes 1474568 | tf_op jit(solution)/shard_map/ppermute | solution.py:268
  215.1 9.6 %copy-start.8 = (bf16[192,448]{1,0:T(8,128)(2,1)S(1)}, bf16[192,448]{1,0:T(8,128)(2,1)}, u32[]{:S(2)}) copy-start(bf16[192,448]{1,0:T(8,128)(2,1)} %constant.31.clone.refs_2_) | copy-start | bytes 516100
  215.1 23.3 %collective-permute-start.24 = (bf16[2,192,640]{2,1,0:T(8,128)(2,1)S(1)}, bf16[2,192,640]{2,1,0:T(8,128)(2,1)S(1)}, u32[]{:S(2)}, u32[]{:S(2)}) collective-permute-start(bf16[2,192,640]{2,1,0:T(8,128)(2,1)S(1)} %get-tuple-element.50), channel_id=1, source_target_pairs={{0,4},{4,8},{8,12},{12,16},{16,20},{20,24},{24,28},{1,5},{5,9},{9,... | collective-permute-start | bytes 1474568 | tf_op jit(solution)/shard_map/ppermute | solution.py:268
  217.3 25.1 %collective-permute-start.25 = (bf16[2,256,640]{2,1,0:T(8,128)(2,1)S(1)}, bf16[2,256,640]{2,1,0:T(8,128)(2,1)S(1)}, u32[]{:S(2)}, u32[]{:S(2)}) collective-permute-start(bf16[2,256,640]{2,1,0:T(8,128)(2,1)S(1)} %pad_maximum_fusion.2), channel_id=1, source_target_pairs={{0,4},{4,8},{8,12},{12,16},{16,20},{20,24},{24,28},{1,5},{5,9},{9,... | collective-permute-start | bytes 1966088 | tf_op jit(solution)/shard_map/ppermute | solution.py:268
  220.9 21.4 %collective-permute-start.27 = (bf16[2,256,640]{2,1,0:T(8,128)(2,1)S(1)}, bf16[2,256,640]{2,1,0:T(8,128)(2,1)S(1)}, u32[]{:S(2)}, u32[]{:S(2)}) collective-permute-start(bf16[2,256,640]{2,1,0:T(8,128)(2,1)S(1)} %pad_maximum_fusion.3), channel_id=1, source_target_pairs={{4,0},{8,4},{12,8},{16,12},{20,16},{24,20},{28,24},{5,1},{9,5},{13... | collective-permute-start | bytes 1966088 | tf_op jit(solution)/shard_map/ppermute | solution.py:268
  238.4 13.9 %copy-start.11 = (bf16[640,1280]{1,0:T(8,128)(2,1)S(1)}, bf16[640,1280]{1,0:T(8,128)(2,1)}, u32[]{:S(2)}) copy-start(bf16[640,1280]{1,0:T(8,128)(2,1)} %get-tuple-element.38.w_in) | copy-start | bytes 4915204
  238.4 13.9 %copy-start.12 = (bf16[1280,640]{1,0:T(8,128)(2,1)S(1)}, bf16[1280,640]{1,0:T(8,128)(2,1)}, u32[]{:S(2)}) copy-start(bf16[1280,640]{1,0:T(8,128)(2,1)} %get-tuple-element.36.w_out) | copy-start | bytes 4915204
where the time goes:
time: 266 us; the launch traced here: 265 us
  waiting for transfers between devices  102 us (38%)
  Pallas kernels  78.1 us (29%)
  starting transfers between devices  55.1 us (21%)
  local copies, waits for them, and re-layouts  23.6 us (9%)
  matrix products  4.36 us (2%)
    ppermute x20, waiting for transfers between devices, rotate(): lax.ppermute(block, axis, [(i, (i + hops) % count) for i in range(count)])  97.7 us
    pallas_call x8, Pallas kernels, convolve(): pl.pallas_call(kernel, grid=(blocks,), out_shape=out, in_specs=[pl.BlockS...  50.5 us
    ppermute x20, starting transfers between devices, rotate(): lax.ppermute(block, axis, [(i, (i + hops) % count) for i in range(count)])  33.9 us
    pallas_call x5, Pallas kernels, mlp(): pl.pallas_call(functools.partial(mlp_kernel, half=edge, kept=len(extra),...  25.2 us
    ppermute x8, starting transfers between devices, step_rows(): return lax.ppermute(block, 'lat', pairs)  21.2 us
    unnamed x62, local copies, waits for them, and re-layouts  12 us
    squeeze x2, local copies, waits for them, and re-layouts, body(): weights = (gains[layer], input_weight[layer], output_weight[layer])  6.02 us
  transfers between devices with their start and end apart: 28, of which 9 were waited for; matrix products, arithmetic and copies ran while one was open for 6% of the time, Pallas kernels for 15%

commit v1 on v0

--- a/solution.py
+++ b/solution.py
@@ -216,33 +216,6 @@
     )(gain, w_in, w_out, *(list(mixed) * together), *extra)
 
 
-def edge_kernel(state, first, last, sems, *, spans):
-    edge, width = first.shape[1], state.shape[1]
-    copies = []
-    for k, (row, at, count) in enumerate(spans):
-        for side, (target, lon) in enumerate([(last, width - edge), (first, 0)]):
-            source = state.at[pl.ds(row, count), pl.ds(lon, edge)]
-            copy = pltpu.make_async_copy(source, target.at[pl.ds(at, count)], sems.at[2 * k + side])
-            copy.start()
-            copies.append(copy)
-    for copy in copies:
-        copy.wait()
-
-
-def edges(state, spans, edge):
-    rows = sum(count for _, _, count in spans)
-    out = jax.ShapeDtypeStruct((rows, edge, state.shape[2]), state.dtype)
-    return pl.pallas_call(
-        functools.partial(edge_kernel, spans=spans),
-        out_shape=[out, out],
-        in_specs=[pl.BlockSpec(memory_space=pltpu.HBM)],
-        out_specs=[pl.BlockSpec(memory_space=pltpu.VMEM)] * 2,
-        scratch_shapes=[pltpu.SemaphoreType.DMA((2 * len(spans),))],
-        compiler_params=pltpu.CompilerParams(vmem_limit_bytes=60 << 20),
-        name="edges",
-    )(state)
-
-
 def rotate(block, axis, hops):
     count = lax.axis_size(axis)
     return lax.ppermute(block, axis, [(i, (i + hops) % count) for i in range(count)])
@@ -317,9 +290,10 @@
     lanes = [slice(0, channels)] * 2 + pieces
     groups_of = [groups[0], groups[1]] + [groups[2]] * len(parts)
     head, tail = slice(0, edge), slice(width - edge, width)
-    first, last = edges(state, [(0, 0, rim), (rows - rim, rim, rim)], edge)
-    firsts, lasts = [first], [last]
-    pairs, _ = lax.optimization_barrier((pairs, first[:1, :1, :1]))
+    lasts = [pick(pairs, groups[0], tail, lanes[0])]
+    pairs, _ = lax.optimization_barrier((pairs, lasts[0]))
+    firsts = [pick(pairs, groups[0], head, lanes[0])]
+    pairs, _ = lax.optimization_barrier((pairs, firsts[0]))
     firsts += [pick(pairs, members, head, cut) for members, cut in zip(groups_of[1:], lanes[1:])]
     lasts += [pick(pairs, members, tail, cut) for members, cut in zip(groups_of[1:], lanes[1:])]
     tables = (forward, inverse)

time: 266 us -> 266 us (level)
  waiting for transfers between devices: 102 us -> 115 us
  starting transfers between devices: 55.1 us -> 44 us
    ppermute x20, waiting for transfers between devices: 97.7 us -> 112 us  [rotate(): lax.ppermute(block, axis, [(i, (i + hops) % count) for i in range(count)])]
    ppermute x20, starting transfers between devices: 33.9 us -> 22.8 us  [rotate(): lax.ppermute(block, axis, [(i, (i + hops) % count) for i in range(count)])]
    unnamed x62 -> x60, local copies, waits for them, and re-layouts: 12 us -> 13 us
  transfers between devices with their start and end apart: 28 -> 28, of which waited for: 9 -> 10; matrix products, arithmetic and copies ran while one was open for 6% -> 6% of each run, Pallas kernels for 15% -> 14%
where the time goes in v1:
time: 266 us
  waiting for transfers between devices  115 us (43%)
  Pallas kernels  75.7 us (28%)
  starting transfers between devices  44 us (17%)
  local copies, waits for them, and re-layouts  23.7 us (9%)
  matrix products  4.35 us (2%)
    ppermute x20, waiting for transfers between devices, rotate(): lax.ppermute(block, axis, [(i, (i + hops) % count) for i in range(count)])  112 us
    pallas_call x8, Pallas kernels, convolve(): pl.pallas_call(kernel, grid=(blocks,), out_shape=out, in_specs=[pl.BlockS...  50.5 us
    pallas_call x5, Pallas kernels, mlp(): pl.pallas_call(functools.partial(mlp_kernel, half=edge, kept=len(extra),...  25.2 us
    ppermute x20, starting transfers between devices, rotate(): lax.ppermute(block, axis, [(i, (i + hops) % count) for i in range(count)])  22.8 us
    ppermute x8, starting transfers between devices, step_rows(): return lax.ppermute(block, 'lat', pairs)  21.2 us
    unnamed x60, local copies, waits for them, and re-layouts  13 us
  transfers between devices with their start and end apart: 28, of which 10 were waited for; matrix products, arithmetic and copies ran while one was open for 6% of the time, Pallas kernels for 14%

profile of v1, /device:TPU:20, one launch (start us, length us, event | category | flops | bytes accessed | tf_op | source)
XLA Modules:
  0.0 265.7 jit_solution(1459189105440296604)
XLA Ops:
  0.0 1.3 slice.100
  1.3 1.6 collective-permute-start
  2.9 1.1 slice.101
  4.6 1.0 fusion.4
  5.6 1.6 collective-permute-start.12
  7.7 0.8 fusion.5
  8.5 1.6 collective-permute-start.10
  10.1 1.0 fusion.7
  11.1 1.9 slice_bitcast_fusion.1
  13.1 1.2 copy-done.24
  14.2 2.0 slice_bitcast_fusion
  16.2 1.1 fusion.6
  17.8 3.4 %convolution_bitcast_fusion.refs_3_ = f32[5,448,640]{2,1,0:T(8,128)} fusion(bf16[448,256,1]{1,0,2:T(8,128)(2,1)S(1)} %copy-done.27, bf16[2,5,256,640]{3,2,1,0:T(8,128)(2,1)S(1)} %copy-done.25), kind=kOutput, calls=%fused_computation | convolution fusion | flops 734003200 | bytes 7602176 | tf_op jit(solution)/shard_map/kt,rtc->rkc/dot_general | solution.py:265
  21.2 11.6 %collective-permute-done.2.refs_7_.refs_8_ = bf16[4,128,640]{2,1,0:T(8,128)(2,1)S(1)} collective-permute-done((bf16[4,128,640]{2,1,0:T(8,128)(2,1)S(1)}, bf16[4,128,640]{2,1,0:T(8,128)(2,1)S(1)}, u32[]{:S(2)}, u32[]{:S(2)}) %collective-permute-start.2) | collective-permute-done | bytes 655392 | tf_op jit(solution)/shard_map/ppermute | solution.py:221
  32.8 1.6 collective-permute-start.1
  34.5 4.2 %collective-permute-done.12.refs_7_ = bf16[4,128,128]{2,1,0:T(8,128)(2,1)S(1)} collective-permute-done((bf16[4,128,128]{2,1,0:T(8,128)(2,1)S(1)}, bf16[4,128,128]{2,1,0:T(8,128)(2,1)S(1)}, u32[]{:S(2)}, u32[]{:S(2)}) %collective-permute-start.12) | collective-permute-done | bytes 131104 | tf_op jit(solution)/shard_map/ppermute | solution.py:221
  39.3 1.3 collective-permute-start.9
  40.6 3.2 %collective-permute-start.3 = (bf16[4,128,640]{2,1,0:T(8,128)(2,1)}, bf16[4,128,640]{2,1,0:T(8,128)(2,1)}, u32[]{:S(2)}, u32[]{:S(2)}) collective-permute-start(bf16[4,128,640]{2,1,0:T(8,128)(2,1)} %bitcast.17), channel_id=1, source_target_pairs={{0,3},{1,0},{2,1},{3,2},{4,7},{5,4},{6,5},{7,6},{8,11},{9,8},{10,9... | collective-permute-start | bytes 1966088 | tf_op jit(solution)/shard_map/ppermute | solution.py:221
  43.9 0.9 pad_maximum_fusion.1
  44.8 0.9 pad_maximum_fusion
  45.7 0.7 copy-done.15
  46.4 1.9 collective-permute-start.6
  48.4 15.4 %collective-permute-done.11.refs_10_ = bf16[4,128,256]{2,1,0:T(8,128)(2,1)S(1)} collective-permute-done((bf16[4,128,256]{2,1,0:T(8,128)(2,1)S(1)}, bf16[4,128,256]{2,1,0:T(8,128)(2,1)S(1)}, u32[]{:S(2)}, u32[]{:S(2)}) %collective-permute-start.11) | collective-permute-done | bytes 262176 | tf_op jit(solution)/shard_map/ppermute | solution.py:221
  63.8 0.7 copy-done.17
  64.5 1.9 collective-permute-start.4
  66.4 3.0 %collective-permute-done.9.refs_10_ = bf16[4,128,256]{2,1,0:T(8,128)(2,1)S(1)} collective-permute-done((bf16[4,128,256]{2,1,0:T(8,128)(2,1)S(1)}, bf16[4,128,256]{2,1,0:T(8,128)(2,1)S(1)}, u32[]{:S(2)}, u32[]{:S(2)}) %collective-permute-start.9) | collective-permute-done | bytes 262176 | tf_op jit(solution)/shard_map/ppermute | solution.py:221
  69.4 0.7 copy-done.19
  70.1 1.9 collective-permute-start.5
  72.0 0.8 copy-done.9
  72.9 4.5 %collective-permute-start.7 = (bf16[2,256,640]{2,1,0:T(8,128)(2,1)}, bf16[2,256,640]{2,1,0:T(8,128)(2,1)}, u32[]{:S(2)}, u32[]{:S(2)}) collective-permute-start(bf16[2,256,640]{2,1,0:T(8,128)(2,1)} %pad_maximum_fusion.1), channel_id=1, source_target_pairs={{4,0},{8,4},{12,8},{16,12},{20,16},{24,20},{28,24},{5,1},{9,5},{13... | collective-permute-start | bytes 1966088 | tf_op jit(solution)/shard_map/ppermute | solution.py:241
  77.4 5.0 %collective-permute-done.3.refs_8_.refs_9_ = bf16[4,128,640]{2,1,0:T(8,128)(2,1)} collective-permute-done((bf16[4,128,640]{2,1,0:T(8,128)(2,1)}, bf16[4,128,640]{2,1,0:T(8,128)(2,1)}, u32[]{:S(2)}, u32[]{:S(2)}) %collective-permute-start.3) | collective-permute-done | bytes 655392 | tf_op jit(solution)/shard_map/ppermute | solution.py:221
  82.5 4.4 %collective-permute-start.8 = (bf16[4,128,256]{2,1,0:T(8,128)(2,1)}, bf16[4,128,256]{2,1,0:T(8,128)(2,1)S(1)}, u32[]{:S(2)}, u32[]{:S(2)}) collective-permute-start(bf16[4,128,256]{2,1,0:T(8,128)(2,1)} %bitcast.52), channel_id=1, source_target_pairs={{0,1},{1,2},{2,3},{3,0},{4,5},{5,6},{6,7},{7,4},{8,9},{9,10},{10,1... | collective-permute-start | bytes 786440 | tf_op jit(solution)/shard_map/ppermute | solution.py:221
  86.9 2.6 copy-done
  89.5 1.1 copy-done.4
  90.6 1.1 copy-done.6
  91.7 0.9 copy-done.7
  92.6 1.1 copy-done.10
  93.7 0.9 copy-done.22
  94.6 3.5 %zonal_conv.11.refs_2_ = bf16[8,192,128]{2,1,0:T(8,128)(2,1)S(1)} custom-call(f32[16]{0:T(128)S(1)} %and_select_fusion.refs_0_, bf16[448,448]{1,0:T(8,128)(2,1)S(1)} %copy-done.2, bf16[192,448]{1,0:T(8,128)(2,1)S(1)} %copy-done.7, f32[5,448,640]{2,1,0:T(8,128)S(1)} %copy-done, bf16[12,192,640]{2,1,0:T(8,128)(2,1)S(1)} %bitcast.45, ...), custom_call_target="tpu_custom_call" | custom-call | flops 792723456 | bytes 2523136 | tf_op jit(solution)/shard_map/zonal_conv/pallas_call | solution.py:113
  98.2 5.9 %zonal_conv.10.refs_1_ = bf16[8,192,256]{2,1,0:T(8,128)(2,1)S(1)} custom-call(f32[16]{0:T(128)S(1)} %and_select_fusion.refs_0_, bf16[448,448]{1,0:T(8,128)(2,1)S(1)} %copy-done.2, bf16[192,448]{1,0:T(8,128)(2,1)S(1)} %copy-done.7, f32[5,448,640]{2,1,0:T(8,128)S(1)} %copy-done, bf16[12,192,640]{2,1,0:T(8,128)(2,1)S(1)} %bitcast.46, ...), custom_call_target="tpu_custom_call" | custom-call | flops 1585446912 | bytes 5046272 | tf_op jit(solution)/shard_map/zonal_conv/pallas_call | solution.py:113
  104.2 5.9 %zonal_conv.9.refs_0_ = bf16[8,192,256]{2,1,0:T(8,128)(2,1)S(1)} custom-call(f32[16]{0:T(128)S(1)} %and_select_fusion.refs_0_, bf16[448,448]{1,0:T(8,128)(2,1)S(1)} %copy-done.2, bf16[192,448]{1,0:T(8,128)(2,1)S(1)} %copy-done.7, f32[5,448,640]{2,1,0:T(8,128)S(1)} %copy-done, bf16[12,192,640]{2,1,0:T(8,128)(2,1)S(1)} %bitcast.47, ...), custom_call_target="tpu_custom_call" | custom-call | flops 1585446912 | bytes 5046272 | tf_op jit(solution)/shard_map/zonal_conv/pallas_call | solution.py:113
  110.2 11.4 %zonal_conv.8.refs_0_ = bf16[4,192,640]{2,1,0:T(8,128)(2,1)S(1)} custom-call(f32[16]{0:T(128)S(1)} %and_select_fusion.refs_0_, bf16[448,448]{1,0:T(8,128)(2,1)S(1)} %copy-done.2, bf16[192,448]{1,0:T(8,128)(2,1)S(1)} %copy-done.7, f32[5,448,640]{2,1,0:T(8,128)S(1)} %copy-done, bf16[12,192,640]{2,1,0:T(8,128)(2,1)S(1)} %bitcast.48, ...), custom_call_target="tpu_custom_call" | custom-call | flops 3523215360 | bytes 12615680 | tf_op jit(solution)/shard_map/zonal_conv/pallas_call | solution.py:113
  121.7 4.1 %channel_mlp.5 = (bf16[4,192,640]{2,1,0:T(8,128)(2,1)S(1)}, bf16[4,128,640]{2,1,0:T(8,128)(2,1)S(1)}, bf16[4,128,640]{2,1,0:T(8,128)(2,1)S(1)}) custom-call(f32[1,640]{1,0:T(1,128)S(1)} %get-tuple-element.59.gain, bf16[640,1280]{1,0:T(8,128)(2,1)S(1)} %copy-done.13, bf16[1280,640]{1,0:T(8,128)(2,1)S(1)} %copy-done.14, bf16[4,192,640]{2,1,0:T(8,128)(2,1)S(1)} %zonal_conv.8.refs_0_), custom_call_target="tpu_custom_call" | custom-call | flops 2516582400 | bytes 5242880 | tf_op jit(solution)/shard_map/channel_mlp/pallas_call | solution.py:196
  126.0 4.0 %channel_mlp.7 = (bf16[4,192,640]{2,1,0:T(8,128)(2,1)S(1)}, bf16[4,128,256]{2,1,0:T(8,128)(2,1)S(1)}, bf16[4,128,256]{2,1,0:T(8,128)(2,1)S(1)}, bf16[4,128,256]{...) custom-call(f32[1,640]{1,0:T(1,128)S(1)} %get-tuple-element.59.gain,, ...), custom_call_target="tpu_custom_call" | custom-call | flops 2516582400 | bytes 5242880 | tf_op jit(solution)/shard_map/channel_mlp/pallas_call | solution.py:196
  130.1 2.0 collective-permute-start.23
  132.2 2.0 collective-permute-start.17
  134.1 4.0 %channel_mlp.6 = (bf16[4,192,640]{2,1,0:T(8,128)(2,1)S(1)}, bf16[4,128,640]{2,1,0:T(8,128)(2,1)S(1)}, bf16[4,128,640]{2,1,0:T(8,128)(2,1)S(1)}) custom-call(f32[1,640]{1,0:T(1,128)S(1)} %get-tuple-element.59.gain, bf16[640,1280]{1,0:T(8,128)(2,1)S(1)} %copy-done.13, bf16[1280,640]{1,0:T(8,128)(2,1)S(1)} %copy-done.14, ...), custom_call_target="tpu_custom_call" | custom-call | flops 2516582400 | bytes 5242880 | tf_op jit(solution)/shard_map/channel_mlp/pallas_call | solution.py:196
  138.4 22.1 %collective-permute-done.14.refs_7_.refs_6_ = bf16[4,128,640]{2,1,0:T(8,128)(2,1)S(1)} collective-permute-done((bf16[4,128,640]{2,1,0:T(8,128)(2,1)S(1)}, bf16[4,128,640]{2,1,0:T(8,128)(2,1)S(1)}, u32[]{:S(2)}, u32[]{:S(2)}) %collective-permute-start.14) | collective-permute-done | bytes 655392 | tf_op jit(solution)/shard_map/ppermute | solution.py:221
  160.5 2.7 %collective-permute-done.22.refs_9_ = bf16[4,128,128]{2,1,0:T(8,128)(2,1)S(1)} collective-permute-done((bf16[4,128,128]{2,1,0:T(8,128)(2,1)S(1)}, bf16[4,128,128]{2,1,0:T(8,128)(2,1)S(1)}, u32[]{:S(2)}, u32[]{:S(2)}) %collective-permute-start.22) | collective-permute-done | bytes 131104 | tf_op jit(solution)/shard_map/ppermute | solution.py:221
  163.3 2.0 collective-permute-start.21
  165.5 31.9 %collective-permute-done.16.refs_9_ = bf16[4,128,256]{2,1,0:T(8,128)(2,1)S(1)} collective-permute-done((bf16[4,128,256]{2,1,0:T(8,128)(2,1)S(1)}, bf16[4,128,256]{2,1,0:T(8,128)(2,1)S(1)}, u32[]{:S(2)}, u32[]{:S(2)}) %collective-permute-start.16) | collective-permute-done | bytes 262176 | tf_op jit(solution)/shard_map/ppermute | solution.py:221
  197.5 15.6 %collective-permute-done.20.refs_9_ = bf16[4,128,256]{2,1,0:T(8,128)(2,1)S(1)} collective-permute-done((bf16[4,128,256]{2,1,0:T(8,128)(2,1)S(1)}, bf16[4,128,256]{2,1,0:T(8,128)(2,1)S(1)}, u32[]{:S(2)}, u32[]{:S(2)}) %collective-permute-start.20) | collective-permute-done | bytes 262176 | tf_op jit(solution)/shard_map/ppermute | solution.py:221
  213.1 2.3 collective-permute-start.26
  215.4 2.1 collective-permute-start.24
  217.6 3.7 %collective-permute-start.25 = (bf16[2,256,640]{2,1,0:T(8,128)(2,1)S(1)}, bf16[2,256,640]{2,1,0:T(8,128)(2,1)S(1)}, u32[]{:S(2)}, u32[]{:S(2)}) collective-permute-start(bf16[2,256,640]{2,1,0:T(8,128)(2,1)S(1)} %pad_maximum_fusion.2), channel_id=1, source_target_pairs={{0,4},{4,8},{8,12},{12,16},{16,20},{20,24},{24,28},{1,5},{5,9},{9,... | collective-permute-start | bytes 1966088 | tf_op jit(solution)/shard_map/ppermute | solution.py:241
  221.2 2.8 %collective-permute-start.27 = (bf16[2,256,640]{2,1,0:T(8,128)(2,1)S(1)}, bf16[2,256,640]{2,1,0:T(8,128)(2,1)S(1)}, u32[]{:S(2)}, u32[]{:S(2)}) collective-permute-start(bf16[2,256,640]{2,1,0:T(8,128)(2,1)S(1)} %pad_maximum_fusion.3), channel_id=1, source_target_pairs={{4,0},{8,4},{12,8},{16,12},{20,16},{24,20},{28,24},{5,1},{9,5},{13... | collective-permute-start | bytes 1966088 | tf_op jit(solution)/shard_map/ppermute | solution.py:241
  224.1 0.9 convolution_bitcast_fusion.1.refs_3_
  225.0 2.9 %zonal_conv.14.refs_2_.refs_5_ = bf16[8,192,128]{2,1,0:T(8,128)(2,1)S(1)} custom-call(f32[16]{0:T(128)S(1)} %and_select_fusion.refs_0_, bf16[448,448]{1,0:T(8,128)(2,1)S(1)} %copy-done.2, bf16[192,448]{1,0:T(8,128)(2,1)S(1)} %copy-done.8, f32[5,448,640]{2,1,0:T(8,128)S(1)} %convolution_bitcast_fusion.1.refs_3_, ...), custom_call_target="tpu_custom_call" | custom-call | flops 792723456 | bytes 2523136 | tf_op jit(solution)/shard_map/zonal_conv/pallas_call | solution.py:113
  227.9 5.4 %zonal_conv.13.refs_1_.refs_4_ = bf16[8,192,256]{2,1,0:T(8,128)(2,1)S(1)} custom-call(f32[16]{0:T(128)S(1)} %and_select_fusion.refs_0_, bf16[448,448]{1,0:T(8,128)(2,1)S(1)} %copy-done.2, bf16[192,448]{1,0:T(8,128)(2,1)S(1)} %copy-done.8, f32[5,448,640]{2,1,0:T(8,128)S(1)} %convolution_bitcast_fusion.1.refs_3_, ...), custom_call_target="tpu_custom_call" | custom-call | flops 1585446912 | bytes 5046272 | tf_op jit(solution)/shard_map/zonal_conv/pallas_call | solution.py:113
  233.3 5.4 %zonal_conv.12.refs_0_.refs_3_ = bf16[8,192,256]{2,1,0:T(8,128)(2,1)S(1)} custom-call(f32[16]{0:T(128)S(1)} %and_select_fusion.refs_0_, bf16[448,448]{1,0:T(8,128)(2,1)S(1)} %copy-done.2, bf16[192,448]{1,0:T(8,128)(2,1)S(1)} %copy-done.8, f32[5,448,640]{2,1,0:T(8,128)S(1)} %convolution_bitcast_fusion.1.refs_3_, ...), custom_call_target="tpu_custom_call" | custom-call | flops 1585446912 | bytes 5046272 | tf_op jit(solution)/shard_map/zonal_conv/pallas_call | solution.py:113
  238.8 3.8 %collective-permute-done.25.refs_11_ = bf16[2,256,640]{2,1,0:T(8,128)(2,1)S(1)} collective-permute-done((bf16[2,256,640]{2,1,0:T(8,128)(2,1)S(1)}, bf16[2,256,640]{2,1,0:T(8,128)(2,1)S(1)}, u32[]{:S(2)}, u32[]{:S(2)}) %collective-permute-start.25) | collective-permute-done | bytes 655392 | tf_op jit(solution)/shard_map/ppermute | solution.py:241
  242.6 10.0 %zonal_conv.15.refs_0_ = bf16[4,192,640]{2,1,0:T(8,128)(2,1)S(1)} custom-call(f32[16]{0:T(128)S(1)} %and_select_fusion.refs_0_, bf16[448,448]{1,0:T(8,128)(2,1)S(1)} %copy-done.2, bf16[192,448]{1,0:T(8,128)(2,1)S(1)} %copy-done.8, f32[5,448,640]{2,1,0:T(8,128)S(1)} %convolution_bitcast_fusion.1.refs_3_, bf16[4,192,640]{2,1,0:T(8,128)(2,1)S(1)} %get-tuple-element.22.refs_4_, ...), custom_call_target="tpu_custom_call" | custom-call | flops 3523215360 | bytes 12615680 | tf_op jit(solution)/shard_map/zonal_conv/pallas_call | solution.py:113
  252.6 4.8 %channel_mlp.8.refs_6_ = bf16[12,192,640]{2,1,0:T(8,128)(2,1)} custom-call(f32[1,640]{1,0:T(1,128)S(1)} %get-tuple-element.60.gain, bf16[640,1280]{1,0:T(8,128)(2,1)S(1)} %copy-done.11, bf16[1280,640]{1,0:T(8,128)(2,1)S(1)} %copy-done.12, bf16[4,192,640]{2,1,0:T(8,128)(2,1)S(1)} %zonal_conv.15.refs_0_), custom_call_target="tpu_custom_call" | custom-call | flops 2516582400 | bytes 5242880 | tf_op jit(solution)/shard_map/channel_mlp/pallas_call | solution.py:196
  257.4 8.2 %channel_mlp.9 = bf16[12,192,640]{2,1,0:T(8,128)(2,1)} custom-call(f32[1,640]{1,0:T(1,128)S(1)} %get-tuple-element.60.gain, bf16[640,1280]{1,0:T(8,128)(2,1)S(1)} %copy-done.11, bf16[1280,640]{1,0:T(8,128)(2,1)S(1)} %copy-done.12, bf16[8,192,256]{2,1,0:T(8,128)(2,1)S(1)} %zonal_conv.12.refs_0_.refs_3_, ...), custom_call_target="tpu_custom_call", output_to_operand_aliasing={{}: (9, {})} | custom-call | flops 5033164800 | bytes 7208960 | tf_op jit(solution)/shard_map/channel_mlp/pallas_call | solution.py:196
  (86 shorter events, 3.2 us)
Async XLA Ops:
  0.0 7.7 %copy-start.1 = (bf16[1,12,640,192]{2,3,1,0:T(8,128)(2,1)S(1)}, bf16[1,12,640,192]{2,3,1,0:T(8,128)(2,1)}, u32[]{:S(2)}) copy-start(bf16[1,12,640,192]{2,3,1,0:T(8,128)(2,1)} %param.8) | copy-start | bytes 8847364
  1.3 39.3 %collective-permute-start = (bf16[4,128,640]{2,1,0:T(8,128)(2,1)S(1)}, bf16[4,128,640]{2,1,0:T(8,128)(2,1)S(1)}, u32[]{:S(2)}, u32[]{:S(2)}) collective-permute-start(bf16[4,128,640]{2,1,0:T(8,128)(2,1)S(1)} %bitcast.50), channel_id=1, source_target_pairs={{0,1},{1,2},{2,3},{3,0},{4,5},{5,6},{6,7},{7,4},{8,9},{9,10},{10,1... | collective-permute-start | bytes 1966088 | tf_op jit(solution)/shard_map/ppermute | solution.py:221
  4.1 28.7 %collective-permute-start.2 = (bf16[4,128,640]{2,1,0:T(8,128)(2,1)S(1)}, bf16[4,128,640]{2,1,0:T(8,128)(2,1)S(1)}, u32[]{:S(2)}, u32[]{:S(2)}) collective-permute-start(bf16[4,128,640]{2,1,0:T(8,128)(2,1)S(1)} %bitcast.51), channel_id=1, source_target_pairs={{0,3},{1,0},{2,1},{3,2},{4,7},{5,4},{6,5},{7,6},{8,11},{9,8},{10,9... | collective-permute-start | bytes 1966088 | tf_op jit(solution)/shard_map/ppermute | solution.py:221
  5.6 33.0 %collective-permute-start.12 = (bf16[4,128,128]{2,1,0:T(8,128)(2,1)S(1)}, bf16[4,128,128]{2,1,0:T(8,128)(2,1)S(1)}, u32[]{:S(2)}, u32[]{:S(2)}) collective-permute-start(bf16[4,128,128]{2,1,0:T(8,128)(2,1)S(1)} %bitcast.57), channel_id=1, source_target_pairs={{0,1},{1,2},{2,3},{3,0},{4,5},{5,6},{6,7},{7,4},{8,9},{9,10},{10,1... | collective-permute-start | bytes 393224 | tf_op jit(solution)/shard_map/ppermute | solution.py:221
  7.2 31.4 %collective-permute-start.13 = (bf16[4,128,128]{2,1,0:T(8,128)(2,1)S(1)}, bf16[4,128,128]{2,1,0:T(8,128)(2,1)S(1)}, u32[]{:S(2)}, u32[]{:S(2)}) collective-permute-start(bf16[4,128,128]{2,1,0:T(8,128)(2,1)S(1)} %bitcast.56), channel_id=1, source_target_pairs={{0,3},{1,0},{2,1},{3,2},{4,7},{5,4},{6,5},{7,6},{8,11},{9,8},{10,9... | collective-permute-start | bytes 393224 | tf_op jit(solution)/shard_map/ppermute | solution.py:221
  7.7 3.4 %copy-start.23 = (bf16[2,640,1280]{2,1,0:T(8,128)(2,1)S(1)}, bf16[2,640,1280]{2,1,0:T(8,128)(2,1)}, u32[]{:S(2)}) copy-start(bf16[2,640,1280]{2,1,0:T(8,128)(2,1)} %param.11) | copy-start | bytes 9830404
  8.5 37.2 %collective-permute-start.10 = (bf16[4,128,256]{2,1,0:T(8,128)(2,1)S(1)}, bf16[4,128,256]{2,1,0:T(8,128)(2,1)S(1)}, u32[]{:S(2)}, u32[]{:S(2)}) collective-permute-start(bf16[4,128,256]{2,1,0:T(8,128)(2,1)S(1)} %bitcast.55), channel_id=1, source_target_pairs={{0,1},{1,2},{2,3},{3,0},{4,5},{5,6},{6,7},{7,4},{8,9},{9,10},{10,1... | collective-permute-start | bytes 786440 | tf_op jit(solution)/shard_map/ppermute | solution.py:221
  11.1 3.1 %copy-start.24 = (bf16[2,1280,640]{2,1,0:T(8,128)(2,1)S(1)}, bf16[2,1280,640]{2,1,0:T(8,128)(2,1)}, u32[]{:S(2)}) copy-start(bf16[2,1280,640]{2,1,0:T(8,128)(2,1)} %param.12) | copy-start | bytes 9830404
  14.2 3.2 %copy-start.25 = (bf16[2,5,256,640]{3,2,1,0:T(8,128)(2,1)S(1)}, bf16[2,5,256,640]{3,2,1,0:T(8,128)(2,1)}, u32[]{:S(2)}) copy-start(bf16[2,5,256,640]{3,2,1,0:T(8,128)(2,1)} %param.9) | copy-start | bytes 9830404
  16.2 1.6 copy-start.27
  32.8 12.0 %copy-start.5 = (bf16[4,128,640]{2,1,0:T(8,128)(2,1)}, bf16[4,128,640]{2,1,0:T(8,128)(2,1)S(1)}, u32[]{:S(2)}) copy-start(bf16[4,128,640]{2,1,0:T(8,128)(2,1)S(1)} %collective-permute-done.2.refs_7_.refs_8_) | copy-start | bytes 1966084
  32.8 39.2 %collective-permute-start.1 = (bf16[4,128,640]{2,1,0:T(8,128)(2,1)S(1)}, bf16[4,128,640]{2,1,0:T(8,128)(2,1)S(1)}, u32[]{:S(2)}, u32[]{:S(2)}) collective-permute-start(bf16[4,128,640]{2,1,0:T(8,128)(2,1)S(1)} %bitcast.49), channel_id=1, source_target_pairs={{0,1},{1,2},{2,3},{3,0},{4,5},{5,6},{6,7},{7,4},{8,9},{9,10},{10,1... | collective-permute-start | bytes 1966088 | tf_op jit(solution)/shard_map/ppermute | solution.py:221
  38.6 25.1 %collective-permute-start.11 = (bf16[4,128,256]{2,1,0:T(8,128)(2,1)S(1)}, bf16[4,128,256]{2,1,0:T(8,128)(2,1)S(1)}, u32[]{:S(2)}, u32[]{:S(2)}) collective-permute-start(bf16[4,128,256]{2,1,0:T(8,128)(2,1)S(1)} %bitcast.54), channel_id=1, source_target_pairs={{0,3},{1,0},{2,1},{3,2},{4,7},{5,4},{6,5},{7,6},{8,11},{9,8},{10,9... | collective-permute-start | bytes 786440 | tf_op jit(solution)/shard_map/ppermute | solution.py:221
  38.6 0.7 copy-start.21
  39.3 30.1 %collective-permute-start.9 = (bf16[4,128,256]{2,1,0:T(8,128)(2,1)S(1)}, bf16[4,128,256]{2,1,0:T(8,128)(2,1)S(1)}, u32[]{:S(2)}, u32[]{:S(2)}) collective-permute-start(bf16[4,128,256]{2,1,0:T(8,128)(2,1)S(1)} %bitcast.53), channel_id=1, source_target_pairs={{0,3},{1,0},{2,1},{3,2},{4,7},{5,4},{6,5},{7,6},{8,11},{9,8},{10,9... | collective-permute-start | bytes 786440 | tf_op jit(solution)/shard_map/ppermute | solution.py:221
  40.6 5.1 %copy-start.3 = (bf16[4,128,640]{2,1,0:T(8,128)(2,1)}, bf16[4,128,640]{2,1,0:T(8,128)(2,1)S(1)}, u32[]{:S(2)}) copy-start(bf16[4,128,640]{2,1,0:T(8,128)(2,1)S(1)} %collective-permute-done.refs_5_) | copy-start | bytes 1966084
  40.6 41.8 %collective-permute-start.3 = (bf16[4,128,640]{2,1,0:T(8,128)(2,1)}, bf16[4,128,640]{2,1,0:T(8,128)(2,1)}, u32[]{:S(2)}, u32[]{:S(2)}) collective-permute-start(bf16[4,128,640]{2,1,0:T(8,128)(2,1)} %bitcast.17), channel_id=1, source_target_pairs={{0,3},{1,0},{2,1},{3,2},{4,7},{5,4},{6,5},{7,6},{8,11},{9,8},{10,9... | collective-permute-start | bytes 1966088 | tf_op jit(solution)/shard_map/ppermute | solution.py:221
  43.9 33.5 %copy-start.29 = (bf16[2,640]{1,0:T(2,128)(2,1)S(1)}, bf16[2,640]{1,0:T(2,128)(2,1)}, u32[]{:S(2)}) copy-start(bf16[2,640]{1,0:T(2,128)(2,1)} %param.10) | copy-start | bytes 7684
  43.9 43.0 %copy-start.2 = (bf16[448,448]{1,0:T(8,128)(2,1)S(1)}, bf16[448,448]{1,0:T(8,128)(2,1)}, u32[]{:S(2)}) copy-start(bf16[448,448]{1,0:T(8,128)(2,1)} %constant.30.clone.refs_1_) | copy-start | bytes 1204228
  45.7 0.7 copy-start.15
  46.4 63.7 %collective-permute-start.6 = (bf16[2,192,640]{2,1,0:T(8,128)(2,1)}, bf16[2,192,640]{2,1,0:T(8,128)(2,1)}, u32[]{:S(2)}, u32[]{:S(2)}) collective-permute-start(bf16[2,192,640]{2,1,0:T(8,128)(2,1)} %get-tuple-element.45), channel_id=1, source_target_pairs={{4,0},{8,4},{12,8},{16,12},{20,16},{24,20},{28,24},{5,1},{9,5},{13... | collective-permute-start | bytes 1474568 | tf_op jit(solution)/shard_map/ppermute | solution.py:241
  63.8 0.7 copy-start.17
  64.5 45.7 %collective-permute-start.4 = (bf16[2,192,640]{2,1,0:T(8,128)(2,1)}, bf16[2,192,640]{2,1,0:T(8,128)(2,1)}, u32[]{:S(2)}, u32[]{:S(2)}) collective-permute-start(bf16[2,192,640]{2,1,0:T(8,128)(2,1)} %get-tuple-element.46), channel_id=1, source_target_pairs={{0,4},{4,8},{8,12},{12,16},{16,20},{20,24},{24,28},{1,5},{5,9},{9,... | collective-permute-start | bytes 1474568 | tf_op jit(solution)/shard_map/ppermute | solution.py:241
  69.4 0.7 copy-start.19
  70.1 40.1 %collective-permute-start.5 = (bf16[2,256,640]{2,1,0:T(8,128)(2,1)}, bf16[2,256,640]{2,1,0:T(8,128)(2,1)}, u32[]{:S(2)}, u32[]{:S(2)}) collective-permute-start(bf16[2,256,640]{2,1,0:T(8,128)(2,1)} %pad_maximum_fusion), channel_id=1, source_target_pairs={{0,4},{4,8},{8,12},{12,16},{16,20},{20,24},{24,28},{1,5},{5,9},{9,... | collective-permute-start | bytes 1966088 | tf_op jit(solution)/shard_map/ppermute | solution.py:241
  72.0 0.8 copy-start.9
  72.9 37.3 %collective-permute-start.7 = (bf16[2,256,640]{2,1,0:T(8,128)(2,1)}, bf16[2,256,640]{2,1,0:T(8,128)(2,1)}, u32[]{:S(2)}, u32[]{:S(2)}) collective-permute-start(bf16[2,256,640]{2,1,0:T(8,128)(2,1)} %pad_maximum_fusion.1), channel_id=1, source_target_pairs={{4,0},{8,4},{12,8},{16,12},{20,16},{24,20},{28,24},{5,1},{9,5},{13... | collective-permute-start | bytes 1966088 | tf_op jit(solution)/shard_map/ppermute | solution.py:241
  82.5 21.7 %collective-permute-start.8 = (bf16[4,128,256]{2,1,0:T(8,128)(2,1)}, bf16[4,128,256]{2,1,0:T(8,128)(2,1)S(1)}, u32[]{:S(2)}, u32[]{:S(2)}) collective-permute-start(bf16[4,128,256]{2,1,0:T(8,128)(2,1)} %bitcast.52), channel_id=1, source_target_pairs={{0,1},{1,2},{2,3},{3,0},{4,5},{5,6},{6,7},{7,4},{8,9},{9,10},{10,1... | collective-permute-start | bytes 786440 | tf_op jit(solution)/shard_map/ppermute | solution.py:221
  86.9 2.6 copy-start
  89.5 1.1 copy-start.4
  90.6 1.1 copy-start.6
  91.7 0.9 copy-start.7
  92.6 1.1 copy-start.10
  93.7 0.9 copy-start.22
  94.6 3.5 %copy-start.16 = (bf16[4,128,256]{2,1,0:T(8,128)(2,1)S(1)}, bf16[4,128,256]{2,1,0:T(8,128)(2,1)}, u32[]{:S(2)}) copy-start(bf16[4,128,256]{2,1,0:T(8,128)(2,1)} %copy-done.15) | copy-start | bytes 786436
  94.6 3.6 %copy-start.18 = (bf16[4,128,256]{2,1,0:T(8,128)(2,1)S(1)}, bf16[4,128,256]{2,1,0:T(8,128)(2,1)}, u32[]{:S(2)}) copy-start(bf16[4,128,256]{2,1,0:T(8,128)(2,1)} %copy-done.17) | copy-start | bytes 786436
  98.2 6.0 %copy-start.20 = (bf16[4,128,256]{2,1,0:T(8,128)(2,1)S(1)}, bf16[4,128,256]{2,1,0:T(8,128)(2,1)}, u32[]{:S(2)}) copy-start(bf16[4,128,256]{2,1,0:T(8,128)(2,1)} %copy-done.19) | copy-start | bytes 786436
  110.1 11.5 %copy-start.13 = (bf16[640,1280]{1,0:T(8,128)(2,1)S(1)}, bf16[640,1280]{1,0:T(8,128)(2,1)}, u32[]{:S(2)}) copy-start(bf16[640,1280]{1,0:T(8,128)(2,1)} %get-tuple-element.37.w_in) | copy-start | bytes 4915204
  110.2 11.5 %copy-start.14 = (bf16[1280,640]{1,0:T(8,128)(2,1)S(1)}, bf16[1280,640]{1,0:T(8,128)(2,1)}, u32[]{:S(2)}) copy-start(bf16[1280,640]{1,0:T(8,128)(2,1)} %get-tuple-element.35.w_out) | copy-start | bytes 4915204
  125.7 34.7 %collective-permute-start.14 = (bf16[4,128,640]{2,1,0:T(8,128)(2,1)S(1)}, bf16[4,128,640]{2,1,0:T(8,128)(2,1)S(1)}, u32[]{:S(2)}, u32[]{:S(2)}) collective-permute-start(bf16[4,128,640]{2,1,0:T(8,128)(2,1)S(1)} %get-tuple-element.25), channel_id=1, source_target_pairs={{0,1},{1,2},{2,3},{3,0},{4,5},{5,6},{6,7},{7,4},{8,9},{9,10},{10,1... | collective-permute-start | bytes 1966088 | tf_op jit(solution)/shard_map/ppermute | solution.py:221
  130.0 33.2 %collective-permute-start.22 = (bf16[4,128,128]{2,1,0:T(8,128)(2,1)S(1)}, bf16[4,128,128]{2,1,0:T(8,128)(2,1)S(1)}, u32[]{:S(2)}, u32[]{:S(2)}) collective-permute-start(bf16[4,128,128]{2,1,0:T(8,128)(2,1)S(1)} %get-tuple-element.33), channel_id=1, source_target_pairs={{0,1},{1,2},{2,3},{3,0},{4,5},{5,6},{6,7},{7,4},{8,9},{9,10},{10,1... | collective-permute-start | bytes 393224 | tf_op jit(solution)/shard_map/ppermute | solution.py:221
  130.1 33.1 %collective-permute-start.23 = (bf16[4,128,128]{2,1,0:T(8,128)(2,1)S(1)}, bf16[4,128,128]{2,1,0:T(8,128)(2,1)S(1)}, u32[]{:S(2)}, u32[]{:S(2)}) collective-permute-start(bf16[4,128,128]{2,1,0:T(8,128)(2,1)S(1)} %get-tuple-element.34), channel_id=1, source_target_pairs={{0,3},{1,0},{2,1},{3,2},{4,7},{5,4},{6,5},{7,6},{8,11},{9,8},{10,9... | collective-permute-start | bytes 393224 | tf_op jit(solution)/shard_map/ppermute | solution.py:221
  132.2 31.1 %collective-permute-start.17 = (bf16[4,128,640]{2,1,0:T(8,128)(2,1)S(1)}, bf16[4,128,640]{2,1,0:T(8,128)(2,1)S(1)}, u32[]{:S(2)}, u32[]{:S(2)}) collective-permute-start(bf16[4,128,640]{2,1,0:T(8,128)(2,1)S(1)} %get-tuple-element.28), channel_id=1, source_target_pairs={{0,3},{1,0},{2,1},{3,2},{4,7},{5,4},{6,5},{7,6},{8,11},{9,8},{10,9... | collective-permute-start | bytes 1966088 | tf_op jit(solution)/shard_map/ppermute | solution.py:221
  138.1 79.4 %collective-permute-start.15 = (bf16[4,128,640]{2,1,0:T(8,128)(2,1)S(1)}, bf16[4,128,640]{2,1,0:T(8,128)(2,1)S(1)}, u32[]{:S(2)}, u32[]{:S(2)}) collective-permute-start(bf16[4,128,640]{2,1,0:T(8,128)(2,1)S(1)} %get-tuple-element.26), channel_id=1, source_target_pairs={{0,1},{1,2},{2,3},{3,0},{4,5},{5,6},{6,7},{7,4},{8,9},{9,10},{10,1... | collective-permute-start | bytes 1966088 | tf_op jit(solution)/shard_map/ppermute | solution.py:221
  160.4 60.8 %collective-permute-start.18 = (bf16[4,128,640]{2,1,0:T(8,128)(2,1)S(1)}, bf16[4,128,640]{2,1,0:T(8,128)(2,1)S(1)}, u32[]{:S(2)}, u32[]{:S(2)}) collective-permute-start(bf16[4,128,640]{2,1,0:T(8,128)(2,1)S(1)} %get-tuple-element.29), channel_id=1, source_target_pairs={{0,3},{1,0},{2,1},{3,2},{4,7},{5,4},{6,5},{7,6},{8,11},{9,8},{10,9... | collective-permute-start | bytes 1966088 | tf_op jit(solution)/shard_map/ppermute | solution.py:221
  163.2 34.2 %collective-permute-start.16 = (bf16[4,128,256]{2,1,0:T(8,128)(2,1)S(1)}, bf16[4,128,256]{2,1,0:T(8,128)(2,1)S(1)}, u32[]{:S(2)}, u32[]{:S(2)}) collective-permute-start(bf16[4,128,256]{2,1,0:T(8,128)(2,1)S(1)} %get-tuple-element.27), channel_id=1, source_target_pairs={{0,1},{1,2},{2,3},{3,0},{4,5},{5,6},{6,7},{7,4},{8,9},{9,10},{10,1... | collective-permute-start | bytes 786440 | tf_op jit(solution)/shard_map/ppermute | solution.py:221
  163.3 49.8 %collective-permute-start.20 = (bf16[4,128,256]{2,1,0:T(8,128)(2,1)S(1)}, bf16[4,128,256]{2,1,0:T(8,128)(2,1)S(1)}, u32[]{:S(2)}, u32[]{:S(2)}) collective-permute-start(bf16[4,128,256]{2,1,0:T(8,128)(2,1)S(1)} %get-tuple-element.31), channel_id=1, source_target_pairs={{0,1},{1,2},{2,3},{3,0},{4,5},{5,6},{6,7},{7,4},{8,9},{9,10},{10,1... | collective-permute-start | bytes 786440 | tf_op jit(solution)/shard_map/ppermute | solution.py:221
  163.3 52.1 %collective-permute-start.21 = (bf16[4,128,256]{2,1,0:T(8,128)(2,1)S(1)}, bf16[4,128,256]{2,1,0:T(8,128)(2,1)S(1)}, u32[]{:S(2)}, u32[]{:S(2)}) collective-permute-start(bf16[4,128,256]{2,1,0:T(8,128)(2,1)S(1)} %get-tuple-element.32), channel_id=1, source_target_pairs={{0,3},{1,0},{2,1},{3,2},{4,7},{5,4},{6,5},{7,6},{8,11},{9,8},{10,9... | collective-permute-start | bytes 786440 | tf_op jit(solution)/shard_map/ppermute | solution.py:221
  165.3 58.7 %copy-start.26 = (bf16[2,5,256,640]{3,2,1,0:T(8,128)(2,1)S(1)}, bf16[2,5,256,640]{3,2,1,0:T(8,128)(2,1)}, u32[]{:S(2)}) copy-start(bf16[2,5,256,640]{3,2,1,0:T(8,128)(2,1)} %param.9) | copy-start | bytes 9830404
  165.4 58.7 %copy-start.28 = (bf16[448,256,1]{1,0,2:T(8,128)(2,1)S(1)}, bf16[448,256,1]{1,0,2:T(8,128)(2,1)}, u32[]{:S(2)}) copy-start(bf16[448,256,1]{1,0,2:T(8,128)(2,1)} %constant.34) | copy-start | bytes 688132
  197.4 35.9 %collective-permute-start.19 = (bf16[4,128,256]{2,1,0:T(8,128)(2,1)S(1)}, bf16[4,128,256]{2,1,0:T(8,128)(2,1)S(1)}, u32[]{:S(2)}, u32[]{:S(2)}) collective-permute-start(bf16[4,128,256]{2,1,0:T(8,128)(2,1)S(1)} %get-tuple-element.30), channel_id=1, source_target_pairs={{0,3},{1,0},{2,1},{3,2},{4,7},{5,4},{6,5},{7,6},{8,11},{9,8},{10,9... | collective-permute-start | bytes 786440 | tf_op jit(solution)/shard_map/ppermute | solution.py:221
  213.1 25.7 %collective-permute-start.26 = (bf16[2,192,640]{2,1,0:T(8,128)(2,1)S(1)}, bf16[2,192,640]{2,1,0:T(8,128)(2,1)S(1)}, u32[]{:S(2)}, u32[]{:S(2)}) collective-permute-start(bf16[2,192,640]{2,1,0:T(8,128)(2,1)S(1)} %get-tuple-element.49), channel_id=1, source_target_pairs={{4,0},{8,4},{12,8},{16,12},{20,16},{24,20},{28,24},{5,1},{9,5},{13... | collective-permute-start | bytes 1474568 | tf_op jit(solution)/shard_map/ppermute | solution.py:241
  215.4 9.6 %copy-start.8 = (bf16[192,448]{1,0:T(8,128)(2,1)S(1)}, bf16[192,448]{1,0:T(8,128)(2,1)}, u32[]{:S(2)}) copy-start(bf16[192,448]{1,0:T(8,128)(2,1)} %constant.31.clone.refs_2_) | copy-start | bytes 516100
  215.4 23.4 %collective-permute-start.24 = (bf16[2,192,640]{2,1,0:T(8,128)(2,1)S(1)}, bf16[2,192,640]{2,1,0:T(8,128)(2,1)S(1)}, u32[]{:S(2)}, u32[]{:S(2)}) collective-permute-start(bf16[2,192,640]{2,1,0:T(8,128)(2,1)S(1)} %get-tuple-element.50), channel_id=1, source_target_pairs={{0,4},{4,8},{8,12},{12,16},{16,20},{20,24},{24,28},{1,5},{5,9},{9,... | collective-permute-start | bytes 1474568 | tf_op jit(solution)/shard_map/ppermute | solution.py:241
  217.6 25.1 %collective-permute-start.25 = (bf16[2,256,640]{2,1,0:T(8,128)(2,1)S(1)}, bf16[2,256,640]{2,1,0:T(8,128)(2,1)S(1)}, u32[]{:S(2)}, u32[]{:S(2)}) collective-permute-start(bf16[2,256,640]{2,1,0:T(8,128)(2,1)S(1)} %pad_maximum_fusion.2), channel_id=1, source_target_pairs={{0,4},{4,8},{8,12},{12,16},{16,20},{20,24},{24,28},{1,5},{5,9},{9,... | collective-permute-start | bytes 1966088 | tf_op jit(solution)/shard_map/ppermute | solution.py:241
  221.2 21.4 %collective-permute-start.27 = (bf16[2,256,640]{2,1,0:T(8,128)(2,1)S(1)}, bf16[2,256,640]{2,1,0:T(8,128)(2,1)S(1)}, u32[]{:S(2)}, u32[]{:S(2)}) collective-permute-start(bf16[2,256,640]{2,1,0:T(8,128)(2,1)S(1)} %pad_maximum_fusion.3), channel_id=1, source_target_pairs={{4,0},{8,4},{12,8},{16,12},{20,16},{24,20},{28,24},{5,1},{9,5},{13... | collective-permute-start | bytes 1966088 | tf_op jit(solution)/shard_map/ppermute | solution.py:241
  238.7 13.9 %copy-start.11 = (bf16[640,1280]{1,0:T(8,128)(2,1)S(1)}, bf16[640,1280]{1,0:T(8,128)(2,1)}, u32[]{:S(2)}) copy-start(bf16[640,1280]{1,0:T(8,128)(2,1)} %get-tuple-element.38.w_in) | copy-start | bytes 4915204
  238.7 13.9 %copy-start.12 = (bf16[1280,640]{1,0:T(8,128)(2,1)S(1)}, bf16[1280,640]{1,0:T(8,128)(2,1)}, u32[]{:S(2)}) copy-start(bf16[1280,640]{1,0:T(8,128)(2,1)} %get-tuple-element.36.w_out) | copy-start | bytes 4915204

commit v2 on v1

--- a/solution.py
+++ b/solution.py
@@ -290,12 +290,12 @@
     lanes = [slice(0, channels)] * 2 + pieces
     groups_of = [groups[0], groups[1]] + [groups[2]] * len(parts)
     head, tail = slice(0, edge), slice(width - edge, width)
-    lasts = [pick(pairs, groups[0], tail, lanes[0])]
-    pairs, _ = lax.optimization_barrier((pairs, lasts[0]))
-    firsts = [pick(pairs, groups[0], head, lanes[0])]
-    pairs, _ = lax.optimization_barrier((pairs, firsts[0]))
-    firsts += [pick(pairs, members, head, cut) for members, cut in zip(groups_of[1:], lanes[1:])]
-    lasts += [pick(pairs, members, tail, cut) for members, cut in zip(groups_of[1:], lanes[1:])]
+    firsts, lasts = [None] * len(lanes), [None] * len(lanes)
+    for k in [len(lanes) - 1] + list(range(len(lanes) - 1)):
+        for edges, lon in ((lasts, tail), (firsts, head)):
+            edges[k] = pick(pairs, groups_of[k], lon, lanes[k])
+            if k in (0, len(lanes) - 1):
+                pairs, _ = lax.optimization_barrier((pairs, edges[k]))
     tables = (forward, inverse)
     out = None
     for layer in range(blocks):

time: 266 us -> 264 us (level)
  the two profiles are of different devices: /device:TPU:20 before, /device:TPU:28 now
where the time goes in v2:
time: 264 us; the launch traced here: 263 us
  waiting for transfers between devices  112 us (42%)
  Pallas kernels  75.7 us (29%)
  starting transfers between devices  43.9 us (17%)
  local copies, waits for them, and re-layouts  24.5 us (9%)
  matrix products  4.36 us (2%)
    ppermute x20, waiting for transfers between devices, rotate(): lax.ppermute(block, axis, [(i, (i + hops) % count) for i in range(count)])  108 us
    pallas_call x8, Pallas kernels, convolve(): pl.pallas_call(kernel, grid=(blocks,), out_shape=out, in_specs=[pl.BlockS...  50.5 us
    pallas_call x5, Pallas kernels, mlp(): pl.pallas_call(functools.partial(mlp_kernel, half=edge, kept=len(extra),...  25.2 us
    ppermute x20, starting transfers between devices, rotate(): lax.ppermute(block, axis, [(i, (i + hops) % count) for i in range(count)])  22.8 us
    ppermute x8, starting transfers between devices, step_rows(): return lax.ppermute(block, 'lat', pairs)  21.2 us
    unnamed x60, local copies, waits for them, and re-layouts  13 us
    slice x6, local copies, waits for them, and re-layouts, pick(): chosen = lax.slice(pairs, low, high, (stride, 1, 1, 1))  6.14 us
  transfers between devices with their start and end apart: 28, of which 9 were waited for; matrix products, arithmetic and copies ran while one was open for 6% of the time, Pallas kernels for 14%

profile of v2, /device:TPU:28, one launch (start us, length us, event | category | flops | bytes accessed | tf_op | source)
XLA Modules:
  0.0 262.7 jit_solution(17263526062524268877)
XLA Ops:
  0.0 1.1 slice.124
  1.4 0.9 slice.101
  2.3 1.9 collective-permute-start.13
  4.1 1.1 slice.102
  5.3 2.1 collective-permute-start
  7.4 1.1 slice.103
  8.6 0.8 fusion.4
  9.4 3.8 %collective-permute-start.10 = (bf16[4,128,256]{2,1,0:T(8,128)(2,1)S(1)}, bf16[4,128,256]{2,1,0:T(8,128)(2,1)S(1)}, u32[]{:S(2)}, u32[]{:S(2)}) collective-permute-start(bf16[4,128,256]{2,1,0:T(8,128)(2,1)S(1)} %bitcast.56), channel_id=1, source_target_pairs={{0,1},{1,2},{2,3},{3,0},{4,5},{5,6},{6,7},{7,4},{8,9},{9,10},{10,1... | collective-permute-start | bytes 786440 | tf_op jit(solution)/shard_map/ppermute | solution.py:221
  13.2 1.0 fusion.6
  14.2 1.9 slice_bitcast_fusion.1
  16.2 1.2 copy-done.24
  17.4 2.0 slice_bitcast_fusion
  19.4 1.1 fusion.5
  20.9 3.4 %convolution_bitcast_fusion.refs_3_ = f32[5,448,640]{2,1,0:T(8,128)} fusion(bf16[448,256,1]{1,0,2:T(8,128)(2,1)S(1)} %copy-done.27, bf16[2,5,256,640]{3,2,1,0:T(8,128)(2,1)S(1)} %copy-done.25), kind=kOutput, calls=%fused_computation | convolution fusion | flops 734003200 | bytes 7602176 | tf_op jit(solution)/shard_map/kt,rtc->rkc/dot_general | solution.py:265
  24.4 14.3 %collective-permute-done.2.refs_7_.refs_8_ = bf16[4,128,640]{2,1,0:T(8,128)(2,1)S(1)} collective-permute-done((bf16[4,128,640]{2,1,0:T(8,128)(2,1)S(1)}, bf16[4,128,640]{2,1,0:T(8,128)(2,1)S(1)}, u32[]{:S(2)}, u32[]{:S(2)}) %collective-permute-start.2) | collective-permute-done | bytes 655392 | tf_op jit(solution)/shard_map/ppermute | solution.py:221
  38.6 2.1 collective-permute-start.1
  41.8 1.4 collective-permute-start.3
  43.2 0.9 pad_maximum_fusion.1
  44.2 0.9 pad_maximum_fusion
  45.1 0.7 copy-done.15
  45.8 1.9 collective-permute-start.6
  47.7 16.2 %collective-permute-done.11.refs_10_ = bf16[4,128,256]{2,1,0:T(8,128)(2,1)S(1)} collective-permute-done((bf16[4,128,256]{2,1,0:T(8,128)(2,1)S(1)}, bf16[4,128,256]{2,1,0:T(8,128)(2,1)S(1)}, u32[]{:S(2)}, u32[]{:S(2)}) %collective-permute-start.11) | collective-permute-done | bytes 262176 | tf_op jit(solution)/shard_map/ppermute | solution.py:221
  64.6 1.9 collective-permute-start.4
  66.5 3.0 %collective-permute-done.9.refs_10_ = bf16[4,128,256]{2,1,0:T(8,128)(2,1)S(1)} collective-permute-done((bf16[4,128,256]{2,1,0:T(8,128)(2,1)S(1)}, bf16[4,128,256]{2,1,0:T(8,128)(2,1)S(1)}, u32[]{:S(2)}, u32[]{:S(2)}) %collective-permute-start.9) | collective-permute-done | bytes 262176 | tf_op jit(solution)/shard_map/ppermute | solution.py:221
  69.5 0.7 copy-done.19
  70.2 1.9 collective-permute-start.5
  72.2 0.8 copy-done.9
  73.0 4.5 %collective-permute-start.7 = (bf16[2,256,640]{2,1,0:T(8,128)(2,1)}, bf16[2,256,640]{2,1,0:T(8,128)(2,1)}, u32[]{:S(2)}, u32[]{:S(2)}) collective-permute-start(bf16[2,256,640]{2,1,0:T(8,128)(2,1)} %pad_maximum_fusion.1), channel_id=1, source_target_pairs={{4,0},{8,4},{12,8},{16,12},{20,16},{24,20},{28,24},{5,1},{9,5},{13... | collective-permute-start | bytes 1966088 | tf_op jit(solution)/shard_map/ppermute | solution.py:241
  77.6 4.8 %collective-permute-done.3.refs_8_.refs_9_ = bf16[4,128,640]{2,1,0:T(8,128)(2,1)} collective-permute-done((bf16[4,128,640]{2,1,0:T(8,128)(2,1)}, bf16[4,128,640]{2,1,0:T(8,128)(2,1)}, u32[]{:S(2)}, u32[]{:S(2)}) %collective-permute-start.3) | collective-permute-done | bytes 655392 | tf_op jit(solution)/shard_map/ppermute | solution.py:221
  82.3 2.1 collective-permute-start.8
  84.5 2.6 copy-done
  87.1 1.1 copy-done.4
  88.2 1.1 copy-done.6
  89.3 0.9 copy-done.7
  90.2 1.1 copy-done.10
  91.3 0.9 copy-done.22
  92.2 3.5 %zonal_conv.11.refs_2_ = bf16[8,192,128]{2,1,0:T(8,128)(2,1)S(1)} custom-call(f32[16]{0:T(128)S(1)} %and_select_fusion.refs_0_, bf16[448,448]{1,0:T(8,128)(2,1)S(1)} %copy-done.2, bf16[192,448]{1,0:T(8,128)(2,1)S(1)} %copy-done.7, f32[5,448,640]{2,1,0:T(8,128)S(1)} %copy-done, bf16[12,192,640]{2,1,0:T(8,128)(2,1)S(1)} %bitcast.46, ...), custom_call_target="tpu_custom_call" | custom-call | flops 792723456 | bytes 2523136 | tf_op jit(solution)/shard_map/zonal_conv/pallas_call | solution.py:113
  95.8 5.9 %zonal_conv.10.refs_1_ = bf16[8,192,256]{2,1,0:T(8,128)(2,1)S(1)} custom-call(f32[16]{0:T(128)S(1)} %and_select_fusion.refs_0_, bf16[448,448]{1,0:T(8,128)(2,1)S(1)} %copy-done.2, bf16[192,448]{1,0:T(8,128)(2,1)S(1)} %copy-done.7, f32[5,448,640]{2,1,0:T(8,128)S(1)} %copy-done, bf16[12,192,640]{2,1,0:T(8,128)(2,1)S(1)} %bitcast.47, ...), custom_call_target="tpu_custom_call" | custom-call | flops 1585446912 | bytes 5046272 | tf_op jit(solution)/shard_map/zonal_conv/pallas_call | solution.py:113
  101.8 5.9 %zonal_conv.9.refs_0_ = bf16[8,192,256]{2,1,0:T(8,128)(2,1)S(1)} custom-call(f32[16]{0:T(128)S(1)} %and_select_fusion.refs_0_, bf16[448,448]{1,0:T(8,128)(2,1)S(1)} %copy-done.2, bf16[192,448]{1,0:T(8,128)(2,1)S(1)} %copy-done.7, f32[5,448,640]{2,1,0:T(8,128)S(1)} %copy-done, bf16[12,192,640]{2,1,0:T(8,128)(2,1)S(1)} %bitcast.48, ...), custom_call_target="tpu_custom_call" | custom-call | flops 1585446912 | bytes 5046272 | tf_op jit(solution)/shard_map/zonal_conv/pallas_call | solution.py:113
  107.8 11.4 %zonal_conv.8.refs_0_ = bf16[4,192,640]{2,1,0:T(8,128)(2,1)S(1)} custom-call(f32[16]{0:T(128)S(1)} %and_select_fusion.refs_0_, bf16[448,448]{1,0:T(8,128)(2,1)S(1)} %copy-done.2, bf16[192,448]{1,0:T(8,128)(2,1)S(1)} %copy-done.7, f32[5,448,640]{2,1,0:T(8,128)S(1)} %copy-done, bf16[12,192,640]{2,1,0:T(8,128)(2,1)S(1)} %bitcast.49, ...), custom_call_target="tpu_custom_call" | custom-call | flops 3523215360 | bytes 12615680 | tf_op jit(solution)/shard_map/zonal_conv/pallas_call | solution.py:113
  119.3 4.1 %channel_mlp.5 = (bf16[4,192,640]{2,1,0:T(8,128)(2,1)S(1)}, bf16[4,128,640]{2,1,0:T(8,128)(2,1)S(1)}, bf16[4,128,640]{2,1,0:T(8,128)(2,1)S(1)}) custom-call(f32[1,640]{1,0:T(1,128)S(1)} %get-tuple-element.61.gain, bf16[640,1280]{1,0:T(8,128)(2,1)S(1)} %copy-done.13, bf16[1280,640]{1,0:T(8,128)(2,1)S(1)} %copy-done.14, bf16[4,192,640]{2,1,0:T(8,128)(2,1)S(1)} %zonal_conv.8.refs_0_), custom_call_target="tpu_custom_call" | custom-call | flops 2516582400 | bytes 5242880 | tf_op jit(solution)/shard_map/channel_mlp/pallas_call | solution.py:196
  123.3 0.8 collective-permute-start.14
  124.1 4.0 %channel_mlp.7 = (bf16[4,192,640]{2,1,0:T(8,128)(2,1)S(1)}, bf16[4,128,256]{2,1,0:T(8,128)(2,1)S(1)}, bf16[4,128,256]{2,1,0:T(8,128)(2,1)S(1)}, bf16[4,128,256]{...) custom-call(f32[1,640]{1,0:T(1,128)S(1)} %get-tuple-element.61.gain,, ...), custom_call_target="tpu_custom_call" | custom-call | flops 2516582400 | bytes 5242880 | tf_op jit(solution)/shard_map/channel_mlp/pallas_call | solution.py:196
  128.8 1.4 collective-permute-start.23
  130.2 1.5 collective-permute-start.17
  131.7 4.0 %channel_mlp.6 = (bf16[4,192,640]{2,1,0:T(8,128)(2,1)S(1)}, bf16[4,128,640]{2,1,0:T(8,128)(2,1)S(1)}, bf16[4,128,640]{2,1,0:T(8,128)(2,1)S(1)}) custom-call(f32[1,640]{1,0:T(1,128)S(1)} %get-tuple-element.61.gain, bf16[640,1280]{1,0:T(8,128)(2,1)S(1)} %copy-done.13, bf16[1280,640]{1,0:T(8,128)(2,1)S(1)} %copy-done.14, ...), custom_call_target="tpu_custom_call" | custom-call | flops 2516582400 | bytes 5242880 | tf_op jit(solution)/shard_map/channel_mlp/pallas_call | solution.py:196
  135.8 2.4 collective-permute-start.15
  138.2 4.1 %collective-permute-done.14.refs_7_.refs_6_ = bf16[4,128,640]{2,1,0:T(8,128)(2,1)S(1)} collective-permute-done((bf16[4,128,640]{2,1,0:T(8,128)(2,1)S(1)}, bf16[4,128,640]{2,1,0:T(8,128)(2,1)S(1)}, u32[]{:S(2)}, u32[]{:S(2)}) %collective-permute-start.14) | collective-permute-done | bytes 655392 | tf_op jit(solution)/shard_map/ppermute | solution.py:221
  142.4 18.4 %collective-permute-done.22.refs_9_ = bf16[4,128,128]{2,1,0:T(8,128)(2,1)S(1)} collective-permute-done((bf16[4,128,128]{2,1,0:T(8,128)(2,1)S(1)}, bf16[4,128,128]{2,1,0:T(8,128)(2,1)S(1)}, u32[]{:S(2)}, u32[]{:S(2)}) %collective-permute-start.22) | collective-permute-done | bytes 131104 | tf_op jit(solution)/shard_map/ppermute | solution.py:221
  160.9 2.1 collective-permute-start.21
  163.2 31.4 %collective-permute-done.16.refs_9_ = bf16[4,128,256]{2,1,0:T(8,128)(2,1)S(1)} collective-permute-done((bf16[4,128,256]{2,1,0:T(8,128)(2,1)S(1)}, bf16[4,128,256]{2,1,0:T(8,128)(2,1)S(1)}, u32[]{:S(2)}, u32[]{:S(2)}) %collective-permute-start.16) | collective-permute-done | bytes 262176 | tf_op jit(solution)/shard_map/ppermute | solution.py:221
  194.6 15.6 %collective-permute-done.20.refs_9_ = bf16[4,128,256]{2,1,0:T(8,128)(2,1)S(1)} collective-permute-done((bf16[4,128,256]{2,1,0:T(8,128)(2,1)S(1)}, bf16[4,128,256]{2,1,0:T(8,128)(2,1)S(1)}, u32[]{:S(2)}, u32[]{:S(2)}) %collective-permute-start.20) | collective-permute-done | bytes 262176 | tf_op jit(solution)/shard_map/ppermute | solution.py:221
  210.2 1.9 collective-permute-start.26
  212.1 2.5 collective-permute-start.24
  214.7 3.0 %collective-permute-start.25 = (bf16[2,256,640]{2,1,0:T(8,128)(2,1)S(1)}, bf16[2,256,640]{2,1,0:T(8,128)(2,1)S(1)}, u32[]{:S(2)}, u32[]{:S(2)}) collective-permute-start(bf16[2,256,640]{2,1,0:T(8,128)(2,1)S(1)} %pad_maximum_fusion.2), channel_id=1, source_target_pairs={{0,4},{4,8},{8,12},{12,16},{16,20},{20,24},{24,28},{1,5},{5,9},{9,... | collective-permute-start | bytes 1966088 | tf_op jit(solution)/shard_map/ppermute | solution.py:241
  217.7 3.4 %collective-permute-start.27 = (bf16[2,256,640]{2,1,0:T(8,128)(2,1)S(1)}, bf16[2,256,640]{2,1,0:T(8,128)(2,1)S(1)}, u32[]{:S(2)}, u32[]{:S(2)}) collective-permute-start(bf16[2,256,640]{2,1,0:T(8,128)(2,1)S(1)} %pad_maximum_fusion.3), channel_id=1, source_target_pairs={{4,0},{8,4},{12,8},{16,12},{20,16},{24,20},{28,24},{5,1},{9,5},{13... | collective-permute-start | bytes 1966088 | tf_op jit(solution)/shard_map/ppermute | solution.py:241
  221.2 0.9 convolution_bitcast_fusion.1.refs_3_
  222.1 2.9 %zonal_conv.14.refs_2_.refs_5_ = bf16[8,192,128]{2,1,0:T(8,128)(2,1)S(1)} custom-call(f32[16]{0:T(128)S(1)} %and_select_fusion.refs_0_, bf16[448,448]{1,0:T(8,128)(2,1)S(1)} %copy-done.2, bf16[192,448]{1,0:T(8,128)(2,1)S(1)} %copy-done.8, f32[5,448,640]{2,1,0:T(8,128)S(1)} %convolution_bitcast_fusion.1.refs_3_, ...), custom_call_target="tpu_custom_call" | custom-call | flops 792723456 | bytes 2523136 | tf_op jit(solution)/shard_map/zonal_conv/pallas_call | solution.py:113
  225.0 5.4 %zonal_conv.13.refs_1_.refs_4_ = bf16[8,192,256]{2,1,0:T(8,128)(2,1)S(1)} custom-call(f32[16]{0:T(128)S(1)} %and_select_fusion.refs_0_, bf16[448,448]{1,0:T(8,128)(2,1)S(1)} %copy-done.2, bf16[192,448]{1,0:T(8,128)(2,1)S(1)} %copy-done.8, f32[5,448,640]{2,1,0:T(8,128)S(1)} %convolution_bitcast_fusion.1.refs_3_, ...), custom_call_target="tpu_custom_call" | custom-call | flops 1585446912 | bytes 5046272 | tf_op jit(solution)/shard_map/zonal_conv/pallas_call | solution.py:113
  230.4 5.4 %zonal_conv.12.refs_0_.refs_3_ = bf16[8,192,256]{2,1,0:T(8,128)(2,1)S(1)} custom-call(f32[16]{0:T(128)S(1)} %and_select_fusion.refs_0_, bf16[448,448]{1,0:T(8,128)(2,1)S(1)} %copy-done.2, bf16[192,448]{1,0:T(8,128)(2,1)S(1)} %copy-done.8, f32[5,448,640]{2,1,0:T(8,128)S(1)} %convolution_bitcast_fusion.1.refs_3_, ...), custom_call_target="tpu_custom_call" | custom-call | flops 1585446912 | bytes 5046272 | tf_op jit(solution)/shard_map/zonal_conv/pallas_call | solution.py:113
  235.9 3.7 %collective-permute-done.25.refs_11_ = bf16[2,256,640]{2,1,0:T(8,128)(2,1)S(1)} collective-permute-done((bf16[2,256,640]{2,1,0:T(8,128)(2,1)S(1)}, bf16[2,256,640]{2,1,0:T(8,128)(2,1)S(1)}, u32[]{:S(2)}, u32[]{:S(2)}) %collective-permute-start.25) | collective-permute-done | bytes 655392 | tf_op jit(solution)/shard_map/ppermute | solution.py:241
  239.6 10.0 %zonal_conv.15.refs_0_ = bf16[4,192,640]{2,1,0:T(8,128)(2,1)S(1)} custom-call(f32[16]{0:T(128)S(1)} %and_select_fusion.refs_0_, bf16[448,448]{1,0:T(8,128)(2,1)S(1)} %copy-done.2, bf16[192,448]{1,0:T(8,128)(2,1)S(1)} %copy-done.8, f32[5,448,640]{2,1,0:T(8,128)S(1)} %convolution_bitcast_fusion.1.refs_3_, bf16[4,192,640]{2,1,0:T(8,128)(2,1)S(1)} %get-tuple-element.26.refs_4_, ...), custom_call_target="tpu_custom_call" | custom-call | flops 3523215360 | bytes 12615680 | tf_op jit(solution)/shard_map/zonal_conv/pallas_call | solution.py:113
  249.6 4.8 %channel_mlp.8.refs_6_ = bf16[12,192,640]{2,1,0:T(8,128)(2,1)} custom-call(f32[1,640]{1,0:T(1,128)S(1)} %get-tuple-element.62.gain, bf16[640,1280]{1,0:T(8,128)(2,1)S(1)} %copy-done.11, bf16[1280,640]{1,0:T(8,128)(2,1)S(1)} %copy-done.12, bf16[4,192,640]{2,1,0:T(8,128)(2,1)S(1)} %zonal_conv.15.refs_0_), custom_call_target="tpu_custom_call" | custom-call | flops 2516582400 | bytes 5242880 | tf_op jit(solution)/shard_map/channel_mlp/pallas_call | solution.py:196
  254.4 8.2 %channel_mlp.9 = bf16[12,192,640]{2,1,0:T(8,128)(2,1)} custom-call(f32[1,640]{1,0:T(1,128)S(1)} %get-tuple-element.62.gain, bf16[640,1280]{1,0:T(8,128)(2,1)S(1)} %copy-done.11, bf16[1280,640]{1,0:T(8,128)(2,1)S(1)} %copy-done.12, bf16[8,192,256]{2,1,0:T(8,128)(2,1)S(1)} %zonal_conv.12.refs_0_.refs_3_, ...), custom_call_target="tpu_custom_call", output_to_operand_aliasing={{}: (9, {})} | custom-call | flops 5033164800 | bytes 7208960 | tf_op jit(solution)/shard_map/channel_mlp/pallas_call | solution.py:196
  (87 shorter events, 3.8 us)
Async XLA Ops:
  0.0 8.6 %copy-start.1 = (bf16[1,12,640,192]{2,3,1,0:T(8,128)(2,1)S(1)}, bf16[1,12,640,192]{2,3,1,0:T(8,128)(2,1)}, u32[]{:S(2)}) copy-start(bf16[1,12,640,192]{2,3,1,0:T(8,128)(2,1)} %param.8) | copy-start | bytes 8847364
  1.1 40.4 %collective-permute-start.12 = (bf16[4,128,128]{2,1,0:T(8,128)(2,1)S(1)}, bf16[4,128,128]{2,1,0:T(8,128)(2,1)S(1)}, u32[]{:S(2)}, u32[]{:S(2)}) collective-permute-start(bf16[4,128,128]{2,1,0:T(8,128)(2,1)S(1)} %bitcast.57), channel_id=1, source_target_pairs={{0,1},{1,2},{2,3},{3,0},{4,5},{5,6},{6,7},{7,4},{8,9},{9,10},{10,1... | collective-permute-start | bytes 393224 | tf_op jit(solution)/shard_map/ppermute | solution.py:221
  2.3 38.5 %collective-permute-start.13 = (bf16[4,128,128]{2,1,0:T(8,128)(2,1)S(1)}, bf16[4,128,128]{2,1,0:T(8,128)(2,1)S(1)}, u32[]{:S(2)}, u32[]{:S(2)}) collective-permute-start(bf16[4,128,128]{2,1,0:T(8,128)(2,1)S(1)} %bitcast.58), channel_id=1, source_target_pairs={{0,3},{1,0},{2,1},{3,2},{4,7},{5,4},{6,5},{7,6},{8,11},{9,8},{10,9... | collective-permute-start | bytes 393224 | tf_op jit(solution)/shard_map/ppermute | solution.py:221
  5.3 36.5 %collective-permute-start = (bf16[4,128,640]{2,1,0:T(8,128)(2,1)S(1)}, bf16[4,128,640]{2,1,0:T(8,128)(2,1)S(1)}, u32[]{:S(2)}, u32[]{:S(2)}) collective-permute-start(bf16[4,128,640]{2,1,0:T(8,128)(2,1)S(1)} %bitcast.51), channel_id=1, source_target_pairs={{0,1},{1,2},{2,3},{3,0},{4,5},{5,6},{6,7},{7,4},{8,9},{9,10},{10,1... | collective-permute-start | bytes 1966088 | tf_op jit(solution)/shard_map/ppermute | solution.py:221
  8.5 30.1 %collective-permute-start.2 = (bf16[4,128,640]{2,1,0:T(8,128)(2,1)S(1)}, bf16[4,128,640]{2,1,0:T(8,128)(2,1)S(1)}, u32[]{:S(2)}, u32[]{:S(2)}) collective-permute-start(bf16[4,128,640]{2,1,0:T(8,128)(2,1)S(1)} %bitcast.52), channel_id=1, source_target_pairs={{0,3},{1,0},{2,1},{3,2},{4,7},{5,4},{6,5},{7,6},{8,11},{9,8},{10,9... | collective-permute-start | bytes 1966088 | tf_op jit(solution)/shard_map/ppermute | solution.py:221
  8.6 5.7 %copy-start.23 = (bf16[2,640,1280]{2,1,0:T(8,128)(2,1)S(1)}, bf16[2,640,1280]{2,1,0:T(8,128)(2,1)}, u32[]{:S(2)}) copy-start(bf16[2,640,1280]{2,1,0:T(8,128)(2,1)} %param.11) | copy-start | bytes 9830404
  9.4 35.6 %collective-permute-start.10 = (bf16[4,128,256]{2,1,0:T(8,128)(2,1)S(1)}, bf16[4,128,256]{2,1,0:T(8,128)(2,1)S(1)}, u32[]{:S(2)}, u32[]{:S(2)}) collective-permute-start(bf16[4,128,256]{2,1,0:T(8,128)(2,1)S(1)} %bitcast.56), channel_id=1, source_target_pairs={{0,1},{1,2},{2,3},{3,0},{4,5},{5,6},{6,7},{7,4},{8,9},{9,10},{10,1... | collective-permute-start | bytes 786440 | tf_op jit(solution)/shard_map/ppermute | solution.py:221
  14.2 3.1 %copy-start.24 = (bf16[2,1280,640]{2,1,0:T(8,128)(2,1)S(1)}, bf16[2,1280,640]{2,1,0:T(8,128)(2,1)}, u32[]{:S(2)}) copy-start(bf16[2,1280,640]{2,1,0:T(8,128)(2,1)} %param.12) | copy-start | bytes 9830404
  17.4 3.2 %copy-start.25 = (bf16[2,5,256,640]{3,2,1,0:T(8,128)(2,1)S(1)}, bf16[2,5,256,640]{3,2,1,0:T(8,128)(2,1)}, u32[]{:S(2)}) copy-start(bf16[2,5,256,640]{3,2,1,0:T(8,128)(2,1)} %param.9) | copy-start | bytes 9830404
  19.4 1.6 copy-start.27
  38.6 5.5 %copy-start.5 = (bf16[4,128,640]{2,1,0:T(8,128)(2,1)}, bf16[4,128,640]{2,1,0:T(8,128)(2,1)S(1)}, u32[]{:S(2)}) copy-start(bf16[4,128,640]{2,1,0:T(8,128)(2,1)S(1)} %collective-permute-done.2.refs_7_.refs_8_) | copy-start | bytes 1966084
  38.6 33.5 %collective-permute-start.1 = (bf16[4,128,640]{2,1,0:T(8,128)(2,1)S(1)}, bf16[4,128,640]{2,1,0:T(8,128)(2,1)S(1)}, u32[]{:S(2)}, u32[]{:S(2)}) collective-permute-start(bf16[4,128,640]{2,1,0:T(8,128)(2,1)S(1)} %bitcast.50), channel_id=1, source_target_pairs={{0,1},{1,2},{2,3},{3,0},{4,5},{5,6},{6,7},{7,4},{8,9},{9,10},{10,1... | collective-permute-start | bytes 1966088 | tf_op jit(solution)/shard_map/ppermute | solution.py:221
  40.8 0.6 copy-start.21
  41.4 22.5 %collective-permute-start.11 = (bf16[4,128,256]{2,1,0:T(8,128)(2,1)S(1)}, bf16[4,128,256]{2,1,0:T(8,128)(2,1)S(1)}, u32[]{:S(2)}, u32[]{:S(2)}) collective-permute-start(bf16[4,128,256]{2,1,0:T(8,128)(2,1)S(1)} %bitcast.55), channel_id=1, source_target_pairs={{0,3},{1,0},{2,1},{3,2},{4,7},{5,4},{6,5},{7,6},{8,11},{9,8},{10,9... | collective-permute-start | bytes 786440 | tf_op jit(solution)/shard_map/ppermute | solution.py:221
  41.4 28.1 %collective-permute-start.9 = (bf16[4,128,256]{2,1,0:T(8,128)(2,1)S(1)}, bf16[4,128,256]{2,1,0:T(8,128)(2,1)S(1)}, u32[]{:S(2)}, u32[]{:S(2)}) collective-permute-start(bf16[4,128,256]{2,1,0:T(8,128)(2,1)S(1)} %bitcast.54), channel_id=1, source_target_pairs={{0,3},{1,0},{2,1},{3,2},{4,7},{5,4},{6,5},{7,6},{8,11},{9,8},{10,9... | collective-permute-start | bytes 786440 | tf_op jit(solution)/shard_map/ppermute | solution.py:221
  41.8 3.3 %copy-start.3 = (bf16[4,128,640]{2,1,0:T(8,128)(2,1)}, bf16[4,128,640]{2,1,0:T(8,128)(2,1)S(1)}, u32[]{:S(2)}) copy-start(bf16[4,128,640]{2,1,0:T(8,128)(2,1)S(1)} %collective-permute-done.refs_5_) | copy-start | bytes 1966084
  41.8 40.6 %collective-permute-start.3 = (bf16[4,128,640]{2,1,0:T(8,128)(2,1)}, bf16[4,128,640]{2,1,0:T(8,128)(2,1)}, u32[]{:S(2)}, u32[]{:S(2)}) collective-permute-start(bf16[4,128,640]{2,1,0:T(8,128)(2,1)} %bitcast.19), channel_id=1, source_target_pairs={{0,3},{1,0},{2,1},{3,2},{4,7},{5,4},{6,5},{7,6},{8,11},{9,8},{10,9... | collective-permute-start | bytes 1966088 | tf_op jit(solution)/shard_map/ppermute | solution.py:221
  43.2 34.3 %copy-start.29 = (bf16[2,640]{1,0:T(2,128)(2,1)S(1)}, bf16[2,640]{1,0:T(2,128)(2,1)}, u32[]{:S(2)}) copy-start(bf16[2,640]{1,0:T(2,128)(2,1)} %param.10) | copy-start | bytes 7684
  43.2 41.3 %copy-start.2 = (bf16[448,448]{1,0:T(8,128)(2,1)S(1)}, bf16[448,448]{1,0:T(8,128)(2,1)}, u32[]{:S(2)}) copy-start(bf16[448,448]{1,0:T(8,128)(2,1)} %constant.30.clone.refs_1_) | copy-start | bytes 1204228
  45.1 0.7 copy-start.15
  45.8 62.0 %collective-permute-start.6 = (bf16[2,192,640]{2,1,0:T(8,128)(2,1)}, bf16[2,192,640]{2,1,0:T(8,128)(2,1)}, u32[]{:S(2)}, u32[]{:S(2)}) collective-permute-start(bf16[2,192,640]{2,1,0:T(8,128)(2,1)} %get-tuple-element.47), channel_id=1, source_target_pairs={{4,0},{8,4},{12,8},{16,12},{20,16},{24,20},{28,24},{5,1},{9,5},{13... | collective-permute-start | bytes 1474568 | tf_op jit(solution)/shard_map/ppermute | solution.py:241
  63.9 0.7 copy-start.17
  64.6 43.2 %collective-permute-start.4 = (bf16[2,192,640]{2,1,0:T(8,128)(2,1)}, bf16[2,192,640]{2,1,0:T(8,128)(2,1)}, u32[]{:S(2)}, u32[]{:S(2)}) collective-permute-start(bf16[2,192,640]{2,1,0:T(8,128)(2,1)} %get-tuple-element.48), channel_id=1, source_target_pairs={{0,4},{4,8},{8,12},{12,16},{16,20},{20,24},{24,28},{1,5},{5,9},{9,... | collective-permute-start | bytes 1474568 | tf_op jit(solution)/shard_map/ppermute | solution.py:241
  69.5 0.7 copy-start.19
  70.2 37.6 %collective-permute-start.5 = (bf16[2,256,640]{2,1,0:T(8,128)(2,1)}, bf16[2,256,640]{2,1,0:T(8,128)(2,1)}, u32[]{:S(2)}, u32[]{:S(2)}) collective-permute-start(bf16[2,256,640]{2,1,0:T(8,128)(2,1)} %pad_maximum_fusion), channel_id=1, source_target_pairs={{0,4},{4,8},{8,12},{12,16},{16,20},{20,24},{24,28},{1,5},{5,9},{9,... | collective-permute-start | bytes 1966088 | tf_op jit(solution)/shard_map/ppermute | solution.py:241
  72.2 0.8 copy-start.9
  73.0 34.8 %collective-permute-start.7 = (bf16[2,256,640]{2,1,0:T(8,128)(2,1)}, bf16[2,256,640]{2,1,0:T(8,128)(2,1)}, u32[]{:S(2)}, u32[]{:S(2)}) collective-permute-start(bf16[2,256,640]{2,1,0:T(8,128)(2,1)} %pad_maximum_fusion.1), channel_id=1, source_target_pairs={{4,0},{8,4},{12,8},{16,12},{20,16},{24,20},{28,24},{5,1},{9,5},{13... | collective-permute-start | bytes 1966088 | tf_op jit(solution)/shard_map/ppermute | solution.py:241
  82.3 19.4 %collective-permute-start.8 = (bf16[4,128,256]{2,1,0:T(8,128)(2,1)}, bf16[4,128,256]{2,1,0:T(8,128)(2,1)S(1)}, u32[]{:S(2)}, u32[]{:S(2)}) collective-permute-start(bf16[4,128,256]{2,1,0:T(8,128)(2,1)} %bitcast.53), channel_id=1, source_target_pairs={{0,1},{1,2},{2,3},{3,0},{4,5},{5,6},{6,7},{7,4},{8,9},{9,10},{10,1... | collective-permute-start | bytes 786440 | tf_op jit(solution)/shard_map/ppermute | solution.py:221
  84.5 2.6 %copy-start = (f32[5,448,640]{2,1,0:T(8,128)S(1)}, f32[5,448,640]{2,1,0:T(8,128)}, u32[]{:S(2)}) copy-start(f32[5,448,640]{2,1,0:T(8,128)} %convolution_bitcast_fusion.refs_3_) | copy-start | bytes 17203204
  87.1 1.1 copy-start.4
  88.2 1.1 copy-start.6
  89.3 0.9 copy-start.7
  90.2 1.1 copy-start.10
  91.3 0.9 copy-start.22
  92.2 3.5 %copy-start.16 = (bf16[4,128,256]{2,1,0:T(8,128)(2,1)S(1)}, bf16[4,128,256]{2,1,0:T(8,128)(2,1)}, u32[]{:S(2)}) copy-start(bf16[4,128,256]{2,1,0:T(8,128)(2,1)} %copy-done.15) | copy-start | bytes 786436
  92.2 3.6 %copy-start.18 = (bf16[4,128,256]{2,1,0:T(8,128)(2,1)S(1)}, bf16[4,128,256]{2,1,0:T(8,128)(2,1)}, u32[]{:S(2)}) copy-start(bf16[4,128,256]{2,1,0:T(8,128)(2,1)} %copy-done.17) | copy-start | bytes 786436
  95.8 6.0 %copy-start.20 = (bf16[4,128,256]{2,1,0:T(8,128)(2,1)S(1)}, bf16[4,128,256]{2,1,0:T(8,128)(2,1)}, u32[]{:S(2)}) copy-start(bf16[4,128,256]{2,1,0:T(8,128)(2,1)} %copy-done.19) | copy-start | bytes 786436
  107.7 11.5 %copy-start.13 = (bf16[640,1280]{1,0:T(8,128)(2,1)S(1)}, bf16[640,1280]{1,0:T(8,128)(2,1)}, u32[]{:S(2)}) copy-start(bf16[640,1280]{1,0:T(8,128)(2,1)} %get-tuple-element.41.w_in) | copy-start | bytes 4915204
  107.8 11.5 %copy-start.14 = (bf16[1280,640]{1,0:T(8,128)(2,1)S(1)}, bf16[1280,640]{1,0:T(8,128)(2,1)}, u32[]{:S(2)}) copy-start(bf16[1280,640]{1,0:T(8,128)(2,1)} %get-tuple-element.39.w_out) | copy-start | bytes 4915204
  123.3 19.0 %collective-permute-start.14 = (bf16[4,128,640]{2,1,0:T(8,128)(2,1)S(1)}, bf16[4,128,640]{2,1,0:T(8,128)(2,1)S(1)}, u32[]{:S(2)}, u32[]{:S(2)}) collective-permute-start(bf16[4,128,640]{2,1,0:T(8,128)(2,1)S(1)} %get-tuple-element.29), channel_id=1, source_target_pairs={{0,1},{1,2},{2,3},{3,0},{4,5},{5,6},{6,7},{7,4},{8,9},{9,10},{10,1... | collective-permute-start | bytes 1966088 | tf_op jit(solution)/shard_map/ppermute | solution.py:221
  128.2 32.7 %collective-permute-start.22 = (bf16[4,128,128]{2,1,0:T(8,128)(2,1)S(1)}, bf16[4,128,128]{2,1,0:T(8,128)(2,1)S(1)}, u32[]{:S(2)}, u32[]{:S(2)}) collective-permute-start(bf16[4,128,128]{2,1,0:T(8,128)(2,1)S(1)} %get-tuple-element.37), channel_id=1, source_target_pairs={{0,1},{1,2},{2,3},{3,0},{4,5},{5,6},{6,7},{7,4},{8,9},{9,10},{10,1... | collective-permute-start | bytes 393224 | tf_op jit(solution)/shard_map/ppermute | solution.py:221
  128.8 32.0 %collective-permute-start.23 = (bf16[4,128,128]{2,1,0:T(8,128)(2,1)S(1)}, bf16[4,128,128]{2,1,0:T(8,128)(2,1)S(1)}, u32[]{:S(2)}, u32[]{:S(2)}) collective-permute-start(bf16[4,128,128]{2,1,0:T(8,128)(2,1)S(1)} %get-tuple-element.38), channel_id=1, source_target_pairs={{0,3},{1,0},{2,1},{3,2},{4,7},{5,4},{6,5},{7,6},{8,11},{9,8},{10,9... | collective-permute-start | bytes 393224 | tf_op jit(solution)/shard_map/ppermute | solution.py:221
  130.2 30.6 %collective-permute-start.17 = (bf16[4,128,640]{2,1,0:T(8,128)(2,1)S(1)}, bf16[4,128,640]{2,1,0:T(8,128)(2,1)S(1)}, u32[]{:S(2)}, u32[]{:S(2)}) collective-permute-start(bf16[4,128,640]{2,1,0:T(8,128)(2,1)S(1)} %get-tuple-element.32), channel_id=1, source_target_pairs={{0,3},{1,0},{2,1},{3,2},{4,7},{5,4},{6,5},{7,6},{8,11},{9,8},{10,9... | collective-permute-start | bytes 1966088 | tf_op jit(solution)/shard_map/ppermute | solution.py:221
  135.8 78.9 %collective-permute-start.15 = (bf16[4,128,640]{2,1,0:T(8,128)(2,1)S(1)}, bf16[4,128,640]{2,1,0:T(8,128)(2,1)S(1)}, u32[]{:S(2)}, u32[]{:S(2)}) collective-permute-start(bf16[4,128,640]{2,1,0:T(8,128)(2,1)S(1)} %get-tuple-element.30), channel_id=1, source_target_pairs={{0,1},{1,2},{2,3},{3,0},{4,5},{5,6},{6,7},{7,4},{8,9},{9,10},{10,1... | collective-permute-start | bytes 1966088 | tf_op jit(solution)/shard_map/ppermute | solution.py:221
  142.4 75.3 %collective-permute-start.18 = (bf16[4,128,640]{2,1,0:T(8,128)(2,1)S(1)}, bf16[4,128,640]{2,1,0:T(8,128)(2,1)S(1)}, u32[]{:S(2)}, u32[]{:S(2)}) collective-permute-start(bf16[4,128,640]{2,1,0:T(8,128)(2,1)S(1)} %get-tuple-element.33), channel_id=1, source_target_pairs={{0,3},{1,0},{2,1},{3,2},{4,7},{5,4},{6,5},{7,6},{8,11},{9,8},{10,9... | collective-permute-start | bytes 1966088 | tf_op jit(solution)/shard_map/ppermute | solution.py:221
  160.9 33.7 %collective-permute-start.16 = (bf16[4,128,256]{2,1,0:T(8,128)(2,1)S(1)}, bf16[4,128,256]{2,1,0:T(8,128)(2,1)S(1)}, u32[]{:S(2)}, u32[]{:S(2)}) collective-permute-start(bf16[4,128,256]{2,1,0:T(8,128)(2,1)S(1)} %get-tuple-element.31), channel_id=1, source_target_pairs={{0,1},{1,2},{2,3},{3,0},{4,5},{5,6},{6,7},{7,4},{8,9},{9,10},{10,1... | collective-permute-start | bytes 786440 | tf_op jit(solution)/shard_map/ppermute | solution.py:221
  160.9 49.3 %collective-permute-start.20 = (bf16[4,128,256]{2,1,0:T(8,128)(2,1)S(1)}, bf16[4,128,256]{2,1,0:T(8,128)(2,1)S(1)}, u32[]{:S(2)}, u32[]{:S(2)}) collective-permute-start(bf16[4,128,256]{2,1,0:T(8,128)(2,1)S(1)} %get-tuple-element.35), channel_id=1, source_target_pairs={{0,1},{1,2},{2,3},{3,0},{4,5},{5,6},{6,7},{7,4},{8,9},{9,10},{10,1... | collective-permute-start | bytes 786440 | tf_op jit(solution)/shard_map/ppermute | solution.py:221
  160.9 51.2 %collective-permute-start.21 = (bf16[4,128,256]{2,1,0:T(8,128)(2,1)S(1)}, bf16[4,128,256]{2,1,0:T(8,128)(2,1)S(1)}, u32[]{:S(2)}, u32[]{:S(2)}) collective-permute-start(bf16[4,128,256]{2,1,0:T(8,128)(2,1)S(1)} %get-tuple-element.36), channel_id=1, source_target_pairs={{0,3},{1,0},{2,1},{3,2},{4,7},{5,4},{6,5},{7,6},{8,11},{9,8},{10,9... | collective-permute-start | bytes 786440 | tf_op jit(solution)/shard_map/ppermute | solution.py:221
  162.9 58.2 %copy-start.26 = (bf16[2,5,256,640]{3,2,1,0:T(8,128)(2,1)S(1)}, bf16[2,5,256,640]{3,2,1,0:T(8,128)(2,1)}, u32[]{:S(2)}) copy-start(bf16[2,5,256,640]{3,2,1,0:T(8,128)(2,1)} %param.9) | copy-start | bytes 9830404
  163.0 58.2 %copy-start.28 = (bf16[448,256,1]{1,0,2:T(8,128)(2,1)S(1)}, bf16[448,256,1]{1,0,2:T(8,128)(2,1)}, u32[]{:S(2)}) copy-start(bf16[448,256,1]{1,0,2:T(8,128)(2,1)} %constant.34) | copy-start | bytes 688132
  194.6 35.9 %collective-permute-start.19 = (bf16[4,128,256]{2,1,0:T(8,128)(2,1)S(1)}, bf16[4,128,256]{2,1,0:T(8,128)(2,1)S(1)}, u32[]{:S(2)}, u32[]{:S(2)}) collective-permute-start(bf16[4,128,256]{2,1,0:T(8,128)(2,1)S(1)} %get-tuple-element.34), channel_id=1, source_target_pairs={{0,3},{1,0},{2,1},{3,2},{4,7},{5,4},{6,5},{7,6},{8,11},{9,8},{10,9... | collective-permute-start | bytes 786440 | tf_op jit(solution)/shard_map/ppermute | solution.py:221
  210.2 25.7 %collective-permute-start.26 = (bf16[2,192,640]{2,1,0:T(8,128)(2,1)S(1)}, bf16[2,192,640]{2,1,0:T(8,128)(2,1)S(1)}, u32[]{:S(2)}, u32[]{:S(2)}) collective-permute-start(bf16[2,192,640]{2,1,0:T(8,128)(2,1)S(1)} %get-tuple-element.51), channel_id=1, source_target_pairs={{4,0},{8,4},{12,8},{16,12},{20,16},{24,20},{28,24},{5,1},{9,5},{13... | collective-permute-start | bytes 1474568 | tf_op jit(solution)/shard_map/ppermute | solution.py:241
  212.1 10.0 %copy-start.8 = (bf16[192,448]{1,0:T(8,128)(2,1)S(1)}, bf16[192,448]{1,0:T(8,128)(2,1)}, u32[]{:S(2)}) copy-start(bf16[192,448]{1,0:T(8,128)(2,1)} %constant.31.clone.refs_2_) | copy-start | bytes 516100
  212.1 23.8 %collective-permute-start.24 = (bf16[2,192,640]{2,1,0:T(8,128)(2,1)S(1)}, bf16[2,192,640]{2,1,0:T(8,128)(2,1)S(1)}, u32[]{:S(2)}, u32[]{:S(2)}) collective-permute-start(bf16[2,192,640]{2,1,0:T(8,128)(2,1)S(1)} %get-tuple-element.52), channel_id=1, source_target_pairs={{0,4},{4,8},{8,12},{12,16},{16,20},{20,24},{24,28},{1,5},{5,9},{9,... | collective-permute-start | bytes 1474568 | tf_op jit(solution)/shard_map/ppermute | solution.py:241
  214.7 24.9 %collective-permute-start.25 = (bf16[2,256,640]{2,1,0:T(8,128)(2,1)S(1)}, bf16[2,256,640]{2,1,0:T(8,128)(2,1)S(1)}, u32[]{:S(2)}, u32[]{:S(2)}) collective-permute-start(bf16[2,256,640]{2,1,0:T(8,128)(2,1)S(1)} %pad_maximum_fusion.2), channel_id=1, source_target_pairs={{0,4},{4,8},{8,12},{12,16},{16,20},{20,24},{24,28},{1,5},{5,9},{9,... | collective-permute-start | bytes 1966088 | tf_op jit(solution)/shard_map/ppermute | solution.py:241
  217.7 21.9 %collective-permute-start.27 = (bf16[2,256,640]{2,1,0:T(8,128)(2,1)S(1)}, bf16[2,256,640]{2,1,0:T(8,128)(2,1)S(1)}, u32[]{:S(2)}, u32[]{:S(2)}) collective-permute-start(bf16[2,256,640]{2,1,0:T(8,128)(2,1)S(1)} %pad_maximum_fusion.3), channel_id=1, source_target_pairs={{4,0},{8,4},{12,8},{16,12},{20,16},{24,20},{28,24},{5,1},{9,5},{13... | collective-permute-start | bytes 1966088 | tf_op jit(solution)/shard_map/ppermute | solution.py:241
  235.8 13.7 %copy-start.11 = (bf16[640,1280]{1,0:T(8,128)(2,1)S(1)}, bf16[640,1280]{1,0:T(8,128)(2,1)}, u32[]{:S(2)}) copy-start(bf16[640,1280]{1,0:T(8,128)(2,1)} %get-tuple-element.42.w_in) | copy-start | bytes 4915204
  235.9 13.7 %copy-start.12 = (bf16[1280,640]{1,0:T(8,128)(2,1)S(1)}, bf16[1280,640]{1,0:T(8,128)(2,1)}, u32[]{:S(2)}) copy-start(bf16[1280,640]{1,0:T(8,128)(2,1)} %get-tuple-element.40.w_out) | copy-start | bytes 4915204

commit v3 on v1

--- a/solution.py
+++ b/solution.py
@@ -42,9 +42,12 @@
 
     def block_of(ref):
         offset = 0 if ref.shape[2] == part else begin
+        if part == lanes:
+            return slice(offset * lanes, (offset + 1) * lanes)
         return pl.ds(pl.multiple_of((step + offset) * lanes, lanes), lanes)
 
     ours = [block_of(ref) for ref in sources]
+    its = block_of(factors) if part == lanes else slice(None)
     freqs = forward.shape[0] // 2
     every = len(row_refs)
     taps_r = factors.shape[0]
@@ -62,8 +65,8 @@
         start = pl.multiple_of(f * SUBLANES, SUBLANES)
         re = pl.ds(start, SUBLANES)
         im = pl.ds(pl.multiple_of(freqs + start, SUBLANES), SUBLANES)
-        fr = [factors[r, re] for r in range(taps_r)]
-        fi = [factors[r, im] for r in range(taps_r)]
+        fr = [factors[r, re, its] for r in range(taps_r)]
+        fi = [factors[r, im, its] for r in range(taps_r)]
         fd = [b - a for a, b in zip(fr, fi)]
         fs = [b + a for a, b in zip(fr, fi)]
         h = 0
@@ -118,7 +121,7 @@
             pl.BlockSpec(memory_space=pltpu.SMEM),
             held,
             held,
-            pl.BlockSpec((taps_r, length, LANES), lambda i: (0, 0, i + start)),
+            held if blocks == 1 else pl.BlockSpec((taps_r, length, LANES), lambda i: (0, 0, i + start)),
         ]
         + [held] * len(sources),
         out_specs=held,

time: 266 us -> 266 us (level)
  no operation moved by 1% of the time
where the time goes in v3:
time: 266 us
  waiting for transfers between devices  115 us (43%)
  Pallas kernels  75.9 us (29%)
  starting transfers between devices  43.9 us (17%)
  local copies, waits for them, and re-layouts  23.7 us (9%)
  matrix products  4.35 us (2%)
    ppermute x20, waiting for transfers between devices, rotate(): lax.ppermute(block, axis, [(i, (i + hops) % count) for i in range(count)])  112 us
    pallas_call x8, Pallas kernels, convolve(): pl.pallas_call(kernel, grid=(blocks,), out_shape=out, in_specs=[pl.BlockS...  50.7 us
    pallas_call x5, Pallas kernels, mlp(): pl.pallas_call(functools.partial(mlp_kernel, half=edge, kept=len(extra),...  25.2 us
    ppermute x20, starting transfers between devices, rotate(): lax.ppermute(block, axis, [(i, (i + hops) % count) for i in range(count)])  22.8 us
    ppermute x8, starting transfers between devices, step_rows(): return lax.ppermute(block, 'lat', pairs)  21.2 us
    unnamed x60, local copies, waits for them, and re-layouts  13 us
  transfers between devices with their start and end apart: 28, of which 10 were waited for; matrix products, arithmetic and copies ran while one was open for 6% of the time, Pallas kernels for 14%

profile of v3, /device:TPU:20, one launch (start us, length us, event | category | flops | bytes accessed | tf_op | source)
XLA Modules:
  0.0 265.7 jit_solution(5415471118960899530)
XLA Ops:
  0.0 1.3 slice.100
  1.3 1.6 collective-permute-start
  2.9 1.1 slice.101
  4.6 1.0 fusion.4
  5.6 1.6 collective-permute-start.12
  7.7 0.8 fusion.5
  8.5 1.6 collective-permute-start.10
  10.1 1.0 fusion.7
  11.1 1.9 slice_bitcast_fusion.1
  13.1 1.2 copy-done.24
  14.2 2.0 slice_bitcast_fusion
  16.2 1.1 fusion.6
  17.8 3.4 %convolution_bitcast_fusion.refs_3_ = f32[5,448,640]{2,1,0:T(8,128)} fusion(bf16[448,256,1]{1,0,2:T(8,128)(2,1)S(1)} %copy-done.27, bf16[2,5,256,640]{3,2,1,0:T(8,128)(2,1)S(1)} %copy-done.25), kind=kOutput, calls=%fused_computation | convolution fusion | flops 734003200 | bytes 7602176 | tf_op jit(solution)/shard_map/kt,rtc->rkc/dot_general | solution.py:268
  21.2 11.6 %collective-permute-done.2.refs_7_.refs_8_ = bf16[4,128,640]{2,1,0:T(8,128)(2,1)S(1)} collective-permute-done((bf16[4,128,640]{2,1,0:T(8,128)(2,1)S(1)}, bf16[4,128,640]{2,1,0:T(8,128)(2,1)S(1)}, u32[]{:S(2)}, u32[]{:S(2)}) %collective-permute-start.2) | collective-permute-done | bytes 655392 | tf_op jit(solution)/shard_map/ppermute | solution.py:224
  32.8 1.6 collective-permute-start.1
  34.5 4.2 %collective-permute-done.12.refs_7_ = bf16[4,128,128]{2,1,0:T(8,128)(2,1)S(1)} collective-permute-done((bf16[4,128,128]{2,1,0:T(8,128)(2,1)S(1)}, bf16[4,128,128]{2,1,0:T(8,128)(2,1)S(1)}, u32[]{:S(2)}, u32[]{:S(2)}) %collective-permute-start.12) | collective-permute-done | bytes 131104 | tf_op jit(solution)/shard_map/ppermute | solution.py:224
  39.3 1.3 collective-permute-start.9
  40.6 3.2 %collective-permute-start.3 = (bf16[4,128,640]{2,1,0:T(8,128)(2,1)}, bf16[4,128,640]{2,1,0:T(8,128)(2,1)}, u32[]{:S(2)}, u32[]{:S(2)}) collective-permute-start(bf16[4,128,640]{2,1,0:T(8,128)(2,1)} %bitcast.17), channel_id=1, source_target_pairs={{0,3},{1,0},{2,1},{3,2},{4,7},{5,4},{6,5},{7,6},{8,11},{9,8},{10,9... | collective-permute-start | bytes 1966088 | tf_op jit(solution)/shard_map/ppermute | solution.py:224
  43.9 0.9 pad_maximum_fusion.1
  44.8 0.9 pad_maximum_fusion
  45.7 0.7 copy-done.15
  46.4 1.9 collective-permute-start.6
  48.4 15.4 %collective-permute-done.11.refs_10_ = bf16[4,128,256]{2,1,0:T(8,128)(2,1)S(1)} collective-permute-done((bf16[4,128,256]{2,1,0:T(8,128)(2,1)S(1)}, bf16[4,128,256]{2,1,0:T(8,128)(2,1)S(1)}, u32[]{:S(2)}, u32[]{:S(2)}) %collective-permute-start.11) | collective-permute-done | bytes 262176 | tf_op jit(solution)/shard_map/ppermute | solution.py:224
  63.8 0.7 copy-done.17
  64.5 1.9 collective-permute-start.4
  66.4 3.0 %collective-permute-done.9.refs_10_ = bf16[4,128,256]{2,1,0:T(8,128)(2,1)S(1)} collective-permute-done((bf16[4,128,256]{2,1,0:T(8,128)(2,1)S(1)}, bf16[4,128,256]{2,1,0:T(8,128)(2,1)S(1)}, u32[]{:S(2)}, u32[]{:S(2)}) %collective-permute-start.9) | collective-permute-done | bytes 262176 | tf_op jit(solution)/shard_map/ppermute | solution.py:224
  69.4 0.7 copy-done.19
  70.1 1.9 collective-permute-start.5
  72.0 0.8 copy-done.9
  72.9 4.5 %collective-permute-start.7 = (bf16[2,256,640]{2,1,0:T(8,128)(2,1)}, bf16[2,256,640]{2,1,0:T(8,128)(2,1)}, u32[]{:S(2)}, u32[]{:S(2)}) collective-permute-start(bf16[2,256,640]{2,1,0:T(8,128)(2,1)} %pad_maximum_fusion.1), channel_id=1, source_target_pairs={{4,0},{8,4},{12,8},{16,12},{20,16},{24,20},{28,24},{5,1},{9,5},{13... | collective-permute-start | bytes 1966088 | tf_op jit(solution)/shard_map/ppermute | solution.py:244
  77.4 5.0 %collective-permute-done.3.refs_8_.refs_9_ = bf16[4,128,640]{2,1,0:T(8,128)(2,1)} collective-permute-done((bf16[4,128,640]{2,1,0:T(8,128)(2,1)}, bf16[4,128,640]{2,1,0:T(8,128)(2,1)}, u32[]{:S(2)}, u32[]{:S(2)}) %collective-permute-start.3) | collective-permute-done | bytes 655392 | tf_op jit(solution)/shard_map/ppermute | solution.py:224
  82.5 4.4 %collective-permute-start.8 = (bf16[4,128,256]{2,1,0:T(8,128)(2,1)}, bf16[4,128,256]{2,1,0:T(8,128)(2,1)S(1)}, u32[]{:S(2)}, u32[]{:S(2)}) collective-permute-start(bf16[4,128,256]{2,1,0:T(8,128)(2,1)} %bitcast.52), channel_id=1, source_target_pairs={{0,1},{1,2},{2,3},{3,0},{4,5},{5,6},{6,7},{7,4},{8,9},{9,10},{10,1... | collective-permute-start | bytes 786440 | tf_op jit(solution)/shard_map/ppermute | solution.py:224
  86.9 2.6 copy-done
  89.5 1.1 copy-done.4
  90.6 1.1 copy-done.6
  91.7 0.9 copy-done.7
  92.6 1.1 copy-done.10
  93.7 0.9 copy-done.22
  94.6 3.6 %zonal_conv.11.refs_2_ = bf16[8,192,128]{2,1,0:T(8,128)(2,1)S(1)} custom-call(f32[16]{0:T(128)S(1)} %and_select_fusion.refs_0_, bf16[448,448]{1,0:T(8,128)(2,1)S(1)} %copy-done.2, bf16[192,448]{1,0:T(8,128)(2,1)S(1)} %copy-done.7, f32[5,448,640]{2,1,0:T(8,128)S(1)} %copy-done, bf16[12,192,640]{2,1,0:T(8,128)(2,1)S(1)} %bitcast.45, ...), custom_call_target="tpu_custom_call" | custom-call | flops 792723456 | bytes 2523136 | tf_op jit(solution)/shard_map/zonal_conv/pallas_call | solution.py:116
  98.3 5.9 %zonal_conv.10.refs_1_ = bf16[8,192,256]{2,1,0:T(8,128)(2,1)S(1)} custom-call(f32[16]{0:T(128)S(1)} %and_select_fusion.refs_0_, bf16[448,448]{1,0:T(8,128)(2,1)S(1)} %copy-done.2, bf16[192,448]{1,0:T(8,128)(2,1)S(1)} %copy-done.7, f32[5,448,640]{2,1,0:T(8,128)S(1)} %copy-done, bf16[12,192,640]{2,1,0:T(8,128)(2,1)S(1)} %bitcast.46, ...), custom_call_target="tpu_custom_call" | custom-call | flops 1585446912 | bytes 5046272 | tf_op jit(solution)/shard_map/zonal_conv/pallas_call | solution.py:116
  104.2 5.9 %zonal_conv.9.refs_0_ = bf16[8,192,256]{2,1,0:T(8,128)(2,1)S(1)} custom-call(f32[16]{0:T(128)S(1)} %and_select_fusion.refs_0_, bf16[448,448]{1,0:T(8,128)(2,1)S(1)} %copy-done.2, bf16[192,448]{1,0:T(8,128)(2,1)S(1)} %copy-done.7, f32[5,448,640]{2,1,0:T(8,128)S(1)} %copy-done, bf16[12,192,640]{2,1,0:T(8,128)(2,1)S(1)} %bitcast.47, ...), custom_call_target="tpu_custom_call" | custom-call | flops 1585446912 | bytes 5046272 | tf_op jit(solution)/shard_map/zonal_conv/pallas_call | solution.py:116
  110.3 11.4 %zonal_conv.8.refs_0_ = bf16[4,192,640]{2,1,0:T(8,128)(2,1)S(1)} custom-call(f32[16]{0:T(128)S(1)} %and_select_fusion.refs_0_, bf16[448,448]{1,0:T(8,128)(2,1)S(1)} %copy-done.2, bf16[192,448]{1,0:T(8,128)(2,1)S(1)} %copy-done.7, f32[5,448,640]{2,1,0:T(8,128)S(1)} %copy-done, bf16[12,192,640]{2,1,0:T(8,128)(2,1)S(1)} %bitcast.48, ...), custom_call_target="tpu_custom_call" | custom-call | flops 3523215360 | bytes 12615680 | tf_op jit(solution)/shard_map/zonal_conv/pallas_call | solution.py:116
  121.7 4.1 %channel_mlp.5 = (bf16[4,192,640]{2,1,0:T(8,128)(2,1)S(1)}, bf16[4,128,640]{2,1,0:T(8,128)(2,1)S(1)}, bf16[4,128,640]{2,1,0:T(8,128)(2,1)S(1)}) custom-call(f32[1,640]{1,0:T(1,128)S(1)} %get-tuple-element.59.gain, bf16[640,1280]{1,0:T(8,128)(2,1)S(1)} %copy-done.13, bf16[1280,640]{1,0:T(8,128)(2,1)S(1)} %copy-done.14, bf16[4,192,640]{2,1,0:T(8,128)(2,1)S(1)} %zonal_conv.8.refs_0_), custom_call_target="tpu_custom_call" | custom-call | flops 2516582400 | bytes 5242880 | tf_op jit(solution)/shard_map/channel_mlp/pallas_call | solution.py:199
  126.0 4.1 %channel_mlp.7 = (bf16[4,192,640]{2,1,0:T(8,128)(2,1)S(1)}, bf16[4,128,256]{2,1,0:T(8,128)(2,1)S(1)}, bf16[4,128,256]{2,1,0:T(8,128)(2,1)S(1)}, bf16[4,128,256]{...) custom-call(f32[1,640]{1,0:T(1,128)S(1)} %get-tuple-element.59.gain,, ...), custom_call_target="tpu_custom_call" | custom-call | flops 2516582400 | bytes 5242880 | tf_op jit(solution)/shard_map/channel_mlp/pallas_call | solution.py:199
  130.2 2.0 collective-permute-start.23
  132.2 2.0 collective-permute-start.17
  134.2 4.0 %channel_mlp.6 = (bf16[4,192,640]{2,1,0:T(8,128)(2,1)S(1)}, bf16[4,128,640]{2,1,0:T(8,128)(2,1)S(1)}, bf16[4,128,640]{2,1,0:T(8,128)(2,1)S(1)}) custom-call(f32[1,640]{1,0:T(1,128)S(1)} %get-tuple-element.59.gain, bf16[640,1280]{1,0:T(8,128)(2,1)S(1)} %copy-done.13, bf16[1280,640]{1,0:T(8,128)(2,1)S(1)} %copy-done.14, ...), custom_call_target="tpu_custom_call" | custom-call | flops 2516582400 | bytes 5242880 | tf_op jit(solution)/shard_map/channel_mlp/pallas_call | solution.py:199
  138.4 22.1 %collective-permute-done.14.refs_7_.refs_6_ = bf16[4,128,640]{2,1,0:T(8,128)(2,1)S(1)} collective-permute-done((bf16[4,128,640]{2,1,0:T(8,128)(2,1)S(1)}, bf16[4,128,640]{2,1,0:T(8,128)(2,1)S(1)}, u32[]{:S(2)}, u32[]{:S(2)}) %collective-permute-start.14) | collective-permute-done | bytes 655392 | tf_op jit(solution)/shard_map/ppermute | solution.py:224
  160.5 2.7 %collective-permute-done.22.refs_9_ = bf16[4,128,128]{2,1,0:T(8,128)(2,1)S(1)} collective-permute-done((bf16[4,128,128]{2,1,0:T(8,128)(2,1)S(1)}, bf16[4,128,128]{2,1,0:T(8,128)(2,1)S(1)}, u32[]{:S(2)}, u32[]{:S(2)}) %collective-permute-start.22) | collective-permute-done | bytes 131104 | tf_op jit(solution)/shard_map/ppermute | solution.py:224
  163.3 2.0 collective-permute-start.21
  165.6 31.9 %collective-permute-done.16.refs_9_ = bf16[4,128,256]{2,1,0:T(8,128)(2,1)S(1)} collective-permute-done((bf16[4,128,256]{2,1,0:T(8,128)(2,1)S(1)}, bf16[4,128,256]{2,1,0:T(8,128)(2,1)S(1)}, u32[]{:S(2)}, u32[]{:S(2)}) %collective-permute-start.16) | collective-permute-done | bytes 262176 | tf_op jit(solution)/shard_map/ppermute | solution.py:224
  197.5 15.6 %collective-permute-done.20.refs_9_ = bf16[4,128,256]{2,1,0:T(8,128)(2,1)S(1)} collective-permute-done((bf16[4,128,256]{2,1,0:T(8,128)(2,1)S(1)}, bf16[4,128,256]{2,1,0:T(8,128)(2,1)S(1)}, u32[]{:S(2)}, u32[]{:S(2)}) %collective-permute-start.20) | collective-permute-done | bytes 262176 | tf_op jit(solution)/shard_map/ppermute | solution.py:224
  213.1 2.3 collective-permute-start.26
  215.4 2.1 collective-permute-start.24
  217.6 3.7 %collective-permute-start.25 = (bf16[2,256,640]{2,1,0:T(8,128)(2,1)S(1)}, bf16[2,256,640]{2,1,0:T(8,128)(2,1)S(1)}, u32[]{:S(2)}, u32[]{:S(2)}) collective-permute-start(bf16[2,256,640]{2,1,0:T(8,128)(2,1)S(1)} %pad_maximum_fusion.2), channel_id=1, source_target_pairs={{0,4},{4,8},{8,12},{12,16},{16,20},{20,24},{24,28},{1,5},{5,9},{9,... | collective-permute-start | bytes 1966088 | tf_op jit(solution)/shard_map/ppermute | solution.py:244
  221.3 2.8 %collective-permute-start.27 = (bf16[2,256,640]{2,1,0:T(8,128)(2,1)S(1)}, bf16[2,256,640]{2,1,0:T(8,128)(2,1)S(1)}, u32[]{:S(2)}, u32[]{:S(2)}) collective-permute-start(bf16[2,256,640]{2,1,0:T(8,128)(2,1)S(1)} %pad_maximum_fusion.3), channel_id=1, source_target_pairs={{4,0},{8,4},{12,8},{16,12},{20,16},{24,20},{28,24},{5,1},{9,5},{13... | collective-permute-start | bytes 1966088 | tf_op jit(solution)/shard_map/ppermute | solution.py:244
  224.1 0.9 convolution_bitcast_fusion.1.refs_3_
  225.1 3.0 %zonal_conv.14.refs_2_.refs_5_ = bf16[8,192,128]{2,1,0:T(8,128)(2,1)S(1)} custom-call(f32[16]{0:T(128)S(1)} %and_select_fusion.refs_0_, bf16[448,448]{1,0:T(8,128)(2,1)S(1)} %copy-done.2, bf16[192,448]{1,0:T(8,128)(2,1)S(1)} %copy-done.8, f32[5,448,640]{2,1,0:T(8,128)S(1)} %convolution_bitcast_fusion.1.refs_3_, ...), custom_call_target="tpu_custom_call" | custom-call | flops 792723456 | bytes 2523136 | tf_op jit(solution)/shard_map/zonal_conv/pallas_call | solution.py:116
  228.0 5.4 %zonal_conv.13.refs_1_.refs_4_ = bf16[8,192,256]{2,1,0:T(8,128)(2,1)S(1)} custom-call(f32[16]{0:T(128)S(1)} %and_select_fusion.refs_0_, bf16[448,448]{1,0:T(8,128)(2,1)S(1)} %copy-done.2, bf16[192,448]{1,0:T(8,128)(2,1)S(1)} %copy-done.8, f32[5,448,640]{2,1,0:T(8,128)S(1)} %convolution_bitcast_fusion.1.refs_3_, ...), custom_call_target="tpu_custom_call" | custom-call | flops 1585446912 | bytes 5046272 | tf_op jit(solution)/shard_map/zonal_conv/pallas_call | solution.py:116
  233.5 5.4 %zonal_conv.12.refs_0_.refs_3_ = bf16[8,192,256]{2,1,0:T(8,128)(2,1)S(1)} custom-call(f32[16]{0:T(128)S(1)} %and_select_fusion.refs_0_, bf16[448,448]{1,0:T(8,128)(2,1)S(1)} %copy-done.2, bf16[192,448]{1,0:T(8,128)(2,1)S(1)} %copy-done.8, f32[5,448,640]{2,1,0:T(8,128)S(1)} %convolution_bitcast_fusion.1.refs_3_, ...), custom_call_target="tpu_custom_call" | custom-call | flops 1585446912 | bytes 5046272 | tf_op jit(solution)/shard_map/zonal_conv/pallas_call | solution.py:116
  238.9 3.7 %collective-permute-done.25.refs_11_ = bf16[2,256,640]{2,1,0:T(8,128)(2,1)S(1)} collective-permute-done((bf16[2,256,640]{2,1,0:T(8,128)(2,1)S(1)}, bf16[2,256,640]{2,1,0:T(8,128)(2,1)S(1)}, u32[]{:S(2)}, u32[]{:S(2)}) %collective-permute-start.25) | collective-permute-done | bytes 655392 | tf_op jit(solution)/shard_map/ppermute | solution.py:244
  242.7 10.0 %zonal_conv.15.refs_0_ = bf16[4,192,640]{2,1,0:T(8,128)(2,1)S(1)} custom-call(f32[16]{0:T(128)S(1)} %and_select_fusion.refs_0_, bf16[448,448]{1,0:T(8,128)(2,1)S(1)} %copy-done.2, bf16[192,448]{1,0:T(8,128)(2,1)S(1)} %copy-done.8, f32[5,448,640]{2,1,0:T(8,128)S(1)} %convolution_bitcast_fusion.1.refs_3_, bf16[4,192,640]{2,1,0:T(8,128)(2,1)S(1)} %get-tuple-element.22.refs_4_, ...), custom_call_target="tpu_custom_call" | custom-call | flops 3523215360 | bytes 12615680 | tf_op jit(solution)/shard_map/zonal_conv/pallas_call | solution.py:116
  252.6 4.8 %channel_mlp.8.refs_6_ = bf16[12,192,640]{2,1,0:T(8,128)(2,1)} custom-call(f32[1,640]{1,0:T(1,128)S(1)} %get-tuple-element.60.gain, bf16[640,1280]{1,0:T(8,128)(2,1)S(1)} %copy-done.11, bf16[1280,640]{1,0:T(8,128)(2,1)S(1)} %copy-done.12, bf16[4,192,640]{2,1,0:T(8,128)(2,1)S(1)} %zonal_conv.15.refs_0_), custom_call_target="tpu_custom_call" | custom-call | flops 2516582400 | bytes 5242880 | tf_op jit(solution)/shard_map/channel_mlp/pallas_call | solution.py:199
  257.5 8.2 %channel_mlp.9 = bf16[12,192,640]{2,1,0:T(8,128)(2,1)} custom-call(f32[1,640]{1,0:T(1,128)S(1)} %get-tuple-element.60.gain, bf16[640,1280]{1,0:T(8,128)(2,1)S(1)} %copy-done.11, bf16[1280,640]{1,0:T(8,128)(2,1)S(1)} %copy-done.12, bf16[8,192,256]{2,1,0:T(8,128)(2,1)S(1)} %zonal_conv.12.refs_0_.refs_3_, ...), custom_call_target="tpu_custom_call", output_to_operand_aliasing={{}: (9, {})} | custom-call | flops 5033164800 | bytes 7208960 | tf_op jit(solution)/shard_map/channel_mlp/pallas_call | solution.py:199
  (86 shorter events, 3.2 us)
Async XLA Ops:
  0.0 7.7 %copy-start.1 = (bf16[1,12,640,192]{2,3,1,0:T(8,128)(2,1)S(1)}, bf16[1,12,640,192]{2,3,1,0:T(8,128)(2,1)}, u32[]{:S(2)}) copy-start(bf16[1,12,640,192]{2,3,1,0:T(8,128)(2,1)} %param.8) | copy-start | bytes 8847364
  1.3 39.3 %collective-permute-start = (bf16[4,128,640]{2,1,0:T(8,128)(2,1)S(1)}, bf16[4,128,640]{2,1,0:T(8,128)(2,1)S(1)}, u32[]{:S(2)}, u32[]{:S(2)}) collective-permute-start(bf16[4,128,640]{2,1,0:T(8,128)(2,1)S(1)} %bitcast.50), channel_id=1, source_target_pairs={{0,1},{1,2},{2,3},{3,0},{4,5},{5,6},{6,7},{7,4},{8,9},{9,10},{10,1... | collective-permute-start | bytes 1966088 | tf_op jit(solution)/shard_map/ppermute | solution.py:224
  4.1 28.7 %collective-permute-start.2 = (bf16[4,128,640]{2,1,0:T(8,128)(2,1)S(1)}, bf16[4,128,640]{2,1,0:T(8,128)(2,1)S(1)}, u32[]{:S(2)}, u32[]{:S(2)}) collective-permute-start(bf16[4,128,640]{2,1,0:T(8,128)(2,1)S(1)} %bitcast.51), channel_id=1, source_target_pairs={{0,3},{1,0},{2,1},{3,2},{4,7},{5,4},{6,5},{7,6},{8,11},{9,8},{10,9... | collective-permute-start | bytes 1966088 | tf_op jit(solution)/shard_map/ppermute | solution.py:224
  5.6 33.0 %collective-permute-start.12 = (bf16[4,128,128]{2,1,0:T(8,128)(2,1)S(1)}, bf16[4,128,128]{2,1,0:T(8,128)(2,1)S(1)}, u32[]{:S(2)}, u32[]{:S(2)}) collective-permute-start(bf16[4,128,128]{2,1,0:T(8,128)(2,1)S(1)} %bitcast.57), channel_id=1, source_target_pairs={{0,1},{1,2},{2,3},{3,0},{4,5},{5,6},{6,7},{7,4},{8,9},{9,10},{10,1... | collective-permute-start | bytes 393224 | tf_op jit(solution)/shard_map/ppermute | solution.py:224
  7.2 31.4 %collective-permute-start.13 = (bf16[4,128,128]{2,1,0:T(8,128)(2,1)S(1)}, bf16[4,128,128]{2,1,0:T(8,128)(2,1)S(1)}, u32[]{:S(2)}, u32[]{:S(2)}) collective-permute-start(bf16[4,128,128]{2,1,0:T(8,128)(2,1)S(1)} %bitcast.56), channel_id=1, source_target_pairs={{0,3},{1,0},{2,1},{3,2},{4,7},{5,4},{6,5},{7,6},{8,11},{9,8},{10,9... | collective-permute-start | bytes 393224 | tf_op jit(solution)/shard_map/ppermute | solution.py:224
  7.7 3.4 %copy-start.23 = (bf16[2,640,1280]{2,1,0:T(8,128)(2,1)S(1)}, bf16[2,640,1280]{2,1,0:T(8,128)(2,1)}, u32[]{:S(2)}) copy-start(bf16[2,640,1280]{2,1,0:T(8,128)(2,1)} %param.11) | copy-start | bytes 9830404
  8.5 37.2 %collective-permute-start.10 = (bf16[4,128,256]{2,1,0:T(8,128)(2,1)S(1)}, bf16[4,128,256]{2,1,0:T(8,128)(2,1)S(1)}, u32[]{:S(2)}, u32[]{:S(2)}) collective-permute-start(bf16[4,128,256]{2,1,0:T(8,128)(2,1)S(1)} %bitcast.55), channel_id=1, source_target_pairs={{0,1},{1,2},{2,3},{3,0},{4,5},{5,6},{6,7},{7,4},{8,9},{9,10},{10,1... | collective-permute-start | bytes 786440 | tf_op jit(solution)/shard_map/ppermute | solution.py:224
  11.1 3.1 %copy-start.24 = (bf16[2,1280,640]{2,1,0:T(8,128)(2,1)S(1)}, bf16[2,1280,640]{2,1,0:T(8,128)(2,1)}, u32[]{:S(2)}) copy-start(bf16[2,1280,640]{2,1,0:T(8,128)(2,1)} %param.12) | copy-start | bytes 9830404
  14.2 3.2 %copy-start.25 = (bf16[2,5,256,640]{3,2,1,0:T(8,128)(2,1)S(1)}, bf16[2,5,256,640]{3,2,1,0:T(8,128)(2,1)}, u32[]{:S(2)}) copy-start(bf16[2,5,256,640]{3,2,1,0:T(8,128)(2,1)} %param.9) | copy-start | bytes 9830404
  16.2 1.6 copy-start.27
  32.8 12.0 %copy-start.5 = (bf16[4,128,640]{2,1,0:T(8,128)(2,1)}, bf16[4,128,640]{2,1,0:T(8,128)(2,1)S(1)}, u32[]{:S(2)}) copy-start(bf16[4,128,640]{2,1,0:T(8,128)(2,1)S(1)} %collective-permute-done.2.refs_7_.refs_8_) | copy-start | bytes 1966084
  32.8 39.2 %collective-permute-start.1 = (bf16[4,128,640]{2,1,0:T(8,128)(2,1)S(1)}, bf16[4,128,640]{2,1,0:T(8,128)(2,1)S(1)}, u32[]{:S(2)}, u32[]{:S(2)}) collective-permute-start(bf16[4,128,640]{2,1,0:T(8,128)(2,1)S(1)} %bitcast.49), channel_id=1, source_target_pairs={{0,1},{1,2},{2,3},{3,0},{4,5},{5,6},{6,7},{7,4},{8,9},{9,10},{10,1... | collective-permute-start | bytes 1966088 | tf_op jit(solution)/shard_map/ppermute | solution.py:224
  38.6 25.1 %collective-permute-start.11 = (bf16[4,128,256]{2,1,0:T(8,128)(2,1)S(1)}, bf16[4,128,256]{2,1,0:T(8,128)(2,1)S(1)}, u32[]{:S(2)}, u32[]{:S(2)}) collective-permute-start(bf16[4,128,256]{2,1,0:T(8,128)(2,1)S(1)} %bitcast.54), channel_id=1, source_target_pairs={{0,3},{1,0},{2,1},{3,2},{4,7},{5,4},{6,5},{7,6},{8,11},{9,8},{10,9... | collective-permute-start | bytes 786440 | tf_op jit(solution)/shard_map/ppermute | solution.py:224
  38.6 0.7 copy-start.21
  39.3 30.1 %collective-permute-start.9 = (bf16[4,128,256]{2,1,0:T(8,128)(2,1)S(1)}, bf16[4,128,256]{2,1,0:T(8,128)(2,1)S(1)}, u32[]{:S(2)}, u32[]{:S(2)}) collective-permute-start(bf16[4,128,256]{2,1,0:T(8,128)(2,1)S(1)} %bitcast.53), channel_id=1, source_target_pairs={{0,3},{1,0},{2,1},{3,2},{4,7},{5,4},{6,5},{7,6},{8,11},{9,8},{10,9... | collective-permute-start | bytes 786440 | tf_op jit(solution)/shard_map/ppermute | solution.py:224
  40.6 5.1 %copy-start.3 = (bf16[4,128,640]{2,1,0:T(8,128)(2,1)}, bf16[4,128,640]{2,1,0:T(8,128)(2,1)S(1)}, u32[]{:S(2)}) copy-start(bf16[4,128,640]{2,1,0:T(8,128)(2,1)S(1)} %collective-permute-done.refs_5_) | copy-start | bytes 1966084
  40.6 41.8 %collective-permute-start.3 = (bf16[4,128,640]{2,1,0:T(8,128)(2,1)}, bf16[4,128,640]{2,1,0:T(8,128)(2,1)}, u32[]{:S(2)}, u32[]{:S(2)}) collective-permute-start(bf16[4,128,640]{2,1,0:T(8,128)(2,1)} %bitcast.17), channel_id=1, source_target_pairs={{0,3},{1,0},{2,1},{3,2},{4,7},{5,4},{6,5},{7,6},{8,11},{9,8},{10,9... | collective-permute-start | bytes 1966088 | tf_op jit(solution)/shard_map/ppermute | solution.py:224
  43.9 33.5 %copy-start.29 = (bf16[2,640]{1,0:T(2,128)(2,1)S(1)}, bf16[2,640]{1,0:T(2,128)(2,1)}, u32[]{:S(2)}) copy-start(bf16[2,640]{1,0:T(2,128)(2,1)} %param.10) | copy-start | bytes 7684
  43.9 43.0 %copy-start.2 = (bf16[448,448]{1,0:T(8,128)(2,1)S(1)}, bf16[448,448]{1,0:T(8,128)(2,1)}, u32[]{:S(2)}) copy-start(bf16[448,448]{1,0:T(8,128)(2,1)} %constant.30.clone.refs_1_) | copy-start | bytes 1204228
  45.7 0.7 copy-start.15
  46.4 63.8 %collective-permute-start.6 = (bf16[2,192,640]{2,1,0:T(8,128)(2,1)}, bf16[2,192,640]{2,1,0:T(8,128)(2,1)}, u32[]{:S(2)}, u32[]{:S(2)}) collective-permute-start(bf16[2,192,640]{2,1,0:T(8,128)(2,1)} %get-tuple-element.45), channel_id=1, source_target_pairs={{4,0},{8,4},{12,8},{16,12},{20,16},{24,20},{28,24},{5,1},{9,5},{13... | collective-permute-start | bytes 1474568 | tf_op jit(solution)/shard_map/ppermute | solution.py:244
  63.8 0.7 copy-start.17
  64.5 45.8 %collective-permute-start.4 = (bf16[2,192,640]{2,1,0:T(8,128)(2,1)}, bf16[2,192,640]{2,1,0:T(8,128)(2,1)}, u32[]{:S(2)}, u32[]{:S(2)}) collective-permute-start(bf16[2,192,640]{2,1,0:T(8,128)(2,1)} %get-tuple-element.46), channel_id=1, source_target_pairs={{0,4},{4,8},{8,12},{12,16},{16,20},{20,24},{24,28},{1,5},{5,9},{9,... | collective-permute-start | bytes 1474568 | tf_op jit(solution)/shard_map/ppermute | solution.py:244
  69.4 0.7 copy-start.19
  70.1 40.1 %collective-permute-start.5 = (bf16[2,256,640]{2,1,0:T(8,128)(2,1)}, bf16[2,256,640]{2,1,0:T(8,128)(2,1)}, u32[]{:S(2)}, u32[]{:S(2)}) collective-permute-start(bf16[2,256,640]{2,1,0:T(8,128)(2,1)} %pad_maximum_fusion), channel_id=1, source_target_pairs={{0,4},{4,8},{8,12},{12,16},{16,20},{20,24},{24,28},{1,5},{5,9},{9,... | collective-permute-start | bytes 1966088 | tf_op jit(solution)/shard_map/ppermute | solution.py:244
  72.0 0.8 copy-start.9
  72.9 37.4 %collective-permute-start.7 = (bf16[2,256,640]{2,1,0:T(8,128)(2,1)}, bf16[2,256,640]{2,1,0:T(8,128)(2,1)}, u32[]{:S(2)}, u32[]{:S(2)}) collective-permute-start(bf16[2,256,640]{2,1,0:T(8,128)(2,1)} %pad_maximum_fusion.1), channel_id=1, source_target_pairs={{4,0},{8,4},{12,8},{16,12},{20,16},{24,20},{28,24},{5,1},{9,5},{13... | collective-permute-start | bytes 1966088 | tf_op jit(solution)/shard_map/ppermute | solution.py:244
  82.5 21.8 %collective-permute-start.8 = (bf16[4,128,256]{2,1,0:T(8,128)(2,1)}, bf16[4,128,256]{2,1,0:T(8,128)(2,1)S(1)}, u32[]{:S(2)}, u32[]{:S(2)}) collective-permute-start(bf16[4,128,256]{2,1,0:T(8,128)(2,1)} %bitcast.52), channel_id=1, source_target_pairs={{0,1},{1,2},{2,3},{3,0},{4,5},{5,6},{6,7},{7,4},{8,9},{9,10},{10,1... | collective-permute-start | bytes 786440 | tf_op jit(solution)/shard_map/ppermute | solution.py:224
  86.9 2.6 copy-start
  89.5 1.1 copy-start.4
  90.6 1.1 copy-start.6
  91.7 0.9 copy-start.7
  92.6 1.1 copy-start.10
  93.7 0.9 copy-start.22
  94.6 3.6 %copy-start.16 = (bf16[4,128,256]{2,1,0:T(8,128)(2,1)S(1)}, bf16[4,128,256]{2,1,0:T(8,128)(2,1)}, u32[]{:S(2)}) copy-start(bf16[4,128,256]{2,1,0:T(8,128)(2,1)} %copy-done.15) | copy-start | bytes 786436
  94.6 3.6 %copy-start.18 = (bf16[4,128,256]{2,1,0:T(8,128)(2,1)S(1)}, bf16[4,128,256]{2,1,0:T(8,128)(2,1)}, u32[]{:S(2)}) copy-start(bf16[4,128,256]{2,1,0:T(8,128)(2,1)} %copy-done.17) | copy-start | bytes 786436
  98.2 6.0 %copy-start.20 = (bf16[4,128,256]{2,1,0:T(8,128)(2,1)S(1)}, bf16[4,128,256]{2,1,0:T(8,128)(2,1)}, u32[]{:S(2)}) copy-start(bf16[4,128,256]{2,1,0:T(8,128)(2,1)} %copy-done.19) | copy-start | bytes 786436
  110.2 11.5 %copy-start.13 = (bf16[640,1280]{1,0:T(8,128)(2,1)S(1)}, bf16[640,1280]{1,0:T(8,128)(2,1)}, u32[]{:S(2)}) copy-start(bf16[640,1280]{1,0:T(8,128)(2,1)} %get-tuple-element.37.w_in) | copy-start | bytes 4915204
  110.2 11.5 %copy-start.14 = (bf16[1280,640]{1,0:T(8,128)(2,1)S(1)}, bf16[1280,640]{1,0:T(8,128)(2,1)}, u32[]{:S(2)}) copy-start(bf16[1280,640]{1,0:T(8,128)(2,1)} %get-tuple-element.35.w_out) | copy-start | bytes 4915204
  125.8 34.7 %collective-permute-start.14 = (bf16[4,128,640]{2,1,0:T(8,128)(2,1)S(1)}, bf16[4,128,640]{2,1,0:T(8,128)(2,1)S(1)}, u32[]{:S(2)}, u32[]{:S(2)}) collective-permute-start(bf16[4,128,640]{2,1,0:T(8,128)(2,1)S(1)} %get-tuple-element.25), channel_id=1, source_target_pairs={{0,1},{1,2},{2,3},{3,0},{4,5},{5,6},{6,7},{7,4},{8,9},{9,10},{10,1... | collective-permute-start | bytes 1966088 | tf_op jit(solution)/shard_map/ppermute | solution.py:224
  130.1 33.2 %collective-permute-start.22 = (bf16[4,128,128]{2,1,0:T(8,128)(2,1)S(1)}, bf16[4,128,128]{2,1,0:T(8,128)(2,1)S(1)}, u32[]{:S(2)}, u32[]{:S(2)}) collective-permute-start(bf16[4,128,128]{2,1,0:T(8,128)(2,1)S(1)} %get-tuple-element.33), channel_id=1, source_target_pairs={{0,1},{1,2},{2,3},{3,0},{4,5},{5,6},{6,7},{7,4},{8,9},{9,10},{10,1... | collective-permute-start | bytes 393224 | tf_op jit(solution)/shard_map/ppermute | solution.py:224
  130.2 33.1 %collective-permute-start.23 = (bf16[4,128,128]{2,1,0:T(8,128)(2,1)S(1)}, bf16[4,128,128]{2,1,0:T(8,128)(2,1)S(1)}, u32[]{:S(2)}, u32[]{:S(2)}) collective-permute-start(bf16[4,128,128]{2,1,0:T(8,128)(2,1)S(1)} %get-tuple-element.34), channel_id=1, source_target_pairs={{0,3},{1,0},{2,1},{3,2},{4,7},{5,4},{6,5},{7,6},{8,11},{9,8},{10,9... | collective-permute-start | bytes 393224 | tf_op jit(solution)/shard_map/ppermute | solution.py:224
  132.2 31.1 %collective-permute-start.17 = (bf16[4,128,640]{2,1,0:T(8,128)(2,1)S(1)}, bf16[4,128,640]{2,1,0:T(8,128)(2,1)S(1)}, u32[]{:S(2)}, u32[]{:S(2)}) collective-permute-start(bf16[4,128,640]{2,1,0:T(8,128)(2,1)S(1)} %get-tuple-element.28), channel_id=1, source_target_pairs={{0,3},{1,0},{2,1},{3,2},{4,7},{5,4},{6,5},{7,6},{8,11},{9,8},{10,9... | collective-permute-start | bytes 1966088 | tf_op jit(solution)/shard_map/ppermute | solution.py:224
  138.2 79.4 %collective-permute-start.15 = (bf16[4,128,640]{2,1,0:T(8,128)(2,1)S(1)}, bf16[4,128,640]{2,1,0:T(8,128)(2,1)S(1)}, u32[]{:S(2)}, u32[]{:S(2)}) collective-permute-start(bf16[4,128,640]{2,1,0:T(8,128)(2,1)S(1)} %get-tuple-element.26), channel_id=1, source_target_pairs={{0,1},{1,2},{2,3},{3,0},{4,5},{5,6},{6,7},{7,4},{8,9},{9,10},{10,1... | collective-permute-start | bytes 1966088 | tf_op jit(solution)/shard_map/ppermute | solution.py:224
  160.5 60.8 %collective-permute-start.18 = (bf16[4,128,640]{2,1,0:T(8,128)(2,1)S(1)}, bf16[4,128,640]{2,1,0:T(8,128)(2,1)S(1)}, u32[]{:S(2)}, u32[]{:S(2)}) collective-permute-start(bf16[4,128,640]{2,1,0:T(8,128)(2,1)S(1)} %get-tuple-element.29), channel_id=1, source_target_pairs={{0,3},{1,0},{2,1},{3,2},{4,7},{5,4},{6,5},{7,6},{8,11},{9,8},{10,9... | collective-permute-start | bytes 1966088 | tf_op jit(solution)/shard_map/ppermute | solution.py:224
  163.3 34.2 %collective-permute-start.16 = (bf16[4,128,256]{2,1,0:T(8,128)(2,1)S(1)}, bf16[4,128,256]{2,1,0:T(8,128)(2,1)S(1)}, u32[]{:S(2)}, u32[]{:S(2)}) collective-permute-start(bf16[4,128,256]{2,1,0:T(8,128)(2,1)S(1)} %get-tuple-element.27), channel_id=1, source_target_pairs={{0,1},{1,2},{2,3},{3,0},{4,5},{5,6},{6,7},{7,4},{8,9},{9,10},{10,1... | collective-permute-start | bytes 786440 | tf_op jit(solution)/shard_map/ppermute | solution.py:224
  163.3 49.8 %collective-permute-start.20 = (bf16[4,128,256]{2,1,0:T(8,128)(2,1)S(1)}, bf16[4,128,256]{2,1,0:T(8,128)(2,1)S(1)}, u32[]{:S(2)}, u32[]{:S(2)}) collective-permute-start(bf16[4,128,256]{2,1,0:T(8,128)(2,1)S(1)} %get-tuple-element.31), channel_id=1, source_target_pairs={{0,1},{1,2},{2,3},{3,0},{4,5},{5,6},{6,7},{7,4},{8,9},{9,10},{10,1... | collective-permute-start | bytes 786440 | tf_op jit(solution)/shard_map/ppermute | solution.py:224
  163.3 52.1 %collective-permute-start.21 = (bf16[4,128,256]{2,1,0:T(8,128)(2,1)S(1)}, bf16[4,128,256]{2,1,0:T(8,128)(2,1)S(1)}, u32[]{:S(2)}, u32[]{:S(2)}) collective-permute-start(bf16[4,128,256]{2,1,0:T(8,128)(2,1)S(1)} %get-tuple-element.32), channel_id=1, source_target_pairs={{0,3},{1,0},{2,1},{3,2},{4,7},{5,4},{6,5},{7,6},{8,11},{9,8},{10,9... | collective-permute-start | bytes 786440 | tf_op jit(solution)/shard_map/ppermute | solution.py:224
  165.4 58.7 %copy-start.26 = (bf16[2,5,256,640]{3,2,1,0:T(8,128)(2,1)S(1)}, bf16[2,5,256,640]{3,2,1,0:T(8,128)(2,1)}, u32[]{:S(2)}) copy-start(bf16[2,5,256,640]{3,2,1,0:T(8,128)(2,1)} %param.9) | copy-start | bytes 9830404
  165.4 58.6 %copy-start.28 = (bf16[448,256,1]{1,0,2:T(8,128)(2,1)S(1)}, bf16[448,256,1]{1,0,2:T(8,128)(2,1)}, u32[]{:S(2)}) copy-start(bf16[448,256,1]{1,0,2:T(8,128)(2,1)} %constant.34) | copy-start | bytes 688132
  197.5 36.0 %collective-permute-start.19 = (bf16[4,128,256]{2,1,0:T(8,128)(2,1)S(1)}, bf16[4,128,256]{2,1,0:T(8,128)(2,1)S(1)}, u32[]{:S(2)}, u32[]{:S(2)}) collective-permute-start(bf16[4,128,256]{2,1,0:T(8,128)(2,1)S(1)} %get-tuple-element.30), channel_id=1, source_target_pairs={{0,3},{1,0},{2,1},{3,2},{4,7},{5,4},{6,5},{7,6},{8,11},{9,8},{10,9... | collective-permute-start | bytes 786440 | tf_op jit(solution)/shard_map/ppermute | solution.py:224
  213.1 25.8 %collective-permute-start.26 = (bf16[2,192,640]{2,1,0:T(8,128)(2,1)S(1)}, bf16[2,192,640]{2,1,0:T(8,128)(2,1)S(1)}, u32[]{:S(2)}, u32[]{:S(2)}) collective-permute-start(bf16[2,192,640]{2,1,0:T(8,128)(2,1)S(1)} %get-tuple-element.49), channel_id=1, source_target_pairs={{4,0},{8,4},{12,8},{16,12},{20,16},{24,20},{28,24},{5,1},{9,5},{13... | collective-permute-start | bytes 1474568 | tf_op jit(solution)/shard_map/ppermute | solution.py:244
  215.4 9.6 %copy-start.8 = (bf16[192,448]{1,0:T(8,128)(2,1)S(1)}, bf16[192,448]{1,0:T(8,128)(2,1)}, u32[]{:S(2)}) copy-start(bf16[192,448]{1,0:T(8,128)(2,1)} %constant.31.clone.refs_2_) | copy-start | bytes 516100
  215.4 23.5 %collective-permute-start.24 = (bf16[2,192,640]{2,1,0:T(8,128)(2,1)S(1)}, bf16[2,192,640]{2,1,0:T(8,128)(2,1)S(1)}, u32[]{:S(2)}, u32[]{:S(2)}) collective-permute-start(bf16[2,192,640]{2,1,0:T(8,128)(2,1)S(1)} %get-tuple-element.50), channel_id=1, source_target_pairs={{0,4},{4,8},{8,12},{12,16},{16,20},{20,24},{24,28},{1,5},{5,9},{9,... | collective-permute-start | bytes 1474568 | tf_op jit(solution)/shard_map/ppermute | solution.py:244
  217.6 25.1 %collective-permute-start.25 = (bf16[2,256,640]{2,1,0:T(8,128)(2,1)S(1)}, bf16[2,256,640]{2,1,0:T(8,128)(2,1)S(1)}, u32[]{:S(2)}, u32[]{:S(2)}) collective-permute-start(bf16[2,256,640]{2,1,0:T(8,128)(2,1)S(1)} %pad_maximum_fusion.2), channel_id=1, source_target_pairs={{0,4},{4,8},{8,12},{12,16},{16,20},{20,24},{24,28},{1,5},{5,9},{9,... | collective-permute-start | bytes 1966088 | tf_op jit(solution)/shard_map/ppermute | solution.py:244
  221.3 21.4 %collective-permute-start.27 = (bf16[2,256,640]{2,1,0:T(8,128)(2,1)S(1)}, bf16[2,256,640]{2,1,0:T(8,128)(2,1)S(1)}, u32[]{:S(2)}, u32[]{:S(2)}) collective-permute-start(bf16[2,256,640]{2,1,0:T(8,128)(2,1)S(1)} %pad_maximum_fusion.3), channel_id=1, source_target_pairs={{4,0},{8,4},{12,8},{16,12},{20,16},{24,20},{28,24},{5,1},{9,5},{13... | collective-permute-start | bytes 1966088 | tf_op jit(solution)/shard_map/ppermute | solution.py:244
  238.9 13.8 %copy-start.11 = (bf16[640,1280]{1,0:T(8,128)(2,1)S(1)}, bf16[640,1280]{1,0:T(8,128)(2,1)}, u32[]{:S(2)}) copy-start(bf16[640,1280]{1,0:T(8,128)(2,1)} %get-tuple-element.38.w_in) | copy-start | bytes 4915204
  238.9 13.8 %copy-start.12 = (bf16[1280,640]{1,0:T(8,128)(2,1)S(1)}, bf16[1280,640]{1,0:T(8,128)(2,1)}, u32[]{:S(2)}) copy-start(bf16[1280,640]{1,0:T(8,128)(2,1)} %get-tuple-element.36.w_out) | copy-start | bytes 4915204
